TPU v7x, 32 devices: a whole 2x2x4 slice. The times are simulated.
32 devices in a mesh: group: 2 (over x), ctx: 16 (over z, y, core).
Axes of the slice: x: 2, y: 2, z: 4, core: 2. Of those that a mesh axis runs over, the one named last changes fastest.
Arguments:
- hyena_qkv: bfloat16 [4096, 3, 2048], P(('group', 'ctx')), parts along dimension 0, may hold values from -6 to 6
- short_weight: float32 [3, 3, 2048], replicated, may hold values from -3.5 to 3.5
- filter_rate: float32 [128, 16], replicated, as said below
- filter_residue: float32 [128, 16], replicated, may hold values from -4 to 4
- attn_qkv: bfloat16 [4096, 3, 2048], P(('group', 'ctx')), parts along dimension 0, may hold values from -6 to 6
- doc_lengths: int32 [8], P('group'), parts along dimension 0, may hold values from 1 to 897, 2048 in all
Outputs:
- hyena_out: bfloat16 [4096, 2048], P(('group', 'ctx')), parts along dimension 0
- attn_out: bfloat16 [4096, 2048], P(('group', 'ctx')), parts along dimension 0
There are 2 independent parts, one for each index of `group`. A program takes and returns all parts, laid end to end along the dimension named above; an argument that names none is the same for every part. Nothing has to cross between parts.
Inputs may be any that keep to these rules, and one draw needn't show every extreme that they name: `filter_rate`: every rate is positive and at most 1/30. `doc_lengths`: the lengths sum to 2048 and the longest is exactly 897.
All inputs are finite; a program needn't handle non-finite values.
Results may differ from a plain program's by a relative error of at most 0.0054.
Values may be sent and summed in bfloat16 or wider, within the bound.
No kernel may reach another device: no remote copies, remote signals or barrier semaphores. Data moves between devices by JAX's collectives and lax.ppermute only.
A program may use at most 128 MiB of HBM per device.

v0:
```python
import math

import jax
import jax.numpy as jnp
from jax import lax
from jax.sharding import PartitionSpec as P

HEAD = 128
SPAN = 8


precise = lax.Precision.HIGHEST


def from_behind(value, axis, steps):
    count = lax.axis_size(axis)
    initial, last = (max(0, -steps), min(count, count - steps))
    return lax.ppermute(value, axis, [(source, source + steps) for source in range(initial, last)])


def featurize(token_rows, before, short_weight):
    row_count = token_rows.shape[0]
    padded = jnp.concatenate([before, token_rows], axis=0).astype(jnp.float32)
    return (
        short_weight[0] * padded[2:]
        + short_weight[1] * padded[1 : row_count + 1]
        + short_weight[2] * padded[:row_count]
    )


def filter_terms(filter_rate, filter_residue, row_count):
    mode_coeff = filter_residue * jnp.sqrt(2.0 * filter_rate / filter_rate.shape[1])
    lag_values = jnp.arange(row_count).astype(jnp.float32)
    powers = jnp.exp(-filter_rate[:, :, None] * lag_values)
    filter_taps = jnp.einsum("gm,gmk->gk", mode_coeff, powers, precision=precise)
    return (mode_coeff, filter_taps.astype(jnp.bfloat16))


def toeplitz(filter_taps):
    row_count = filter_taps.shape[1]
    lag_index = (
        jnp.arange(row_count, dtype=jnp.int32)[:, None]
        - jnp.arange(row_count, dtype=jnp.int32)[None, :]
    )
    lag_table = jnp.take(filter_taps, jnp.clip(lag_index, 0, row_count - 1), axis=1)
    return jnp.where(lag_index[None] >= 0, lag_table, jnp.zeros((), filter_taps.dtype))


def block_ends(mixed_in, filter_rate):
    row_count, channels = mixed_in.shape
    groups = filter_rate.shape[0]
    lag_values = (row_count - 1 - jnp.arange(row_count)).astype(jnp.float32)
    powers = jnp.exp(-filter_rate[:, :, None] * lag_values)
    grouped = mixed_in.astype(jnp.float32).reshape(row_count, groups, channels // groups)
    return jnp.einsum("gms,sgc->gmc", powers, grouped, precision=precise)


def block_far(carried, filter_rate, mode_coeff, row_count):
    lag_values = jnp.arange(1, row_count + 1).astype(jnp.float32)
    powers = mode_coeff[:, :, None] * jnp.exp(-filter_rate[:, :, None] * lag_values)
    return jnp.einsum("gmt,gmc->tgc", powers, carried, precision=precise)


def visible(query_pos, key_pos, doc_lengths):
    bounds = jnp.cumsum(doc_lengths, dtype=jnp.int32)
    query_doc = jnp.sum((query_pos[:, None] >= bounds[None, :]).astype(jnp.int32), axis=1)
    key_doc = jnp.sum((key_pos[:, None] >= bounds[None, :]).astype(jnp.int32), axis=1)
    causal = (key_pos[None, :] <= query_pos[:, None]) & (key_pos[None, :] >= 0)
    return causal & (key_doc[None, :] == query_doc[:, None])


def attend(queries, keys, values, allowed):
    row_count, channels = queries.shape
    heads = channels // HEAD

    def split_heads(matrix):
        return matrix.reshape(matrix.shape[0], heads, HEAD).transpose(1, 0, 2)

    def one_head(head_parts):
        query_rows, key_rows, value_rows = head_parts
        scores = jnp.dot(query_rows, key_rows.T, preferred_element_type=jnp.float32) * (
            1.0 / math.sqrt(HEAD)
        )
        scores = jnp.where(allowed, scores, -jnp.inf)
        row_max = jnp.max(scores, axis=1, keepdims=True)
        exp_scores = jnp.exp(scores - row_max)
        weight = (exp_scores / jnp.sum(exp_scores, axis=1, keepdims=True)).astype(jnp.bfloat16)
        return jnp.dot(weight, value_rows, preferred_element_type=jnp.float32).astype(jnp.bfloat16)

    head_out = lax.map(one_head, (split_heads(queries), split_heads(keys), split_heads(values)))
    return head_out.transpose(1, 0, 2).reshape(row_count, channels)


def on_device(hyena_qkv, short_weight, filter_rate, filter_residue, attn_qkv, doc_lengths):
    row_count = hyena_qkv.shape[0]
    channels = hyena_qkv.shape[2]
    groups = filter_rate.shape[0]
    device_index = lax.axis_index("ctx")
    before = from_behind(hyena_qkv[row_count - 2 :], "ctx", 1)
    featured = featurize(hyena_qkv, before, short_weight)
    mixed_in = (featured[:, 1] * featured[:, 2]).astype(jnp.bfloat16)
    mode_coeff, filter_taps = filter_terms(filter_rate, filter_residue, row_count)
    grouped = mixed_in.reshape(row_count, groups, channels // groups)
    near_part = jnp.einsum(
        "gts,sgc->tgc", toeplitz(filter_taps), grouped, preferred_element_type=jnp.float32
    )
    end_states = block_ends(mixed_in, filter_rate)
    pieces = lax.all_gather(end_states[None], "ctx", axis=0, tiled=True)
    owners = jnp.arange(pieces.shape[0], dtype=jnp.int32)
    absorb_distance = device_index - 1 - owners
    lag_values = (jnp.maximum(absorb_distance, 0) * row_count).astype(jnp.float32)
    powers = jnp.exp(-filter_rate[None] * lag_values[:, None, None])
    powers = jnp.where((absorb_distance >= 0)[:, None, None], powers, 0.0)
    carried = jnp.einsum("ngm,ngmc->gmc", powers, pieces, precision=precise)
    far_part = block_far(carried, filter_rate, mode_coeff, row_count)
    hyena_out = (featured[:, 0] * (near_part + far_part).reshape(row_count, channels)).astype(
        jnp.bfloat16
    )
    key_pairs = attn_qkv[:, 1:]
    key_blocks = [key_pairs]
    moving = key_pairs
    for distance in range(1, SPAN):
        moving = from_behind(moving, "ctx", 1)
        key_blocks.append(moving)
    window = jnp.concatenate(key_blocks[::-1], axis=0)
    query_pos = device_index * row_count + jnp.arange(row_count, dtype=jnp.int32)
    key_pos = (device_index - SPAN + 1) * row_count + jnp.arange(SPAN * row_count, dtype=jnp.int32)
    allowed = visible(query_pos, key_pos, doc_lengths)
    attn_out = attend(attn_qkv[:, 0], window[:, 0], window[:, 1], allowed)
    return (hyena_out, attn_out)


def solution(mesh):
    in_specs = (
        P(("group", "ctx"), None, None),
        P(),
        P(),
        P(),
        P(("group", "ctx"), None, None),
        P("group"),
    )
    out_specs = (P(("group", "ctx"), None), P(("group", "ctx"), None))
    return jax.shard_map(
        on_device, mesh=mesh, in_specs=in_specs, out_specs=out_specs, check_vma=False
    )
```

profile of v0, /device:TPU:15, one launch (start us, length us, event | category | flops | bytes accessed | tf_op | source)
XLA Modules:
  0.0 266.5 jit_solution(11131418573891220046)
XLA Ops:
  9.2 3.7 %collective-permute-start.1 = (bf16[128,2,2048]{0,2,1:T(8,128)(2,1)S(1)}, bf16[128,2,2048]{0,2,1:T(8,128)(2,1)}, u32[]{:S(2)}, u32[]{:S(2)}) collective-permute-start(bf16[128,2,2048]{0,2,1:T(8,128)(2,1)S(1)} %copy.73), channel_id=1, source_target_pairs={{0,1},{1,2},{2,3},{3,4},{4,5},{5,6},{6,7},{7,8},{8,9},{9,10},{10,1... | collective-permute-start | bytes 3145736 | tf_op jit(solution)/shard_map/ppermute | solution.py:18
  13.9 1.9 collective-permute-start
  15.8 8.9 %collective-permute-done.1 = bf16[128,2,2048]{0,2,1:T(8,128)(2,1)} collective-permute-done((bf16[128,2,2048]{0,2,1:T(8,128)(2,1)S(1)}, bf16[128,2,2048]{0,2,1:T(8,128)(2,1)}, u32[]{:S(2)}, u32[]{:S(2)}) %collective-permute-start.1) | collective-permute-done | bytes 1048608 | tf_op jit(solution)/shard_map/ppermute | solution.py:18
  24.7 5.4 %collective-permute-start.2 = (bf16[128,2,2048]{0,2,1:T(8,128)(2,1)}, bf16[128,2,2048]{0,2,1:T(8,128)(2,1)}, u32[]{:S(2)}, u32[]{:S(2)}) collective-permute-start(bf16[128,2,2048]{0,2,1:T(8,128)(2,1)} %collective-permute-done.1), channel_id=1, source_target_pairs={{0,1},{1,2},{2,3},{3,4},{4,5},{5,6},{6,7},{7,8},{8,9},{9,10},{10,1... | collective-permute-start | bytes 3145736 | tf_op jit(solution)/shard_map/ppermute | solution.py:18
  30.1 1.9 copy.44
  34.2 7.9 %collective-permute-done.2 = bf16[128,2,2048]{0,2,1:T(8,128)(2,1)} collective-permute-done((bf16[128,2,2048]{0,2,1:T(8,128)(2,1)}, bf16[128,2,2048]{0,2,1:T(8,128)(2,1)}, u32[]{:S(2)}, u32[]{:S(2)}) %collective-permute-start.2) | collective-permute-done | bytes 1048608 | tf_op jit(solution)/shard_map/ppermute | solution.py:18
  42.1 5.3 %collective-permute-start.3 = (bf16[128,2,2048]{0,2,1:T(8,128)(2,1)}, bf16[128,2,2048]{0,2,1:T(8,128)(2,1)}, u32[]{:S(2)}, u32[]{:S(2)}) collective-permute-start(bf16[128,2,2048]{0,2,1:T(8,128)(2,1)} %collective-permute-done.2), channel_id=1, source_target_pairs={{0,1},{1,2},{2,3},{3,4},{4,5},{5,6},{6,7},{7,8},{8,9},{9,10},{10,1... | collective-permute-start | bytes 3145736 | tf_op jit(solution)/shard_map/ppermute | solution.py:18
  47.4 4.7 %fusion.22 = f32[128,3,2048]{0,2,1:T(8,128)S(1)} fusion(f32[130,3,2048]{0,2,1:T(8,128)S(1)} %maximum_convert_fusion, f32[3,2048]{1,0:T(4,128)S(1)} %get-tuple-element.123, f32[3,2048]{1,0:T(4,128)S(1)} %get-tuple-element.124, f32[3,2048]{1,0:T(4,128)S(1)} %get-tuple-element.122), kind=kLoop, calls=%fused_computation.27 | loop fusion | flops 3932160 | bytes 12656640 | tf_op jit(solution)/shard_map/add | solution.py:25
  53.0 2.0 fusion.32
  55.0 2.2 copy.48
  57.2 2.2 collective-permute-done.3
  59.4 5.3 %collective-permute-start.4 = (bf16[128,2,2048]{0,2,1:T(8,128)(2,1)}, bf16[128,2,2048]{0,2,1:T(8,128)(2,1)}, u32[]{:S(2)}, u32[]{:S(2)}) collective-permute-start(bf16[128,2,2048]{0,2,1:T(8,128)(2,1)} %collective-permute-done.3), channel_id=1, source_target_pairs={{0,1},{1,2},{2,3},{3,4},{4,5},{5,6},{6,7},{7,8},{8,9},{9,10},{10,1... | collective-permute-start | bytes 3145736 | tf_op jit(solution)/shard_map/ppermute | solution.py:18
  64.7 16.3 %collective-permute-done.4 = bf16[128,2,2048]{0,2,1:T(8,128)(2,1)} collective-permute-done((bf16[128,2,2048]{0,2,1:T(8,128)(2,1)}, bf16[128,2,2048]{0,2,1:T(8,128)(2,1)}, u32[]{:S(2)}, u32[]{:S(2)}) %collective-permute-start.4) | collective-permute-done | bytes 1048608 | tf_op jit(solution)/shard_map/ppermute | solution.py:18
  80.9 5.3 %collective-permute-start.5 = (bf16[128,2,2048]{0,2,1:T(8,128)(2,1)}, bf16[128,2,2048]{0,2,1:T(8,128)(2,1)}, u32[]{:S(2)}, u32[]{:S(2)}) collective-permute-start(bf16[128,2,2048]{0,2,1:T(8,128)(2,1)} %collective-permute-done.4), channel_id=1, source_target_pairs={{0,1},{1,2},{2,3},{3,4},{4,5},{5,6},{6,7},{7,8},{8,9},{9,10},{10,1... | collective-permute-start | bytes 3145736 | tf_op jit(solution)/shard_map/ppermute | solution.py:18
  87.6 16.3 %collective-permute-done.5 = bf16[128,2,2048]{0,2,1:T(8,128)(2,1)} collective-permute-done((bf16[128,2,2048]{0,2,1:T(8,128)(2,1)}, bf16[128,2,2048]{0,2,1:T(8,128)(2,1)}, u32[]{:S(2)}, u32[]{:S(2)}) %collective-permute-start.5) | collective-permute-done | bytes 1048608 | tf_op jit(solution)/shard_map/ppermute | solution.py:18
  103.9 5.3 %collective-permute-start.6 = (bf16[128,2,2048]{0,2,1:T(8,128)(2,1)}, bf16[128,2,2048]{0,2,1:T(8,128)(2,1)}, u32[]{:S(2)}, u32[]{:S(2)}) collective-permute-start(bf16[128,2,2048]{0,2,1:T(8,128)(2,1)} %collective-permute-done.5), channel_id=1, source_target_pairs={{0,1},{1,2},{2,3},{3,4},{4,5},{5,6},{6,7},{7,8},{8,9},{9,10},{10,1... | collective-permute-start | bytes 3145736 | tf_op jit(solution)/shard_map/ppermute | solution.py:18
  109.8 1.9 slice.52
  111.7 2.0 copy.72
  115.5 57.4 %gather_fusion = bf16[16384,128]{1,0:T(8,128)(2,1)} fusion(bf16[128,128]{0,1:T(8,128)(2,1)S(1)} %copy.60, s32[16384]{0:T(1024)S(1)} %fusion.41), kind=kCustom, calls=%fused_computation | custom fusion | bytes 8454144 | tf_op jit(solution)/shard_map/jit(_take)/gather | solution.py:45
  172.9 6.7 %copy.46 = bf16[128,128,128]{1,0,2:T(8,128)(2,1)} copy(bf16[128,128,128]{2,1,0:T(8,128)(2,1)} %bitcast.83) | data formatting | bytes 8388608 | tf_op jit(solution)/shard_map/jit(_take)/gather | solution.py:45
  180.0 2.1 collective-permute-start.7
  182.1 5.7 %fusion.16 = f32[128,16,128]{2,1,0:T(8,128)} fusion(bf16[128,128,16]{0,2,1:T(8,128)(2,1)} %bitcast.88, bf16[128,128,128]{1,0,2:T(8,128)(2,1)} %copy.46, pred[128,128]{1,0:T(8,128)(4,1)S(1)} %get-tuple-element.127, pred[128,128]{1,0:T(8,128)(4,1)S(1)} %get-tuple-element.128), kind=kOutput, calls=%fused_computation.20 | convolution fusion | flops 71303168 | bytes 5799936 | tf_op jit(solution)/shard_map/gts,sgc->tgc/dot_general | solution.py:104
  187.8 2.0 copy.78
  191.7 3.0 %convolution_add_fusion = f32[128,16,128]{2,1,0:T(8,128)S(1)} fusion(f32[128,16,128]{2,1,0:T(8,128)} %fusion.16, f32[128,16,16]{1,2,0:T(8,128)} %copy.68, f32[128,16]{1,0:T(8,128)} %copy-done.4, f32[128]{0:T(128)S(1)} %add_convert_fusion, f32[128,16]{1,0:T(8,128)S(1)} %copy.45), kind=kOutput, calls=%fused_computation.35 | convolution fusion | flops 51118080 | bytes 2245120 | tf_op jit(solution)/shard_map/gmt,gmc->tgc/dot_general | solution.py:61
  195.6 2.0 copy.56
  199.2 1.6 constant_dynamic-update-slice_fusion.6
  202.4 1.7 constant_dynamic-update-slice_fusion.4
  204.1 1.6 constant_dynamic-update-slice_fusion.3
  205.7 1.6 constant_dynamic-update-slice_fusion.2
  207.2 1.6 constant_dynamic-update-slice_fusion.1
  209.2 3.7 %fusion.50 = (bf16[1024,1,2048]{0,2,1:T(8,128)(2,1)}, bf16[1024,1,2048]{0,2,1:T(8,128)(2,1)}) fusion(bf16[1024,2,2048]{0,2,1:T(8,128)(2,1)S(1)} %constant_dynamic-update-slice_fusion), kind=kLoop, calls=%fused_computation.90 | loop fusion | bytes 16777216 | tf_op jit(solution)/shard_map/slice | solution.py:129
  212.9 45.8 %while.11 = (s32[]{:T(128)}, bf16[16,128,128]{2,1,0:T(8,128)(2,1)S(1)}, bf16[16,128,128]{1,2,0:T(8,128)(2,1)}, bf16[16,1024,128]{1,2,0:T(8,128)(2,1)}, bf16[16,1...) while((s32[]{:T(128)}, ...), condition=%wide.region_6.7_spmd.clone, body=%wide.region_3.6_spmd.clone.sunk | while | flops 68697856 | bytes 2177645 | solution.py:90
  (107 shorter events, 62.8 us)
Async XLA Ops:
  7.2 22.9 %copy-start.6 = (f32[128,16]{0,1:T(8,128)S(1)}, f32[128,16]{0,1:T(8,128)}, u32[]{:S(2)}) copy-start(f32[128,16]{0,1:T(8,128)} %param.10) | copy-start | bytes 24580
  7.2 22.9 %copy-start.7 = (f32[128,16]{0,1:T(8,128)S(1)}, f32[128,16]{0,1:T(8,128)}, u32[]{:S(2)}) copy-start(f32[128,16]{0,1:T(8,128)} %param.11) | copy-start | bytes 24580
  7.2 22.9 %copy-start.5 = (f32[3,3,2048]{2,1,0:T(4,128)S(1)}, f32[3,3,2048]{2,1,0:T(4,128)}, u32[]{:S(2)}) copy-start(f32[3,3,2048]{2,1,0:T(4,128)} %param.9) | copy-start | bytes 221188
  7.2 180.6 %all-gather.3.cloned.1.call-start = ((), (), s32[]{:S(2)}) async-start(), calls=%async_computation | async-start | bytes 2228224 | tf_op jit(solution)/shard_map/all_gather | solution.py:108
  9.2 20.9 %copy-start = (bf16[128,2,2048]{0,2,1:T(8,128)(2,1)}, bf16[128,2,2048]{0,2,1:T(8,128)(2,1)S(1)}, u32[]{:S(2)}) copy-start(bf16[128,2,2048]{0,2,1:T(8,128)(2,1)S(1)} %copy.73) | copy-start | bytes 3145732
  9.2 15.4 %collective-permute-start.1 = (bf16[128,2,2048]{0,2,1:T(8,128)(2,1)S(1)}, bf16[128,2,2048]{0,2,1:T(8,128)(2,1)}, u32[]{:S(2)}, u32[]{:S(2)}) collective-permute-start(bf16[128,2,2048]{0,2,1:T(8,128)(2,1)S(1)} %copy.73), channel_id=1, source_target_pairs={{0,1},{1,2},{2,3},{3,4},{4,5},{5,6},{6,7},{7,8},{8,9},{9,10},{10,1... | collective-permute-start | bytes 3145736 | tf_op jit(solution)/shard_map/ppermute | solution.py:18
  13.9 18.3 %collective-permute-start = (bf16[2,3,2048]{2,0,1:T(2,128)(2,1)S(1)}, bf16[2,3,2048]{2,0,1:T(2,128)(2,1)S(1)}, u32[]{:S(2)}, u32[]{:S(2)}) collective-permute-start(bf16[2,3,2048]{2,0,1:T(2,128)(2,1)S(1)} %slice.43), channel_id=1, source_target_pairs={{0,1},{1,2},{2,3},{3,4},{4,5},{5,6},{6,7},{7,8},{8,9},{9,10},{10,1... | collective-permute-start | bytes 73736 | tf_op jit(solution)/shard_map/ppermute | solution.py:18
  24.7 17.4 %collective-permute-start.2 = (bf16[128,2,2048]{0,2,1:T(8,128)(2,1)}, bf16[128,2,2048]{0,2,1:T(8,128)(2,1)}, u32[]{:S(2)}, u32[]{:S(2)}) collective-permute-start(bf16[128,2,2048]{0,2,1:T(8,128)(2,1)} %collective-permute-done.1), channel_id=1, source_target_pairs={{0,1},{1,2},{2,3},{3,4},{4,5},{5,6},{6,7},{7,8},{8,9},{9,10},{10,1... | collective-permute-start | bytes 3145736 | tf_op jit(solution)/shard_map/ppermute | solution.py:18
  42.1 17.3 %collective-permute-start.3 = (bf16[128,2,2048]{0,2,1:T(8,128)(2,1)}, bf16[128,2,2048]{0,2,1:T(8,128)(2,1)}, u32[]{:S(2)}, u32[]{:S(2)}) collective-permute-start(bf16[128,2,2048]{0,2,1:T(8,128)(2,1)} %collective-permute-done.2), channel_id=1, source_target_pairs={{0,1},{1,2},{2,3},{3,4},{4,5},{5,6},{6,7},{7,8},{8,9},{9,10},{10,1... | collective-permute-start | bytes 3145736 | tf_op jit(solution)/shard_map/ppermute | solution.py:18
  52.2 0.8 copy-start.2
  59.4 21.5 %collective-permute-start.4 = (bf16[128,2,2048]{0,2,1:T(8,128)(2,1)}, bf16[128,2,2048]{0,2,1:T(8,128)(2,1)}, u32[]{:S(2)}, u32[]{:S(2)}) collective-permute-start(bf16[128,2,2048]{0,2,1:T(8,128)(2,1)} %collective-permute-done.3), channel_id=1, source_target_pairs={{0,1},{1,2},{2,3},{3,4},{4,5},{5,6},{6,7},{7,8},{8,9},{9,10},{10,1... | collective-permute-start | bytes 3145736 | tf_op jit(solution)/shard_map/ppermute | solution.py:18
  80.9 23.0 %collective-permute-start.5 = (bf16[128,2,2048]{0,2,1:T(8,128)(2,1)}, bf16[128,2,2048]{0,2,1:T(8,128)(2,1)}, u32[]{:S(2)}, u32[]{:S(2)}) collective-permute-start(bf16[128,2,2048]{0,2,1:T(8,128)(2,1)} %collective-permute-done.4), channel_id=1, source_target_pairs={{0,1},{1,2},{2,3},{3,4},{4,5},{5,6},{6,7},{7,8},{8,9},{9,10},{10,1... | collective-permute-start | bytes 3145736 | tf_op jit(solution)/shard_map/ppermute | solution.py:18
  86.3 25.4 %copy-start.4 = (f32[128,16]{1,0:T(8,128)}, f32[128,16]{1,0:T(8,128)S(1)}, u32[]{:S(2)}) copy-start(f32[128,16]{1,0:T(8,128)S(1)} %copy.74) | copy-start | bytes 24580
  103.9 76.0 %collective-permute-start.6 = (bf16[128,2,2048]{0,2,1:T(8,128)(2,1)}, bf16[128,2,2048]{0,2,1:T(8,128)(2,1)}, u32[]{:S(2)}, u32[]{:S(2)}) collective-permute-start(bf16[128,2,2048]{0,2,1:T(8,128)(2,1)} %collective-permute-done.5), channel_id=1, source_target_pairs={{0,1},{1,2},{2,3},{3,4},{4,5},{5,6},{6,7},{7,8},{8,9},{9,10},{10,1... | collective-permute-start | bytes 3145736 | tf_op jit(solution)/shard_map/ppermute | solution.py:18
  172.9 6.7 %copy-start.8 = (s32[4]{0:T(128)S(1)}, s32[4]{0:T(128)}, u32[]{:S(2)}) copy-start(s32[4]{0:T(128)} %param.13) | copy-start | bytes 52
  180.0 17.7 %collective-permute-start.7 = (bf16[128,2,2048]{0,2,1:T(8,128)(2,1)}, bf16[128,2,2048]{0,2,1:T(8,128)(2,1)}, u32[]{:S(2)}, u32[]{:S(2)}) collective-permute-start(bf16[128,2,2048]{0,2,1:T(8,128)(2,1)} %collective-permute-done.6), channel_id=1, source_target_pairs={{0,1},{1,2},{2,3},{3,4},{4,5},{5,6},{6,7},{7,8},{8,9},{9,10},{10,1... | collective-permute-start | bytes 3145736 | tf_op jit(solution)/shard_map/ppermute | solution.py:18
  202.4 6.5 %copy-start.1 = (bf16[128,2,2048]{0,2,1:T(8,128)(2,1)S(1)}, bf16[128,2,2048]{0,2,1:T(8,128)(2,1)}, u32[]{:S(2)}) copy-start(bf16[128,2,2048]{0,2,1:T(8,128)(2,1)} %copy-done) | copy-start | bytes 3145732
  209.2 3.7 %copy-start.3 = (bf16[16,128,128]{2,1,0:T(8,128)(2,1)S(1)}, bf16[16,128,128]{2,1,0:T(8,128)(2,1)}, u32[]{:S(2)}) copy-start(bf16[16,128,128]{2,1,0:T(8,128)(2,1)} %custom-call.3) | copy-start | bytes 1572868
Sparse Core Ops, SparseCore 0:
  57.4 44.1 all-gather.2
where the time goes:
time: 268 us; the launch traced here: 267 us
  local copies, waits for them, and re-layouts  100 us (37%)
  matrix products  52.4 us (20%)
  waiting for transfers between devices  51.5 us (19%)
  starting transfers between devices  34.3 us (13%)
  between operations  14.4 us (5%)
  other arithmetic  13.5 us (5%)
    gather x2, local copies, waits for them, and re-layouts, toeplitz(): jnp.take(filter_taps, jnp.clip(lag_index, 0, row_count - 1), axis=1)  64 us
    ppermute x8, waiting for transfers between devices, from_behind(): lax.ppermute(value, axis, [(source, source + steps) for source in range(i...  51.5 us
    ppermute x8, starting transfers between devices, from_behind(): lax.ppermute(value, axis, [(source, source + steps) for source in range(i...  34.2 us
    unnamed x32, local copies, waits for them, and re-layouts  22.2 us
    dot_general x16, matrix products, one_head(): jnp.dot(query_rows, key_rows.T, preferred_element_type=jnp.float32)  21.6 us
    dot_general x16, matrix products, one_head(): jnp.dot(weight, value_rows, preferred_element_type=jnp.float32)  20.2 us
    dot_general x1, matrix products, on_device(): jnp.einsum('gts,sgc->tgc', toeplitz(filter_taps), grouped, preferred_elem...  5.66 us
    slice x2, local copies, waits for them, and re-layouts, on_device(): attn_out = attend(attn_qkv[:, 0], window[:, 0], window[:, 1], allowed)  5.59 us
  transfers between devices with their start and end apart: 9, of which 5 were waited for; matrix products, arithmetic and copies ran while one was open for 38% of the time, Pallas kernels for 0%

commit v1 on v0

v1 whole, which is shorter than its diff:
```python
import functools
import math

import jax
import jax.numpy as jnp
from jax import lax
from jax.experimental import pallas as pl
from jax.experimental.pallas import tpu as pltpu
from jax.sharding import PartitionSpec as P

HEAD = 128
LANES = 128
ROW = 4

F32 = jnp.float32
BF16 = jnp.bfloat16


def flip(value, axis, bit):
    count = lax.axis_size(axis)
    return lax.ppermute(value, axis, [(at, at ^ bit) for at in range(count)])


def ahead(value, axis, steps, bit=0):
    count = lax.axis_size(axis)
    pairs = [(at, (at + steps) ^ bit) for at in range(count - steps)]
    return lax.ppermute(value, axis, pairs)


def cost(flops, moved, exps=0):
    return pl.CostEstimate(flops=flops, bytes_accessed=moved, transcendentals=exps)


VMEM = pl.BlockSpec(memory_space=pltpu.VMEM)
SMEM = pl.BlockSpec(memory_space=pltpu.SMEM)
ANY = pl.BlockSpec(memory_space=pl.ANY)


def table(rate_row, lags_down):
    return jnp.exp(-rate_row * lags_down)


def hyena_main_body(modes, x_ref, halo_ref, w_ref, rate_ref, res_ref, near_ref, q_ref, ends_ref, taps_s, u_s):
    rows, lanes = x_ref.shape[1:]
    terms = rate_ref.shape[2]
    filters = terms // modes
    width = lanes // filters
    row_at = lax.broadcasted_iota(jnp.int32, (rows, lanes), 0)
    lane_at = lax.broadcasted_iota(jnp.int32, (rows, lanes), 1)

    def feature(stream):
        here = x_ref[stream].astype(F32)
        halo = halo_ref[stream].astype(F32)
        one = jnp.where(row_at == 0, halo[1:2], pltpu.roll(here, 1, 0))
        two = pltpu.roll(here, 2, 0)
        two = jnp.where(row_at == 0, halo[0:1], jnp.where(row_at == 1, halo[1:2], two))
        tap = [w_ref[n, stream : stream + 1, :] for n in range(3)]
        return tap[0] * here + tap[1] * one + tap[2] * two

    q_ref[...] = feature(0)
    mixed = (feature(1) * feature(2)).astype(BF16)

    rate = jnp.broadcast_to(rate_ref[0], (rows, terms)).T
    residue = jnp.broadcast_to(res_ref[0], (rows, terms)).T
    coeff = residue * jnp.sqrt(2.0 * rate / modes)
    lag = (rows - 1 - lax.broadcasted_iota(jnp.int32, (terms, rows), 1)).astype(F32)
    powers = jnp.exp(-rate * lag)
    backward = jnp.sum((coeff * powers).reshape(filters, modes, rows), axis=1)
    zero = jnp.zeros((rows, lanes), BF16)
    for g in range(filters):
        spread = jnp.broadcast_to(backward[g : g + 1], (rows, rows))
        shifted = pltpu.roll(spread, 1, 1, stride=1, stride_axis=0)
        kept = jnp.where(lane_at <= row_at, shifted, 0.0)
        taps_s[:, g * rows : (g + 1) * rows] = kept.astype(BF16)
        mine = (lane_at // width) == g
        u_s[g * rows : (g + 1) * rows, :] = jnp.where(mine, mixed, zero)
    near_ref[...] = jnp.dot(taps_s[...], u_s[...], preferred_element_type=F32)

    high = powers.astype(BF16)
    low = (powers - high.astype(F32)).astype(BF16)
    ends = jnp.dot(high, mixed, preferred_element_type=F32) + jnp.dot(
        low, mixed, preferred_element_type=F32
    )
    own = (
        lax.broadcasted_iota(jnp.int32, (terms, lanes), 0) // modes
        == lax.broadcasted_iota(jnp.int32, (terms, lanes), 1) // width
    )
    ends_ref[...] = jnp.sum(jnp.where(own, ends, 0.0).reshape(filters, modes, lanes), axis=0)


def hyena_main(streams, halo, short_weight, rate_rows, res_rows, modes):
    _, rows, channels = streams.shape
    blocks, _, terms = rate_rows.shape
    lanes = channels // blocks
    filters = terms // modes
    by_block = lambda n: (0, n)
    lead = lambda n: (0, 0, n)
    whole = lambda n: (n, 0, 0)
    return pl.pallas_call(
        functools.partial(hyena_main_body, modes),
        grid=(blocks,),
        in_specs=[
            pl.BlockSpec((3, rows, lanes), lead),
            pl.BlockSpec((3, 2, lanes), lead),
            pl.BlockSpec((3, 3, lanes), lead),
            pl.BlockSpec((1, 1, terms), whole),
            pl.BlockSpec((1, 1, terms), whole),
        ],
        out_specs=[
            pl.BlockSpec((rows, lanes), by_block),
            pl.BlockSpec((rows, lanes), by_block),
            pl.BlockSpec((modes, lanes), by_block),
        ],
        out_shape=[
            jax.ShapeDtypeStruct((rows, channels), F32),
            jax.ShapeDtypeStruct((rows, channels), F32),
            jax.ShapeDtypeStruct((modes, channels), F32),
        ],
        scratch_shapes=[
            pltpu.VMEM((rows, filters * rows), BF16),
            pltpu.VMEM((filters * rows, lanes), BF16),
        ],
        cost_estimate=cost(2 * rows * rows * filters * channels, 8 * rows * channels),
        name="hyena_main",
    )(streams, halo, short_weight, rate_rows, res_rows)


def hyena_out_body(modes, near_ref, q_ref, carried_ref, rate_ref, res_ref, out_ref):
    rows, lanes = near_ref.shape
    terms = rate_ref.shape[2]
    filters = terms // modes
    width = lanes // filters
    rate = rate_ref[0]
    coeff = res_ref[0] * jnp.sqrt(2.0 * rate / modes)
    lag = (1 + lax.broadcasted_iota(jnp.int32, (rows, terms), 0)).astype(F32)
    powers = coeff * jnp.exp(-rate * lag)
    p_high = powers.astype(BF16)
    p_low = (powers - p_high.astype(F32)).astype(BF16)
    own = (
        lax.broadcasted_iota(jnp.int32, (terms, lanes), 0) // modes
        == lax.broadcasted_iota(jnp.int32, (terms, lanes), 1) // width
    )
    carried = jnp.where(own, jnp.concatenate([carried_ref[...]] * filters, axis=0), 0.0)
    c_high = carried.astype(BF16)
    c_low = (carried - c_high.astype(F32)).astype(BF16)
    far = (
        jnp.dot(p_high, c_high, preferred_element_type=F32)
        + jnp.dot(p_low, c_high, preferred_element_type=F32)
        + jnp.dot(p_high, c_low, preferred_element_type=F32)
    )
    out_ref[...] = (q_ref[...] * (near_ref[...] + far)).astype(BF16)


def hyena_finish(near, query, carried, rate_rows, res_rows, modes):
    rows, channels = near.shape
    blocks, _, terms = rate_rows.shape
    lanes = channels // blocks
    by_block = lambda n: (0, n)
    whole = lambda n: (n, 0, 0)
    return pl.pallas_call(
        functools.partial(hyena_out_body, modes),
        grid=(blocks,),
        in_specs=[
            pl.BlockSpec((rows, lanes), by_block),
            pl.BlockSpec((rows, lanes), by_block),
            pl.BlockSpec((modes, lanes), by_block),
            pl.BlockSpec((1, 1, terms), whole),
            pl.BlockSpec((1, 1, terms), whole),
        ],
        out_specs=pl.BlockSpec((rows, lanes), by_block),
        out_shape=jax.ShapeDtypeStruct((rows, channels), BF16),
        cost_estimate=cost(6 * rows * terms * channels, 10 * rows * channels),
        name="hyena_finish",
    )(near, query, carried, rate_rows, res_rows)


def scan_states(ends, filter_rate, rows):
    modes, channels = ends.shape
    half = channels // 2
    width = channels // filter_rate.shape[0]
    index = lax.axis_index("ctx")
    chips = lax.axis_size("ctx") // 2
    core = index % 2
    rate = jnp.repeat(filter_rate.T, width, axis=1)
    take = lambda matrix, which: lax.dynamic_slice_in_dim(matrix, which * half, half, 1)
    rate = take(rate, core)
    decay = lambda blocks: jnp.exp(-rate * float(rows * blocks))
    mine = take(ends, core)
    theirs = flip(take(ends, 1 - core), "ctx", 1)
    even = jnp.where(core == 0, mine, theirs)
    odd = jnp.where(core == 0, theirs, mine)
    total = decay(1) * even + odd
    before = ahead(total, "ctx", 2)
    reach = 2
    while reach < chips:
        upto = total + decay(2) * before
        before = before + decay(2 * (reach - 1)) * ahead(upto, "ctx", 2 * reach)
        reach *= 2
    second = decay(1) * before + even
    keep = jnp.where(core == 0, before, second)
    back = flip(jnp.where(core == 0, second, before), "ctx", 1)
    return jnp.concatenate(
        [jnp.where(core == 0, keep, back), jnp.where(core == 0, back, keep)], axis=1
    )


def pack_body(at_ref, mine_ref, theirs_ref, own_ref, cross_ref, local_ref, swap_ref):
    side = at_ref[0]
    quarter = own_ref.shape[3]
    here = pl.ds(pl.multiple_of(side * quarter, quarter), quarter)
    there = pl.ds(pl.multiple_of((1 - side) * quarter, quarter), quarter)
    for slot, source in enumerate((mine_ref, theirs_ref)):
        for stream in range(3):
            local_ref[slot, stream] = source[stream, :, here]
            swap_ref[slot, stream] = source[stream, :, there]
        for stream in range(2):
            own_ref[slot, stream] = source[stream + 1, :, here]
            cross_ref[slot, stream] = source[stream + 1, :, there]


def pack(side, mine, theirs):
    _, rows, half = mine.shape
    quarter = half // 2
    pairs = jax.ShapeDtypeStruct((2, 2, rows, quarter), BF16)
    full = jax.ShapeDtypeStruct((2, 3, rows, quarter), BF16)
    return pl.pallas_call(
        pack_body,
        in_specs=[SMEM, VMEM, VMEM],
        out_specs=[VMEM] * 4,
        out_shape=[pairs, pairs, full, full],
        cost_estimate=cost(0, 16 * rows * half),
        name="pack",
    )(side, mine, theirs)


def onward_body(at_ref, own_ref, cross_ref, out_ref):
    place = at_ref[0]
    for block in range(1, ROW):
        slot = place ^ block

        @pl.when(slot < 2)
        def _():
            out_ref[block - 1] = own_ref[slot]

        @pl.when(slot >= 2)
        def _():
            out_ref[block - 1] = cross_ref[slot - 2]


def onward(place, own, cross):
    return pl.pallas_call(
        onward_body,
        in_specs=[SMEM, VMEM, VMEM],
        out_specs=VMEM,
        out_shape=jax.ShapeDtypeStruct((ROW - 1,) + own.shape[1:], BF16),
        cost_estimate=cost(0, 4 * own.size),
        name="onward",
    )(place, own, cross)


def contig_start(info_ref, docs, position):
    first = jnp.zeros_like(position)
    bound = jnp.int32(0)
    for n in range(docs):
        bound = bound + info_ref[2 + n]
        first = jnp.where(position >= bound, bound, first)
    return first


def attend_body(docs, info_ref, local, swap, own, cross, acc_ref, m_ref, l_ref, q_s, k_s, v_s, sems):
    place, base = info_ref[0], info_ref[1]
    rows, quarter = q_s.shape[1:]
    copies = []

    def bring(source, target):
        copies.append(pltpu.make_async_copy(source, target, sems.at[len(copies)]))
        copies[-1].start()

    for slot in range(ROW):
        row = local.at[slot] if slot < 2 else swap.at[slot - 2]
        old = own.at[slot] if slot < 2 else cross.at[slot - 2]
        block = place ^ slot
        older = pl.ds(pl.multiple_of(block * rows, rows), rows)
        newer = pl.ds(pl.multiple_of((ROW + block) * rows, rows), rows)
        bring(row.at[0], q_s.at[block])
        bring(row.at[1], k_s.at[newer])
        bring(row.at[2], v_s.at[newer])
        bring(old.at[0], k_s.at[older])
        bring(old.at[1], v_s.at[older])
    for copy in copies:
        copy.wait()

    scale = 1.0 / math.sqrt(HEAD)
    for block in range(ROW):
        width = (ROW + 1 + block) * rows
        position = base + block * rows + lax.broadcasted_iota(jnp.int32, (rows, 1), 0)
        first = contig_start(info_ref, docs, position)
        at = base - ROW * rows + lax.broadcasted_iota(jnp.int32, (rows, width), 1)
        allowed = (at >= first) & (at <= position)
        for head in range(quarter // HEAD):
            lanes = slice(head * HEAD, (head + 1) * HEAD)
            scores = lax.dot_general(
                q_s[block, :, lanes],
                k_s[0:width, lanes],
                (((1,), (1,)), ((), ())),
                preferred_element_type=F32,
            )
            scores = jnp.where(allowed, scores * scale, -jnp.inf)
            top = jnp.max(scores, axis=1, keepdims=True)
            weight = jnp.exp(scores - top)
            m_ref[block, :, head : head + 1] = top
            l_ref[block, :, head : head + 1] = jnp.sum(weight, axis=1, keepdims=True)
            acc_ref[block, :, lanes] = jnp.dot(
                weight.astype(BF16), v_s[0:width, lanes], preferred_element_type=F32
            )


def attend(info, docs, local, swap, own, cross):
    _, _, rows, quarter = local.shape
    heads = quarter // HEAD
    return pl.pallas_call(
        functools.partial(attend_body, docs),
        in_specs=[SMEM, ANY, ANY, ANY, ANY],
        out_specs=[VMEM] * 3,
        out_shape=[
            jax.ShapeDtypeStruct((ROW, rows, quarter), F32),
            jax.ShapeDtypeStruct((ROW, rows, heads), F32),
            jax.ShapeDtypeStruct((ROW, rows, heads), F32),
        ],
        scratch_shapes=[
            pltpu.VMEM((ROW, rows, quarter), BF16),
            pltpu.VMEM((2 * ROW * rows, quarter), BF16),
            pltpu.VMEM((2 * ROW * rows, quarter), BF16),
            pltpu.SemaphoreType.DMA((5 * ROW,)),
        ],
        cost_estimate=cost(26 * 4 * rows * rows * quarter, 14 * ROW * rows * quarter, 26 * heads * rows * rows),
        name="attend",
    )(info, local, swap, own, cross)


def attend_last_body(docs, info_ref, local, swap, oldest, acc_ref, m_ref, l_ref, out_ref, q_s, sems):
    place, base = info_ref[0], info_ref[1]
    rows, quarter = q_s.shape[1:]
    copies = []
    for slot in range(ROW):
        row = local.at[slot] if slot < 2 else swap.at[slot - 2]
        copies.append(pltpu.make_async_copy(row.at[0], q_s.at[place ^ slot], sems.at[slot]))
        copies[-1].start()
    for copy in copies:
        copy.wait()
    scale = 1.0 / math.sqrt(HEAD)
    for block in range(ROW):
        slot = place ^ block
        seen = ROW - 1 - block
        width = seen * rows
        if seen:
            position = base + block * rows + lax.broadcasted_iota(jnp.int32, (rows, 1), 0)
            first = contig_start(info_ref, docs, position)
            at = base - (ROW + seen) * rows + lax.broadcasted_iota(jnp.int32, (rows, width), 1)
            allowed = at >= first
        for head in range(quarter // HEAD):
            lanes = slice(head * HEAD, (head + 1) * HEAD)
            total = acc_ref[block, :, lanes]
            below = l_ref[block, :, head : head + 1]
            if seen:
                keys = oldest[block : ROW - 1, 0, :, lanes].reshape(width, HEAD)
                values = oldest[block : ROW - 1, 1, :, lanes].reshape(width, HEAD)
                scores = lax.dot_general(
                    q_s[block, :, lanes],
                    keys,
                    (((1,), (1,)), ((), ())),
                    preferred_element_type=F32,
                )
                scores = jnp.where(allowed, scores * scale, -jnp.inf)
                past = m_ref[block, :, head : head + 1]
                top = jnp.maximum(past, jnp.max(scores, axis=1, keepdims=True))
                fade = jnp.exp(past - top)
                weight = jnp.exp(scores - top)
                below = below * fade + jnp.sum(weight, axis=1, keepdims=True)
                total = total * fade + jnp.dot(
                    weight.astype(BF16), values, preferred_element_type=F32
                )
            out_ref[slot, :, lanes] = (total / below).astype(BF16)


def attend_last(info, docs, local, swap, oldest, acc, top, below):
    _, _, rows, quarter = local.shape
    heads = quarter // HEAD
    return pl.pallas_call(
        functools.partial(attend_last_body, docs),
        in_specs=[SMEM, ANY, ANY, VMEM, VMEM, VMEM, VMEM],
        out_specs=VMEM,
        out_shape=jax.ShapeDtypeStruct((ROW, rows, quarter), BF16),
        scratch_shapes=[pltpu.VMEM((ROW, rows, quarter), BF16), pltpu.SemaphoreType.DMA((ROW,))],
        cost_estimate=cost(6 * 4 * rows * rows * quarter, 12 * ROW * rows * quarter, 6 * heads * rows * rows),
        name="attend_last",
    )(info, local, swap, oldest, acc, top, below)


def assemble_body(at_ref, kept, paired, swapped, out_ref):
    place = at_ref[0]
    quarter = kept.shape[2]
    pieces = (kept.at[0], paired.at[0], swapped.at[0], swapped.at[1])
    for slot, piece in enumerate(pieces):
        maker = place ^ slot
        which = 2 * (maker % 2) + maker // 2
        out_ref[:, pl.ds(pl.multiple_of(which * quarter, quarter), quarter)] = piece[...]


def assemble(place, kept, paired, swapped):
    _, rows, quarter = kept.shape
    return pl.pallas_call(
        assemble_body,
        in_specs=[SMEM, VMEM, VMEM, VMEM],
        out_specs=VMEM,
        out_shape=jax.ShapeDtypeStruct((rows, ROW * quarter), BF16),
        cost_estimate=cost(0, 16 * rows * quarter),
        name="assemble",
    )(place, kept, paired, swapped)


def on_device(hyena_qkv, short_weight, filter_rate, filter_residue, attn_qkv, doc_lengths):
    rows, _, channels = attn_qkv.shape
    groups, modes = filter_rate.shape
    docs = doc_lengths.shape[0]
    index = lax.axis_index("ctx")
    place = index % ROW
    core, side = place % 2, place // 2
    half = channels // 2
    spot = place.reshape(1).astype(jnp.int32)
    info = jnp.concatenate(
        [spot, ((index - place) * rows).reshape(1).astype(jnp.int32), doc_lengths]
    )

    take = lambda which: lax.dynamic_slice_in_dim(attn_qkv, which * half, half, 2).transpose(1, 0, 2)
    mine = take(core)
    theirs = flip(take(1 - core), "ctx", 1)
    own, cross, local, swap = pack(side.reshape(1).astype(jnp.int32), mine, theirs)
    own = ahead(own, "ctx", ROW)
    cross = ahead(cross, "ctx", ROW, 2)
    swap = flip(swap, "ctx", 2)
    oldest = ahead(onward(spot, own, cross), "ctx", ROW)

    halo = ahead(hyena_qkv[rows - 2 :], "ctx", 1)
    blocks = channels // LANES
    rate_rows = filter_rate.reshape(blocks, 1, -1)
    res_rows = filter_residue.reshape(blocks, 1, -1)
    near, query, ends = hyena_main(
        hyena_qkv.transpose(1, 0, 2), halo.transpose(1, 0, 2), short_weight, rate_rows, res_rows, modes
    )
    carried = scan_states(ends, filter_rate, rows)
    hyena_out = hyena_finish(near, query, carried, rate_rows, res_rows, modes)

    acc, top, below = attend(info, docs, local, swap, own, cross)
    made = attend_last(info, docs, local, swap, oldest, acc, top, below)
    paired = flip(made[1::2], "ctx", 1)
    swapped = flip(jnp.stack([made[2], paired[1]]), "ctx", 2)
    attn_out = assemble(spot, made, paired, swapped)
    return (hyena_out, attn_out)


def solution(mesh):
    in_specs = (
        P(("group", "ctx"), None, None),
        P(),
        P(),
        P(),
        P(("group", "ctx"), None, None),
        P("group"),
    )
    out_specs = (P(("group", "ctx"), None), P(("group", "ctx"), None))
    return jax.shard_map(
        on_device, mesh=mesh, in_specs=in_specs, out_specs=out_specs, check_vma=False
    )
```

time: 268 us -> 129 us (0.48)
  the two profiles are of different devices: /device:TPU:15 before, /device:TPU:0 now
where the time goes in v1:
time: 129 us; the launch traced here: 128 us
  starting transfers between devices  53.6 us (42%)
  Pallas kernels  46.9 us (36%)
  local copies, waits for them, and re-layouts  12.7 us (10%)
  waiting for transfers between devices  11.7 us (9%)
  other arithmetic  1.51 us (1%)
    ppermute x7, starting transfers between devices, ahead(): return lax.ppermute(value, axis, pairs)  36.6 us
    ppermute x6, starting transfers between devices, flip(): return lax.ppermute(value, axis, [(at, at ^ bit) for at in range(count)])  17 us
    pallas_call x1, Pallas kernels, hyena_main(): pl.pallas_call(functools.partial(hyena_main_body, modes), grid=(blocks,),...  12.7 us
    pallas_call x1, Pallas kernels, hyena_finish(): pl.pallas_call(functools.partial(hyena_out_body, modes), grid=(blocks,),...  10.2 us
    pallas_call x1, Pallas kernels, attend(): pl.pallas_call(functools.partial(attend_body, docs), in_specs=[SMEM, ANY,...  9.27 us
    ppermute x7, waiting for transfers between devices, ahead(): return lax.ppermute(value, axis, pairs)  8.91 us
    pallas_call x1, Pallas kernels, attend_last(): pl.pallas_call(functools.partial(attend_last_body, docs), in_specs=[SMEM,...  7.66 us
    unnamed x26, local copies, waits for them, and re-layouts  5.19 us
  transfers between devices with their start and end apart: 13, of which 4 were waited for; matrix products, arithmetic and copies ran while one was open for 5% of the time, Pallas kernels for 33%

profile of v1, /device:TPU:0, one launch (start us, length us, event | category | flops | bytes accessed | tf_op | source)
XLA Modules:
  0.0 127.5 jit_solution(1962262301169570032)
XLA Ops:
  0.7 2.5 %dynamic-slice_bitcast_fusion = (bf16[3,128,1024]{2,1,0:T(8,128)(2,1)S(1)}, bf16[3,128,1024]{2,1,0:T(8,128)(2,1)}) fusion(bf16[128,3,2048]{2,0,1:T(8,128)(2,1)} %param.10, s32[]{:T(128)S(6)} %select_n.74, s32[]{:T(128)S(6)} %select_n.73), kind=kLoop, calls=%fused_computation | loop fusion | bytes 3145736 | tf_op jit(solution)/shard_map/transpose | solution.py:435
  3.6 1.9 %collective-permute-done.6.theirs_ref = bf16[3,128,1024]{2,1,0:T(8,128)(2,1)S(1)} collective-permute-done((bf16[3,128,1024]{2,1,0:T(8,128)(2,1)S(1)}, bf16[3,128,1024]{2,1,0:T(8,128)(2,1)S(1)}, u32[]{:S(2)}, u32[]{:S(2)}) %collective-permute-start.6) | collective-permute-done | bytes 786464 | tf_op jit(solution)/shard_map/ppermute | solution.py:21
  5.5 0.9 copy-done.2
  6.5 2.9 %pack.1 = (bf16[2,2,128,512]{3,2,1,0:T(8,128)(2,1)}, bf16[2,2,128,512]{3,2,1,0:T(8,128)(2,1)}, bf16[2,3,128,512]{3,2,1,0:T(8,128)(2,1)}, bf16[2,3,128,512]{3,2,1,0:T(8,128)(2,1)}) custom-call(s32[1]{0:T(128)} %bitcast.7.at_ref, bf16[3,128,1024]{2,1,0:T(8,128)(2,1)} %get-tuple-element.26.mine_ref, bf16[3,128,1024]{2,1,0:T(8,128)(2,1)} %copy-done.2), custom_call_target="tpu_custom_call" | custom-call | bytes 2097152 | tf_op jit(solution)/shard_map/pack/pallas_call | solution.py:226
  9.4 4.9 %collective-permute-start.8 = (bf16[2,2,128,512]{3,2,1,0:T(8,128)(2,1)}, bf16[2,2,128,512]{3,2,1,0:T(8,128)(2,1)S(1)}, u32[]{:S(2)}, u32[]{:S(2)}) collective-permute-start(bf16[2,2,128,512]{3,2,1,0:T(8,128)(2,1)} %get-tuple-element.17), channel_id=1, source_target_pairs={{0,4},{1,5},{2,6},{3,7},{4,8},{5,9},{6,10},{7,11},{8,12},{9,13},{1... | collective-permute-start | bytes 1572872 | tf_op jit(solution)/shard_map/ppermute | solution.py:27
  14.3 4.4 %collective-permute-start.9 = (bf16[2,2,128,512]{3,2,1,0:T(8,128)(2,1)}, bf16[2,2,128,512]{3,2,1,0:T(8,128)(2,1)S(1)}, u32[]{:S(2)}, u32[]{:S(2)}) collective-permute-start(bf16[2,2,128,512]{3,2,1,0:T(8,128)(2,1)} %get-tuple-element.18), channel_id=1, source_target_pairs={{0,6},{1,7},{2,4},{3,5},{4,10},{5,11},{6,8},{7,9},{8,14},{9,15},{1... | collective-permute-start | bytes 1572872 | tf_op jit(solution)/shard_map/ppermute | solution.py:27
  18.7 0.9 slice.12
  19.6 1.5 %collective-permute-start = (bf16[2,3,2048]{2,0,1:T(2,128)(2,1)S(1)}, bf16[2,3,2048]{2,0,1:T(2,128)(2,1)S(1)}, u32[]{:S(2)}, u32[]{:S(2)}) collective-permute-start(bf16[2,3,2048]{2,0,1:T(2,128)(2,1)S(1)} %slice.12), channel_id=1, source_target_pairs={{0,1},{1,2},{2,3},{3,4},{4,5},{5,6},{6,7},{7,8},{8,9},{9,10},{10,1... | collective-permute-start | bytes 73736 | tf_op jit(solution)/shard_map/ppermute | solution.py:27
  21.3 0.7 reshape.22
  22.0 0.7 reshape.23
  23.4 12.7 %hyena_main.1 = (f32[128,2048]{1,0:T(8,128)}, f32[128,2048]{1,0:T(8,128)}, f32[16,2048]{1,0:T(8,128)}) custom-call(bf16[3,128,2048]{2,1,0:T(8,128)(2,1)} %bitcast.17, bf16[3,2,2048]{2,1,0:T(2,128)(2,1)} %bitcast.18, f32[3,3,2048]{2,1,0:T(4,128)} %w_ref.1, f32[16,1,128]{2,1,0:T(1,128)} %bitcast.13, f32[16,1,128]{2,1,0:T(1,128)} %bitcast.15), custom_call_target="tpu_custom_call" | custom-call | flops 536870912 | bytes 2097152 | tf_op jit(solution)/shard_map/hyena_main/pallas_call | solution.py:99
  36.1 0.8 constant_dynamic-slice_fusion
  36.9 1.0 collective-permute-start.1
  38.9 14.8 %collective-permute-start.7 = (bf16[2,3,128,512]{3,2,1,0:T(8,128)(2,1)}, bf16[2,3,128,512]{3,2,1,0:T(8,128)(2,1)S(1)}, u32[]{:S(2)}, u32[]{:S(2)}) collective-permute-start(bf16[2,3,128,512]{3,2,1,0:T(8,128)(2,1)} %get-tuple-element.16), channel_id=1, source_target_pairs={{0,2},{1,3},{2,0},{3,1},{4,6},{5,7},{6,4},{7,5},{8,10},{9,11},{10,... | collective-permute-start | bytes 2359304 | tf_op jit(solution)/shard_map/ppermute | solution.py:21
  53.7 0.8 copy-done.4
  54.7 2.2 %onward.1 = bf16[3,2,128,512]{3,2,1,0:T(8,128)(2,1)} custom-call(s32[1]{0:T(128)} %bitcast.5.at_ref, bf16[2,2,128,512]{3,2,1,0:T(8,128)(2,1)} %copy-done.4, bf16[2,2,128,512]{3,2,1,0:T(8,128)(2,1)} %copy-done.5), custom_call_target="tpu_custom_call" | custom-call | bytes 1048576 | tf_op jit(solution)/shard_map/onward/pallas_call | solution.py:251
  56.8 3.8 %collective-permute-start.10 = (bf16[3,2,128,512]{3,2,1,0:T(8,128)(2,1)}, bf16[3,2,128,512]{3,2,1,0:T(8,128)(2,1)S(1)}, u32[]{:S(2)}, u32[]{:S(2)}) collective-permute-start(bf16[3,2,128,512]{3,2,1,0:T(8,128)(2,1)} %onward.1), channel_id=1, source_target_pairs={{0,4},{1,5},{2,6},{3,7},{4,8},{5,9},{6,10},{7,11},{8,12},{9,13},{1... | collective-permute-start | bytes 2359304 | tf_op jit(solution)/shard_map/ppermute | solution.py:27
  60.7 3.9 %collective-permute-start.2 = (f32[16,1024]{1,0:T(8,128)S(1)}, f32[16,1024]{1,0:T(8,128)S(1)}, u32[]{:S(2)}, u32[]{:S(2)}) collective-permute-start(f32[16,1024]{1,0:T(8,128)S(1)} %select_add_fusion), channel_id=1, source_target_pairs={{0,2},{1,3},{2,4},{3,5},{4,6},{5,7},{6,8},{7,9},{8,10},{9,11},{10,... | collective-permute-start | bytes 196616 | tf_op jit(solution)/shard_map/ppermute | solution.py:27
  64.6 7.7 %collective-permute-done.2 = f32[16,1024]{1,0:T(8,128)S(1)} collective-permute-done((f32[16,1024]{1,0:T(8,128)S(1)}, f32[16,1024]{1,0:T(8,128)S(1)}, u32[]{:S(2)}, u32[]{:S(2)}) %collective-permute-start.2) | collective-permute-done | bytes 65568 | tf_op jit(solution)/shard_map/ppermute | solution.py:27
  72.3 12.9 %collective-permute-start.3 = (f32[16,1024]{1,0:T(8,128)S(1)}, f32[16,1024]{1,0:T(8,128)S(1)}, u32[]{:S(2)}, u32[]{:S(2)}) collective-permute-start(f32[16,1024]{1,0:T(8,128)S(1)} %multiply_add_fusion.4), channel_id=1, source_target_pairs={{0,4},{1,5},{2,6},{3,7},{4,8},{5,9},{6,10},{7,11},{8,12},{9,13},{1... | collective-permute-start | bytes 196616 | tf_op jit(solution)/shard_map/ppermute | solution.py:27
  85.2 0.7 pad_add_fusion.info_ref
  85.9 1.2 collective-permute-done.3
  87.1 5.3 %collective-permute-start.4 = (f32[16,1024]{1,0:T(8,128)S(1)}, f32[16,1024]{1,0:T(8,128)S(1)}, u32[]{:S(2)}, u32[]{:S(2)}) collective-permute-start(f32[16,1024]{1,0:T(8,128)S(1)} %multiply_add_fusion.2), channel_id=1, source_target_pairs={{0,8},{1,9},{2,10},{3,11},{4,12},{5,13},{6,14},{7,15},{16,24},{17,... | collective-permute-start | bytes 196616 | tf_op jit(solution)/shard_map/ppermute | solution.py:27
  92.4 0.9 copy-done
  93.3 9.3 %attend.1 = (f32[4,128,512]{2,1,0:T(8,128)}, f32[4,128,4]{2,1,0:T(8,128)}, f32[4,128,4]{2,1,0:T(8,128)}) custom-call(s32[6]{0:T(128)} %pad_add_fusion.info_ref, bf16[2,3,128,512]{3,2,1,0:T(8,128)(2,1)} %get-tuple-element.15.local, bf16[2,3,128,512]{3,2,1,0:T(8,128)(2,1)} %copy-done, bf16[2,2,128,512]{3,2,1,0:T(8,128)(2,1)} %copy-done.4, ...), custom_call_target="tpu_custom_call" | custom-call | flops 872415232 | bytes 3670016 | tf_op jit(solution)/shard_map/attend/pallas_call | solution.py:321
  102.6 0.9 copy-done.1
  103.5 7.7 %attend_last.1.kept = bf16[4,128,512]{2,1,0:T(8,128)(2,1)} custom-call(s32[6]{0:T(128)} %pad_add_fusion.info_ref, bf16[2,3,128,512]{3,2,1,0:T(8,128)(2,1)} %get-tuple-element.15.local, bf16[2,3,128,512]{3,2,1,0:T(8,128)(2,1)} %copy-done, bf16[3,2,128,512]{3,2,1,0:T(8,128)(2,1)} %copy-done.1, f32[4,128,512]{2,1,0:T(8,128)} %get-tuple-element.19.acc_ref, ...), custom_call_target="tpu_custom_call" | custom-call | flops 201326592 | bytes 3145728 | tf_op jit(solution)/shard_map/attend_last/pallas_call | solution.py:389
  111.2 1.0 slice.13
  112.9 0.9 collective-permute-done.11.paired
  114.6 10.2 %hyena_finish.1 = bf16[128,2048]{1,0:T(8,128)(2,1)} custom-call(f32[128,2048]{1,0:T(8,128)} %get-tuple-element.12.near_ref, f32[128,2048]{1,0:T(8,128)} %get-tuple-element.13.q_ref, f32[16,2048]{1,0:T(8,128)} %pad_maximum_fusion.1.carried_ref, f32[16,1,128]{2,1,0:T(1,128)} %bitcast.14, f32[16,1,128]{2,1,0:T(1,128)} %bitcast.16), custom_call_target="tpu_custom_call" | custom-call | flops 201326592 | bytes 2621440 | tf_op jit(solution)/shard_map/hyena_finish/pallas_call | solution.py:160
  124.8 0.7 copy-done.7
  125.5 2.0 %assemble.1 = bf16[128,2048]{1,0:T(8,128)(2,1)} custom-call(s32[1]{0:T(128)} %bitcast.5.at_ref, bf16[4,128,512]{2,1,0:T(8,128)(2,1)} %attend_last.1.kept, bf16[2,128,512]{2,1,0:T(8,128)(2,1)} %copy-done.3, bf16[2,128,512]{2,1,0:T(8,128)(2,1)} %copy-done.7), custom_call_target="tpu_custom_call" | custom-call | bytes 1048576 | tf_op jit(solution)/shard_map/assemble/pallas_call | solution.py:412
  (46 shorter events, 4.0 us)
Async XLA Ops:
  3.1 18.0 %copy-start.8 = (f32[128,16]{0,1:T(8,128)S(1)}, f32[128,16]{0,1:T(8,128)}, u32[]{:S(2)}) copy-start(f32[128,16]{0,1:T(8,128)} %param.8) | copy-start | bytes 24580
  3.1 18.8 %copy-start.9 = (f32[128,16]{0,1:T(8,128)S(1)}, f32[128,16]{0,1:T(8,128)}, u32[]{:S(2)}) copy-start(f32[128,16]{0,1:T(8,128)} %param.9) | copy-start | bytes 24580
  3.1 2.4 %collective-permute-start.6 = (bf16[3,128,1024]{2,1,0:T(8,128)(2,1)S(1)}, bf16[3,128,1024]{2,1,0:T(8,128)(2,1)S(1)}, u32[]{:S(2)}, u32[]{:S(2)}) collective-permute-start(bf16[3,128,1024]{2,1,0:T(8,128)(2,1)S(1)} %get-tuple-element.25), channel_id=1, source_target_pairs={{0,1},{1,0},{2,3},{3,2},{4,5},{5,4},{6,7},{7,6},{8,9},{9,8},{10,11... | collective-permute-start | bytes 2359304 | tf_op jit(solution)/shard_map/ppermute | solution.py:21
  5.5 0.9 copy-start.2
  9.4 44.3 %collective-permute-start.8 = (bf16[2,2,128,512]{3,2,1,0:T(8,128)(2,1)}, bf16[2,2,128,512]{3,2,1,0:T(8,128)(2,1)S(1)}, u32[]{:S(2)}, u32[]{:S(2)}) collective-permute-start(bf16[2,2,128,512]{3,2,1,0:T(8,128)(2,1)} %get-tuple-element.17), channel_id=1, source_target_pairs={{0,4},{1,5},{2,6},{3,7},{4,8},{5,9},{6,10},{7,11},{8,12},{9,13},{1... | collective-permute-start | bytes 1572872 | tf_op jit(solution)/shard_map/ppermute | solution.py:27
  14.3 39.4 %collective-permute-start.9 = (bf16[2,2,128,512]{3,2,1,0:T(8,128)(2,1)}, bf16[2,2,128,512]{3,2,1,0:T(8,128)(2,1)S(1)}, u32[]{:S(2)}, u32[]{:S(2)}) collective-permute-start(bf16[2,2,128,512]{3,2,1,0:T(8,128)(2,1)} %get-tuple-element.18), channel_id=1, source_target_pairs={{0,6},{1,7},{2,4},{3,5},{4,10},{5,11},{6,8},{7,9},{8,14},{9,15},{1... | collective-permute-start | bytes 1572872 | tf_op jit(solution)/shard_map/ppermute | solution.py:27
  19.6 3.1 %collective-permute-start = (bf16[2,3,2048]{2,0,1:T(2,128)(2,1)S(1)}, bf16[2,3,2048]{2,0,1:T(2,128)(2,1)S(1)}, u32[]{:S(2)}, u32[]{:S(2)}) collective-permute-start(bf16[2,3,2048]{2,0,1:T(2,128)(2,1)S(1)} %slice.12), channel_id=1, source_target_pairs={{0,1},{1,2},{2,3},{3,4},{4,5},{5,6},{6,7},{7,8},{8,9},{9,10},{10,1... | collective-permute-start | bytes 73736 | tf_op jit(solution)/shard_map/ppermute | solution.py:27
  22.7 0.6 copy-start.11
  36.9 23.7 %collective-permute-start.1 = (f32[16,1024]{1,0:T(8,128)S(1)}, f32[16,1024]{1,0:T(8,128)S(1)}, u32[]{:S(2)}, u32[]{:S(2)}) collective-permute-start(f32[16,1024]{1,0:T(8,128)S(1)} %constant_dynamic-slice_fusion), channel_id=1, source_target_pairs={{0,1},{1,0},{2,3},{3,2},{4,5},{5,4},{6,7},{7,6},{8,9},{9,8},{10,11... | collective-permute-start | bytes 196616 | tf_op jit(solution)/shard_map/ppermute | solution.py:21
  38.3 22.3 %copy-start.6 = (f32[16,2048]{1,0:T(8,128)S(1)}, f32[16,2048]{1,0:T(8,128)}, u32[]{:S(2)}) copy-start(f32[16,2048]{1,0:T(8,128)} %get-tuple-element.14) | copy-start | bytes 393220
  38.3 46.9 %copy-start.10 = (s32[4]{0:T(128)S(1)}, s32[4]{0:T(128)}, u32[]{:S(2)}) copy-start(s32[4]{0:T(128)} %param.11) | copy-start | bytes 52
  38.9 53.5 %collective-permute-start.7 = (bf16[2,3,128,512]{3,2,1,0:T(8,128)(2,1)}, bf16[2,3,128,512]{3,2,1,0:T(8,128)(2,1)S(1)}, u32[]{:S(2)}, u32[]{:S(2)}) collective-permute-start(bf16[2,3,128,512]{3,2,1,0:T(8,128)(2,1)} %get-tuple-element.16), channel_id=1, source_target_pairs={{0,2},{1,3},{2,0},{3,1},{4,6},{5,7},{6,4},{7,5},{8,10},{9,11},{10,... | collective-permute-start | bytes 2359304 | tf_op jit(solution)/shard_map/ppermute | solution.py:21
  53.7 0.8 copy-start.4
  53.7 1.0 copy-start.5
  56.8 45.8 %collective-permute-start.10 = (bf16[3,2,128,512]{3,2,1,0:T(8,128)(2,1)}, bf16[3,2,128,512]{3,2,1,0:T(8,128)(2,1)S(1)}, u32[]{:S(2)}, u32[]{:S(2)}) collective-permute-start(bf16[3,2,128,512]{3,2,1,0:T(8,128)(2,1)} %onward.1), channel_id=1, source_target_pairs={{0,4},{1,5},{2,6},{3,7},{4,8},{5,9},{6,10},{7,11},{8,12},{9,13},{1... | collective-permute-start | bytes 2359304 | tf_op jit(solution)/shard_map/ppermute | solution.py:27
  60.7 11.6 %collective-permute-start.2 = (f32[16,1024]{1,0:T(8,128)S(1)}, f32[16,1024]{1,0:T(8,128)S(1)}, u32[]{:S(2)}, u32[]{:S(2)}) collective-permute-start(f32[16,1024]{1,0:T(8,128)S(1)} %select_add_fusion), channel_id=1, source_target_pairs={{0,2},{1,3},{2,4},{3,5},{4,6},{5,7},{6,8},{7,9},{8,10},{9,11},{10,... | collective-permute-start | bytes 196616 | tf_op jit(solution)/shard_map/ppermute | solution.py:27
  72.3 14.8 %collective-permute-start.3 = (f32[16,1024]{1,0:T(8,128)S(1)}, f32[16,1024]{1,0:T(8,128)S(1)}, u32[]{:S(2)}, u32[]{:S(2)}) collective-permute-start(f32[16,1024]{1,0:T(8,128)S(1)} %multiply_add_fusion.4), channel_id=1, source_target_pairs={{0,4},{1,5},{2,6},{3,7},{4,8},{5,9},{6,10},{7,11},{8,12},{9,13},{1... | collective-permute-start | bytes 196616 | tf_op jit(solution)/shard_map/ppermute | solution.py:27
  87.1 25.2 %collective-permute-start.4 = (f32[16,1024]{1,0:T(8,128)S(1)}, f32[16,1024]{1,0:T(8,128)S(1)}, u32[]{:S(2)}, u32[]{:S(2)}) collective-permute-start(f32[16,1024]{1,0:T(8,128)S(1)} %multiply_add_fusion.2), channel_id=1, source_target_pairs={{0,8},{1,9},{2,10},{3,11},{4,12},{5,13},{6,14},{7,15},{16,24},{17,... | collective-permute-start | bytes 196616 | tf_op jit(solution)/shard_map/ppermute | solution.py:27
  92.4 0.9 copy-start
  102.6 0.9 copy-start.1
  111.2 2.6 %slice-start = ((bf16[4,128,512]{2,1,0:T(8,128)(2,1)}), bf16[1,128,512]{2,1,0:T(8,128)(2,1)S(1)}, s32[]{:S(2)}) async-start(bf16[4,128,512]{2,1,0:T(8,128)(2,1)} %attend_last.1.kept), calls=%async_computation | async-start | bytes 262144 | tf_op jit(solution)/shard_map/slice | solution.py:457
  112.2 1.6 %collective-permute-start.11 = (bf16[2,128,512]{2,1,0:T(8,128)(2,1)S(1)}, bf16[2,128,512]{2,1,0:T(8,128)(2,1)S(1)}, u32[]{:S(2)}, u32[]{:S(2)}) collective-permute-start(bf16[2,128,512]{2,1,0:T(8,128)(2,1)S(1)} %slice.13), channel_id=1, source_target_pairs={{0,1},{1,0},{2,3},{3,2},{4,5},{5,4},{6,7},{7,6},{8,9},{9,8},{10,11... | collective-permute-start | bytes 786440 | tf_op jit(solution)/shard_map/ppermute | solution.py:21
  112.3 1.6 %collective-permute-start.5 = (f32[16,1024]{1,0:T(8,128)S(1)}, f32[16,1024]{1,0:T(8,128)S(1)}, u32[]{:S(2)}, u32[]{:S(2)}) collective-permute-start(f32[16,1024]{1,0:T(8,128)S(1)} %get-tuple-element.22), channel_id=1, source_target_pairs={{0,1},{1,0},{2,3},{3,2},{4,5},{5,4},{6,7},{7,6},{8,9},{9,8},{10,11... | collective-permute-start | bytes 196616 | tf_op jit(solution)/shard_map/ppermute | solution.py:21
  113.8 11.0 %copy-start.3 = (bf16[2,128,512]{2,1,0:T(8,128)(2,1)}, bf16[2,128,512]{2,1,0:T(8,128)(2,1)S(1)}, u32[]{:S(2)}) copy-start(bf16[2,128,512]{2,1,0:T(8,128)(2,1)S(1)} %collective-permute-done.11.paired) | copy-start | bytes 786436
  113.8 11.0 %collective-permute-start.12 = (bf16[2,128,512]{2,1,0:T(8,128)(2,1)S(1)}, bf16[2,128,512]{2,1,0:T(8,128)(2,1)S(1)}, u32[]{:S(2)}, u32[]{:S(2)}) collective-permute-start(bf16[2,128,512]{2,1,0:T(8,128)(2,1)S(1)} %pad_maximum_fusion), channel_id=1, source_target_pairs={{0,2},{1,3},{2,0},{3,1},{4,6},{5,7},{6,4},{7,5},{8,10},{9,11},{10,... | collective-permute-start | bytes 786440 | tf_op jit(solution)/shard_map/ppermute | solution.py:21
  124.8 0.7 copy-start.7

commit v2 on v1

v2 whole, which is shorter than its diff:
```python
import functools
import math

import jax
import jax.numpy as jnp
from jax import lax
from jax.experimental import pallas as pl
from jax.experimental.pallas import tpu as pltpu
from jax.sharding import PartitionSpec as P


HEAD = 128
LANES = 128
ROW = 4

F32 = jnp.float32
BF16 = jnp.bfloat16


def flip(value, axis, bit):
    count = lax.axis_size(axis)
    return lax.ppermute(value, axis, [(at, at ^ bit) for at in range(count)])


def ahead(value, axis, steps, bit=0):
    count = lax.axis_size(axis)
    pairs = [(at, (at + steps) ^ bit) for at in range(count - steps)]
    return lax.ppermute(value, axis, pairs)


def limits(mib):
    return pltpu.CompilerParams(vmem_limit_bytes=mib << 20)


def cost(flops, moved, exps=0):
    return pl.CostEstimate(flops=flops, bytes_accessed=moved, transcendentals=exps)


VMEM = pl.BlockSpec(memory_space=pltpu.VMEM)
SMEM = pl.BlockSpec(memory_space=pltpu.SMEM)
ANY = pl.BlockSpec(memory_space=pl.ANY)


def same_filter(modes, width, terms, lanes):
    row_at = lax.broadcasted_iota(jnp.int32, (terms, lanes), 0)
    lane_at = lax.broadcasted_iota(jnp.int32, (terms, lanes), 1)
    kept = None
    for g in range(terms // modes):
        both = (
            (row_at >= g * modes)
            & (row_at < (g + 1) * modes)
            & (lane_at >= g * width)
            & (lane_at < (g + 1) * width)
        )
        kept = both if kept is None else kept | both
    return kept


def hyena_main_body(modes, x_ref, halo_ref, w_ref, rate_ref, res_ref, near_ref, q_ref, ends_ref, taps_s, u_s):
    rows = x_ref.shape[1]
    parts, _, terms = rate_ref.shape
    lanes = x_ref.shape[2] // parts
    filters = terms // modes
    width = lanes // filters
    row_at = lax.broadcasted_iota(jnp.int32, (rows, lanes), 0)
    lane_at = lax.broadcasted_iota(jnp.int32, (rows, lanes), 1)
    lag = (rows - 1 - lax.broadcasted_iota(jnp.int32, (terms, rows), 1)).astype(F32)
    own = same_filter(modes, width, terms, lanes)
    zero = jnp.zeros((rows, lanes), BF16)

    for part in range(parts):
        at = slice(part * lanes, (part + 1) * lanes)

        def feature(stream):
            here = x_ref[stream, :, at].astype(F32)
            halo = halo_ref[stream, :, at].astype(F32)
            one = jnp.where(row_at == 0, halo[1:2], pltpu.roll(here, 1, 0))
            two = pltpu.roll(here, 2, 0)
            two = jnp.where(row_at == 0, halo[0:1], jnp.where(row_at == 1, halo[1:2], two))
            tap = [w_ref[n, stream : stream + 1, at] for n in range(3)]
            return tap[0] * here + tap[1] * one + tap[2] * two

        q_ref[:, at] = feature(0)
        mixed = (feature(1) * feature(2)).astype(BF16)

        coeff = res_ref[part] * jnp.sqrt(2.0 * rate_ref[part] / modes)
        rate = jnp.broadcast_to(rate_ref[part], (rows, terms)).T
        coeff = jnp.broadcast_to(coeff, (rows, terms)).T
        powers = jnp.exp(-rate * lag)
        backward = jnp.sum((coeff * powers).reshape(filters, modes, rows), axis=1)
        for g in range(filters):
            spread = jnp.broadcast_to(backward[g : g + 1], (rows, rows))
            shifted = pltpu.roll(spread, 1, 1, stride=1, stride_axis=0)
            kept = jnp.where(lane_at <= row_at, shifted, 0.0)
            taps_s[part, :, g * rows : (g + 1) * rows] = kept.astype(BF16)
            mine = (lane_at >= g * width) & (lane_at < (g + 1) * width)
            u_s[part, g * rows : (g + 1) * rows, :] = jnp.where(mine, mixed, zero)
        near_ref[:, at] = jnp.dot(taps_s[part], u_s[part], preferred_element_type=F32)

        high = powers.astype(BF16)
        low = (powers - high.astype(F32)).astype(BF16)
        ends = jnp.dot(high, mixed, preferred_element_type=F32) + jnp.dot(
            low, mixed, preferred_element_type=F32
        )
        ends_ref[:, at] = jnp.sum(jnp.where(own, ends, 0.0).reshape(filters, modes, lanes), axis=0)


STEPS = 4


def hyena_main(streams, halo, short_weight, rate_rows, res_rows, modes):
    _, rows, channels = streams.shape
    blocks, _, terms = rate_rows.shape
    parts = blocks // STEPS
    wide = channels // STEPS
    lanes = channels // blocks
    filters = terms // modes
    by_block = lambda n: (0, n)
    lead = lambda n: (0, 0, n)
    whole = lambda n: (n, 0, 0)
    return pl.pallas_call(
        functools.partial(hyena_main_body, modes),
        grid=(STEPS,),
        in_specs=[
            pl.BlockSpec((3, rows, wide), lead),
            pl.BlockSpec((3, 2, wide), lead),
            pl.BlockSpec((3, 3, wide), lead),
            pl.BlockSpec((parts, 1, terms), whole),
            pl.BlockSpec((parts, 1, terms), whole),
        ],
        out_specs=[
            pl.BlockSpec((rows, wide), by_block),
            pl.BlockSpec((rows, wide), by_block),
            pl.BlockSpec((modes, wide), by_block),
        ],
        out_shape=[
            jax.ShapeDtypeStruct((rows, channels), F32),
            jax.ShapeDtypeStruct((rows, channels), F32),
            jax.ShapeDtypeStruct((modes, channels), F32),
        ],
        scratch_shapes=[
            pltpu.VMEM((parts, rows, filters * rows), BF16),
            pltpu.VMEM((parts, filters * rows, lanes), BF16),
        ],
        compiler_params=limits(24),
        cost_estimate=cost(2 * rows * rows * filters * channels, 8 * rows * channels),
        name="hyena_main",
    )(streams, halo, short_weight, rate_rows, res_rows)


def hyena_out_body(modes, near_ref, q_ref, carried_ref, rate_ref, res_ref, out_ref):
    rows = near_ref.shape[0]
    parts, _, terms = rate_ref.shape
    lanes = near_ref.shape[1] // parts
    filters = terms // modes
    width = lanes // filters
    lag = (1 + lax.broadcasted_iota(jnp.int32, (rows, terms), 0)).astype(F32)
    own = same_filter(modes, width, terms, lanes)
    for part in range(parts):
        at = slice(part * lanes, (part + 1) * lanes)
        rate = rate_ref[part]
        coeff = res_ref[part] * jnp.sqrt(2.0 * rate / modes)
        powers = coeff * jnp.exp(-rate * lag)
        p_high = powers.astype(BF16)
        p_low = (powers - p_high.astype(F32)).astype(BF16)
        carried = jnp.where(own, jnp.concatenate([carried_ref[:, at]] * filters, axis=0), 0.0)
        c_high = carried.astype(BF16)
        c_low = (carried - c_high.astype(F32)).astype(BF16)
        far = (
            jnp.dot(p_high, c_high, preferred_element_type=F32)
            + jnp.dot(p_low, c_high, preferred_element_type=F32)
            + jnp.dot(p_high, c_low, preferred_element_type=F32)
        )
        out_ref[:, at] = (q_ref[:, at] * (near_ref[:, at] + far)).astype(BF16)


def hyena_finish(near, query, carried, rate_rows, res_rows, modes):
    rows, channels = near.shape
    blocks, _, terms = rate_rows.shape
    parts = blocks // STEPS
    wide = channels // STEPS
    by_block = lambda n: (0, n)
    whole = lambda n: (n, 0, 0)
    return pl.pallas_call(
        functools.partial(hyena_out_body, modes),
        grid=(STEPS,),
        in_specs=[
            pl.BlockSpec((rows, wide), by_block),
            pl.BlockSpec((rows, wide), by_block),
            pl.BlockSpec((modes, wide), by_block),
            pl.BlockSpec((parts, 1, terms), whole),
            pl.BlockSpec((parts, 1, terms), whole),
        ],
        out_specs=pl.BlockSpec((rows, wide), by_block),
        out_shape=jax.ShapeDtypeStruct((rows, channels), BF16),
        compiler_params=limits(16),
        cost_estimate=cost(6 * rows * terms * channels, 10 * rows * channels),
        name="hyena_finish",
    )(near, query, carried, rate_rows, res_rows)


def scan_states(ends, filter_rate, rows):
    _, channels = ends.shape
    half = channels // 2
    width = channels // filter_rate.shape[0]
    index = lax.axis_index("ctx")
    count = lax.axis_size("ctx") // ROW
    core, side = index % 2, index // 2 % 2
    rate = jnp.repeat(filter_rate.T, width, axis=1)
    take = lambda matrix, which: lax.dynamic_slice_in_dim(matrix, which * half, half, 1)
    rate = take(rate, core)
    decay = lambda blocks: jnp.exp(-rate * float(rows * blocks))
    mine = take(ends, core)
    theirs = flip(take(ends, 1 - core), "ctx", 1)
    even = jnp.where(core == 0, mine, theirs)
    odd = jnp.where(core == 0, theirs, mine)
    chip = decay(1) * even + odd
    other = flip(chip, "ctx", 2)
    left = jnp.where(side == 0, chip, other)
    total = decay(2) * left + jnp.where(side == 0, other, chip)
    before = ahead(total, "ctx", ROW)
    reach = 2
    while reach < count:
        upto = total + decay(ROW) * before
        earlier = ahead(upto, "ctx", ROW * reach)
        before = before + decay(ROW * (reach - 1)) * earlier
        reach *= 2
    before = jnp.where(side == 0, before, decay(2) * before + left)
    second = decay(1) * before + even
    keep = jnp.where(core == 0, before, second)
    back = flip(jnp.where(core == 0, second, before), "ctx", 1)
    return jnp.concatenate(
        [jnp.where(core == 0, keep, back), jnp.where(core == 0, back, keep)], axis=1
    )


def lanes_from(start, size):
    return pl.ds(pl.multiple_of(start * size, size), size)


def halve_body(at_ref, streams_ref, out_ref):
    del at_ref
    out_ref[...] = streams_ref[...]


def halve(which, streams):
    count, rows, channels = streams.shape
    half = channels // 2
    return pl.pallas_call(
        halve_body,
        grid_spec=pltpu.PrefetchScalarGridSpec(
            num_scalar_prefetch=1,
            grid=(1,),
            in_specs=[pl.BlockSpec((count, rows, half), lambda n, at: (0, 0, at[0]))],
            out_specs=pl.BlockSpec((count, rows, half), lambda n, at: (0, 0, 0)),
        ),
        out_shape=jax.ShapeDtypeStruct((count, rows, half), streams.dtype),
        compiler_params=limits(8),
        cost_estimate=cost(0, 4 * count * rows * half),
        name="halve",
    )(which, streams)


def pack_body(first, at_ref, streams_ref, theirs_ref, *outs):
    core, side = at_ref[0], at_ref[1]
    quarter = theirs_ref.shape[2] // 2
    for out, away in zip(outs, (0, 1)[-len(outs) :]):
        to = 1 - side if away else side
        for stream in range(first, 3):
            out[0, stream - first] = streams_ref[stream, :, lanes_from(2 * core + to, quarter)]
            out[1, stream - first] = theirs_ref[stream, :, lanes_from(to, quarter)]


def pack(where, streams, theirs, first, amount):
    _, rows, half = theirs.shape
    shape = jax.ShapeDtypeStruct((2, 3 - first, rows, half // 2), BF16)
    return pl.pallas_call(
        functools.partial(pack_body, first),
        in_specs=[SMEM, VMEM, VMEM],
        out_specs=[VMEM] * amount,
        out_shape=[shape] * amount,
        compiler_params=limits(10),
        cost_estimate=cost(0, 8 * amount * rows * half),
        name="pack",
    )(where, streams, theirs)


def onward_body(at_ref, own_ref, cross_ref, out_ref):
    place = at_ref[2]
    for block in range(1, ROW):
        slot = place ^ block

        @pl.when(slot < 2)
        def _():
            out_ref[block - 1] = own_ref[slot]

        @pl.when(slot >= 2)
        def _():
            out_ref[block - 1] = cross_ref[slot - 2]


def onward(where, own, cross):
    return pl.pallas_call(
        onward_body,
        in_specs=[SMEM, VMEM, VMEM],
        out_specs=VMEM,
        out_shape=jax.ShapeDtypeStruct((ROW - 1,) + own.shape[1:], BF16),
        compiler_params=limits(6),
        cost_estimate=cost(0, 4 * own.size),
        name="onward",
    )(where, own, cross)


FIXED = 4


def contig_start(info_ref, docs, position):
    first = jnp.zeros_like(position)
    bound = jnp.int32(0)
    for n in range(docs):
        bound = bound + info_ref[FIXED + n]
        first = jnp.where(position >= bound, bound, first)
    return first


def row_part(info_ref, streams, theirs, swap, slot, stream, quarter):
    core, side = info_ref[0], info_ref[1]
    if slot == 0:
        return streams.at[stream, :, lanes_from(2 * core + side, quarter)]
    if slot == 1:
        return theirs.at[stream, :, lanes_from(side, quarter)]
    return swap.at[slot - 2, stream]


SCALE = math.log2(math.e) / math.sqrt(HEAD)


def attend_body(docs, info_ref, streams, theirs, swap, own, cross, acc_ref, m_ref, l_ref, q_s, k_s, v_s, sems):
    place, base = info_ref[2], info_ref[3]
    rows, quarter = q_s.shape[1:]
    copies = []

    def bring(source, target):
        copies.append(pltpu.make_async_copy(source, target, sems.at[len(copies)]))
        copies[-1].start()

    for slot in range(ROW):
        part = lambda stream: row_part(info_ref, streams, theirs, swap, slot, stream, quarter)
        old = own.at[slot] if slot < 2 else cross.at[slot - 2]
        block = place ^ slot
        older = lanes_from(block, rows)
        newer = lanes_from(ROW + block, rows)
        bring(part(0), q_s.at[block])
        bring(part(1), k_s.at[newer])
        bring(part(2), v_s.at[newer])
        bring(old.at[0], k_s.at[older])
        bring(old.at[1], v_s.at[older])
    for copy in copies:
        copy.wait()

    for block in range(ROW):
        width = (ROW + 1 + block) * rows
        position = base + block * rows + lax.broadcasted_iota(jnp.int32, (rows, 1), 0)
        first = contig_start(info_ref, docs, position)
        at = base - ROW * rows + lax.broadcasted_iota(jnp.int32, (rows, width), 1)
        allowed = (at >= first) & (at <= position)
        for head in range(quarter // HEAD):
            lanes = slice(head * HEAD, (head + 1) * HEAD)
            scores = lax.dot_general(
                q_s[block, :, lanes],
                k_s[0:width, lanes],
                (((1,), (1,)), ((), ())),
                preferred_element_type=F32,
            )
            scores = jnp.where(allowed, scores, -jnp.inf)
            top = jnp.max(scores, axis=1, keepdims=True)
            weight = jnp.exp2((scores - top) * SCALE)
            m_ref[block, :, head : head + 1] = top
            l_ref[block, :, head : head + 1] = jnp.sum(weight, axis=1, keepdims=True)
            acc_ref[block, :, lanes] = jnp.dot(
                weight.astype(BF16), v_s[0:width, lanes], preferred_element_type=F32
            )


def attend(info, docs, streams, theirs, swap, own, cross):
    _, _, rows, quarter = own.shape
    heads = quarter // HEAD
    return pl.pallas_call(
        functools.partial(attend_body, docs),
        in_specs=[SMEM] + [ANY] * 5,
        out_specs=[VMEM] * 3,
        out_shape=[
            jax.ShapeDtypeStruct((ROW, rows, quarter), F32),
            jax.ShapeDtypeStruct((ROW, rows, heads), F32),
            jax.ShapeDtypeStruct((ROW, rows, heads), F32),
        ],
        scratch_shapes=[
            pltpu.VMEM((ROW, rows, quarter), BF16),
            pltpu.VMEM((2 * ROW * rows, quarter), BF16),
            pltpu.VMEM((2 * ROW * rows, quarter), BF16),
            pltpu.SemaphoreType.DMA((5 * ROW,)),
        ],
        compiler_params=limits(20),
        cost_estimate=cost(26 * 4 * rows * rows * quarter, 14 * ROW * rows * quarter, 26 * heads * rows * rows),
        name="attend",
    )(info, streams, theirs, swap, own, cross)


def attend_last_body(
    docs, info_ref, streams, theirs, swap, oldest, acc_ref, m_ref, l_ref, out0, out1, out2, out3, q_s, o_s, sems
):
    place, base = info_ref[2], info_ref[3]
    rows, quarter = q_s.shape[1:]
    copies = []
    for slot in range(ROW):
        part = row_part(info_ref, streams, theirs, swap, slot, 0, quarter)
        copies.append(pltpu.make_async_copy(part, q_s.at[place ^ slot], sems.at[slot]))
        copies[-1].start()
    for copy in copies:
        copy.wait()
    for block in range(ROW):
        slot = place ^ block
        seen = ROW - 1 - block
        width = seen * rows
        if seen:
            position = base + block * rows + lax.broadcasted_iota(jnp.int32, (rows, 1), 0)
            first = contig_start(info_ref, docs, position)
            at = base - (ROW + seen) * rows + lax.broadcasted_iota(jnp.int32, (rows, width), 1)
            allowed = at >= first
        for head in range(quarter // HEAD):
            lanes = slice(head * HEAD, (head + 1) * HEAD)
            total = acc_ref[block, :, lanes]
            below = l_ref[block, :, head : head + 1]
            if seen:
                keys = oldest[block : ROW - 1, 0, :, lanes].reshape(width, HEAD)
                values = oldest[block : ROW - 1, 1, :, lanes].reshape(width, HEAD)
                scores = lax.dot_general(
                    q_s[block, :, lanes],
                    keys,
                    (((1,), (1,)), ((), ())),
                    preferred_element_type=F32,
                )
                scores = jnp.where(allowed, scores, -jnp.inf)
                past = m_ref[block, :, head : head + 1]
                top = jnp.maximum(past, jnp.max(scores, axis=1, keepdims=True))
                fade = jnp.exp2((past - top) * SCALE)
                weight = jnp.exp2((scores - top) * SCALE)
                share = 1.0 / (below * fade + jnp.sum(weight, axis=1, keepdims=True))
                total = total * (fade * share) + share * jnp.dot(
                    weight.astype(BF16), values, preferred_element_type=F32
                )
            else:
                total = total * (1.0 / below)
            o_s[slot, :, lanes] = total.astype(BF16)
    for slot, out in enumerate((out0, out1, out2, out3)):
        out[...] = o_s[slot]


def attend_last(info, docs, streams, theirs, swap, oldest, acc, top, below):
    _, rows, quarter = acc.shape
    heads = quarter // HEAD
    return pl.pallas_call(
        functools.partial(attend_last_body, docs),
        in_specs=[SMEM] + [ANY] * 3 + [VMEM] * 4,
        out_specs=[VMEM] * ROW,
        out_shape=[jax.ShapeDtypeStruct((rows, quarter), BF16)] * ROW,
        scratch_shapes=[
            pltpu.VMEM((ROW, rows, quarter), BF16),
            pltpu.VMEM((ROW, rows, quarter), BF16),
            pltpu.SemaphoreType.DMA((ROW,)),
        ],
        compiler_params=limits(16),
        cost_estimate=cost(6 * 4 * rows * rows * quarter, 12 * ROW * rows * quarter, 6 * heads * rows * rows),
        name="attend_last",
    )(info, streams, theirs, swap, oldest, acc, top, below)


def assemble_body(at_ref, *refs):
    place = at_ref[2]
    *pieces, out_ref = refs
    quarter = pieces[0].shape[1]
    for slot, piece in enumerate(pieces):
        maker = place ^ slot
        which = 2 * (maker & 1) + lax.shift_right_logical(maker, 1)
        out_ref[:, lanes_from(which, quarter)] = piece[...]


def assemble(where, pieces):
    rows, quarter = pieces[0].shape
    return pl.pallas_call(
        assemble_body,
        in_specs=[SMEM] + [VMEM] * ROW,
        out_specs=VMEM,
        out_shape=jax.ShapeDtypeStruct((rows, ROW * quarter), BF16),
        compiler_params=limits(6),
        cost_estimate=cost(0, 16 * rows * quarter),
        name="assemble",
    )(where, *pieces)


def on_device(hyena_qkv, short_weight, filter_rate, filter_residue, attn_qkv, doc_lengths):
    rows, _, channels = attn_qkv.shape
    _, modes = filter_rate.shape
    docs = doc_lengths.shape[0]
    index = lax.axis_index("ctx")
    place = index % ROW
    core, side = place % 2, place // 2
    fixed = jnp.stack([core, side, place, (index - place) * rows]).astype(jnp.int32)
    info = jnp.concatenate([fixed, doc_lengths])

    halo = ahead(hyena_qkv[rows - 2 :], "ctx", 1)

    streams = attn_qkv.transpose(1, 0, 2)
    theirs = flip(halve((1 - core).reshape(1).astype(jnp.int32), streams), "ctx", 1)
    own, cross = pack(fixed, streams, theirs, 1, 2)
    own = ahead(own, "ctx", ROW)
    cross = ahead(cross, "ctx", ROW, 2)
    (swap,) = pack(fixed, streams, theirs, 0, 1)
    swap = flip(swap, "ctx", 2)
    oldest = ahead(onward(fixed, own, cross), "ctx", ROW)

    blocks = channels // LANES
    rate_rows = filter_rate.reshape(blocks, 1, -1)
    res_rows = filter_residue.reshape(blocks, 1, -1)
    near, query, ends = hyena_main(
        hyena_qkv.transpose(1, 0, 2), halo.transpose(1, 0, 2), short_weight, rate_rows, res_rows, modes
    )
    carried = scan_states(ends, filter_rate, rows)
    hyena_out = hyena_finish(near, query, carried, rate_rows, res_rows, modes)

    acc, top, below = attend(info, docs, streams, theirs, swap, own, cross)
    made = attend_last(info, docs, streams, theirs, swap, oldest, acc, top, below)
    pieces = [made[0]] + [flip(made[n], "ctx", n) for n in range(1, ROW)]
    attn_out = assemble(fixed, pieces)
    return (hyena_out, attn_out)


def solution(mesh):
    in_specs = (
        P(("group", "ctx"), None, None),
        P(),
        P(),
        P(),
        P(("group", "ctx"), None, None),
        P("group"),
    )
    out_specs = (P(("group", "ctx"), None), P(("group", "ctx"), None))
    return jax.shard_map(
        on_device, mesh=mesh, in_specs=in_specs, out_specs=out_specs, check_vma=False
    )
```

time: 129 us -> 103 us (0.80)
  the two profiles are of different devices: /device:TPU:0 before, /device:TPU:27 now
where the time goes in v2:
time: 103 us; the launch traced here: 102 us
  waiting for transfers between devices  42.3 us (41%)
  Pallas kernels  28.8 us (28%)
  starting transfers between devices  17.9 us (17%)
  local copies, waits for them, and re-layouts  10.7 us (10%)
  other arithmetic  1.76 us (2%)
    ppermute x6, waiting for transfers between devices, ahead(): return lax.ppermute(value, axis, pairs)  34.5 us
    ppermute x6, starting transfers between devices, ahead(): return lax.ppermute(value, axis, pairs)  9.49 us
    pallas_call x1, Pallas kernels, attend(): pl.pallas_call(functools.partial(attend_body, docs), in_specs=[SMEM] + [A...  8.47 us
    ppermute x8, starting transfers between devices, flip(): return lax.ppermute(value, axis, [(at, at ^ bit) for at in range(count)])  8.36 us
    ppermute x8, waiting for transfers between devices, flip(): return lax.ppermute(value, axis, [(at, at ^ bit) for at in range(count)])  7.81 us
    unnamed x32, local copies, waits for them, and re-layouts  6.24 us
    pallas_call x1, Pallas kernels, attend_last(): pl.pallas_call(functools.partial(attend_last_body, docs), in_specs=[SMEM]...  5.85 us
    pallas_call x1, Pallas kernels, hyena_main(): pl.pallas_call(functools.partial(hyena_main_body, modes), grid=(STEPS,),...  5.46 us
  transfers between devices with their start and end apart: 14, of which 7 were waited for; matrix products, arithmetic and copies ran while one was open for 6% of the time, Pallas kernels for 21%

profile of v2, /device:TPU:27, one launch (start us, length us, event | category | flops | bytes accessed | tf_op | source)
XLA Modules:
  0.0 102.4 jit_solution(13269757904676554652)
XLA Ops:
  0.7 1.4 %copy-done = bf16[128,3,2048]{2,0,1:T(8,128)(2,1)S(1)} copy-done((bf16[128,3,2048]{2,0,1:T(8,128)(2,1)S(1)}, bf16[128,3,2048]{2,0,1:T(8,128)(2,1)}, u32[]{:S(2)}) %copy-start) | copy-done | bytes 1572888
  2.2 0.7 collective-permute-start.6
  2.9 0.9 slice.3
  3.8 3.1 %collective-permute-start = (bf16[2,3,2048]{2,0,1:T(2,128)(2,1)S(1)}, bf16[2,3,2048]{2,0,1:T(2,128)(2,1)S(1)}, u32[]{:S(2)}, u32[]{:S(2)}) collective-permute-start(bf16[2,3,2048]{2,0,1:T(2,128)(2,1)S(1)} %slice.3), channel_id=1, source_target_pairs={{0,1},{1,2},{2,3},{3,4},{4,5},{5,6},{6,7},{7,8},{8,9},{9,10},{10,1... | collective-permute-start | bytes 73736 | tf_op jit(solution)/shard_map/ppermute | solution.py:28
  7.3 1.3 %broadcast_in_dim.3 = f32[16,128,16]{2,1,0:T(8,128)} broadcast(f32[16,128]{1,0:T(8,128)S(1)} %bitcast.22), dimensions={0,1} | broadcast | bytes 139264 | tf_op jit(solution)/shard_map/broadcast_in_dim | solution.py:209
  8.6 2.0 %reshape.18 = f32[16,2048]{1,0:T(8,128)S(1)} reshape(f32[16,128,16]{2,1,0:T(8,128)} %broadcast_in_dim.3) | data formatting | bytes 262144 | tf_op jit(solution)/shard_map/reshape | solution.py:209
  10.7 1.4 %copy-done.6 = bf16[128,3,2048]{2,0,1:T(8,128)(2,1)S(1)} copy-done((bf16[128,3,2048]{2,0,1:T(8,128)(2,1)S(1)}, bf16[128,3,2048]{2,0,1:T(8,128)(2,1)}, u32[]{:S(2)}) %copy-start.6) | copy-done | bytes 1572888
  12.1 5.5 %hyena_main.1 = (f32[128,2048]{1,0:T(8,128)S(1)}, f32[128,2048]{1,0:T(8,128)S(1)}, f32[16,2048]{1,0:T(8,128)S(1)}) custom-call(bf16[3,128,2048]{2,1,0:T(8,128)(2,1)S(1)} %bitcast.20, bf16[3,2,2048]{2,1,0:T(2,128)(2,1)S(1)} %bitcast.21, f32[3,3,2048]{2,1,0:T(4,128)S(1)} %copy-done.7, f32[16,1,128]{2,1,0:T(1,128)S(1)} %bitcast.16, f32[16,1,128]{2,1,0:T(1,128)S(1)} %bitcast.18), custom_call_target="tpu_custom_call" | custom-call | flops 536870912 | bytes 2097152 | tf_op jit(solution)/shard_map/hyena_main/pallas_call | solution.py:121
  17.5 1.0 copy-done.2
  18.5 1.0 copy-done.4
  19.6 1.6 %pack.3 = (bf16[2,2,128,512]{3,2,1,0:T(8,128)(2,1)}, bf16[2,2,128,512]{3,2,1,0:T(8,128)(2,1)}) custom-call(s32[4]{0:T(128)S(1)} %pad_add_fusion.at_ref, bf16[3,128,2048]{2,1,0:T(8,128)(2,1)S(1)} %bitcast.12, bf16[3,128,1024]{2,1,0:T(8,128)(2,1)S(1)} %collective-permute-done.6.theirs_ref.theirs), custom_call_target="tpu_custom_call" | custom-call | bytes 2097152 | tf_op jit(solution)/shard_map/pack/pallas_call | solution.py:277
  21.2 1.3 %collective-permute-start.8 = (bf16[2,2,128,512]{3,2,1,0:T(8,128)(2,1)}, bf16[2,2,128,512]{3,2,1,0:T(8,128)(2,1)}, u32[]{:S(2)}, u32[]{:S(2)}) collective-permute-start(bf16[2,2,128,512]{3,2,1,0:T(8,128)(2,1)} %get-tuple-element.17), channel_id=1, source_target_pairs={{0,4},{1,5},{2,6},{3,7},{4,8},{5,9},{6,10},{7,11},{8,12},{9,13},{1... | collective-permute-start | bytes 1572872 | tf_op jit(solution)/shard_map/ppermute | solution.py:28
  22.4 1.3 %collective-permute-start.9 = (bf16[2,2,128,512]{3,2,1,0:T(8,128)(2,1)}, bf16[2,2,128,512]{3,2,1,0:T(8,128)(2,1)}, u32[]{:S(2)}, u32[]{:S(2)}) collective-permute-start(bf16[2,2,128,512]{3,2,1,0:T(8,128)(2,1)} %get-tuple-element.18), channel_id=1, source_target_pairs={{0,6},{1,7},{2,4},{3,5},{4,10},{5,11},{6,8},{7,9},{8,14},{9,15},{1... | collective-permute-start | bytes 1572872 | tf_op jit(solution)/shard_map/ppermute | solution.py:28
  25.1 2.9 %collective-permute-done.2 = f32[16,1024]{1,0:T(8,128)S(1)} collective-permute-done((f32[16,1024]{1,0:T(8,128)S(1)}, f32[16,1024]{1,0:T(8,128)S(1)}, u32[]{:S(2)}, u32[]{:S(2)}) %collective-permute-start.2) | collective-permute-done | bytes 65568 | tf_op jit(solution)/shard_map/ppermute | solution.py:22
  28.7 1.3 %collective-permute-start.3 = (f32[16,1024]{1,0:T(8,128)S(1)}, f32[16,1024]{1,0:T(8,128)S(1)}, u32[]{:S(2)}, u32[]{:S(2)}) collective-permute-start(f32[16,1024]{1,0:T(8,128)S(1)} %select_add_fusion), channel_id=1, source_target_pairs={{0,4},{1,5},{2,6},{3,7},{4,8},{5,9},{6,10},{7,11},{8,12},{9,13},{1... | collective-permute-start | bytes 196616 | tf_op jit(solution)/shard_map/ppermute | solution.py:28
  30.0 1.5 %pack.2 = bf16[2,3,128,512]{3,2,1,0:T(8,128)(2,1)} custom-call(s32[4]{0:T(128)S(1)} %pad_add_fusion.at_ref, bf16[3,128,2048]{2,1,0:T(8,128)(2,1)S(1)} %bitcast.13, bf16[3,128,1024]{2,1,0:T(8,128)(2,1)S(1)} %collective-permute-done.6.theirs_ref.theirs), custom_call_target="tpu_custom_call" | custom-call | bytes 1048576 | tf_op jit(solution)/shard_map/pack/pallas_call | solution.py:277
  31.4 0.8 collective-permute-start.7
  32.3 4.1 %collective-permute-done.8.own_ref.own = bf16[2,2,128,512]{3,2,1,0:T(8,128)(2,1)} collective-permute-done((bf16[2,2,128,512]{3,2,1,0:T(8,128)(2,1)}, bf16[2,2,128,512]{3,2,1,0:T(8,128)(2,1)}, u32[]{:S(2)}, u32[]{:S(2)}) %collective-permute-start.8) | collective-permute-done | bytes 524320 | tf_op jit(solution)/shard_map/ppermute | solution.py:28
  36.3 12.1 %collective-permute-done.9.cross_ref.cross = bf16[2,2,128,512]{3,2,1,0:T(8,128)(2,1)} collective-permute-done((bf16[2,2,128,512]{3,2,1,0:T(8,128)(2,1)}, bf16[2,2,128,512]{3,2,1,0:T(8,128)(2,1)}, u32[]{:S(2)}, u32[]{:S(2)}) %collective-permute-start.9) | collective-permute-done | bytes 524320 | tf_op jit(solution)/shard_map/ppermute | solution.py:28
  48.4 2.2 %onward.1 = bf16[3,2,128,512]{3,2,1,0:T(8,128)(2,1)} custom-call(s32[4]{0:T(128)S(1)} %pad_add_fusion.at_ref, bf16[2,2,128,512]{3,2,1,0:T(8,128)(2,1)} %collective-permute-done.8.own_ref.own, bf16[2,2,128,512]{3,2,1,0:T(8,128)(2,1)} %collective-permute-done.9.cross_ref.cross), custom_call_target="tpu_custom_call" | custom-call | bytes 1048576 | tf_op jit(solution)/shard_map/onward/pallas_call | solution.py:303
  50.6 1.3 %collective-permute-start.10 = (bf16[3,2,128,512]{3,2,1,0:T(8,128)(2,1)}, bf16[3,2,128,512]{3,2,1,0:T(8,128)(2,1)}, u32[]{:S(2)}, u32[]{:S(2)}) collective-permute-start(bf16[3,2,128,512]{3,2,1,0:T(8,128)(2,1)} %onward.1), channel_id=1, source_target_pairs={{0,4},{1,5},{2,6},{3,7},{4,8},{5,9},{6,10},{7,11},{8,12},{9,13},{1... | collective-permute-start | bytes 2359304 | tf_op jit(solution)/shard_map/ppermute | solution.py:28
  51.9 1.3 %collective-permute-start.4 = (f32[16,1024]{1,0:T(8,128)S(1)}, f32[16,1024]{1,0:T(8,128)S(1)}, u32[]{:S(2)}, u32[]{:S(2)}) collective-permute-start(f32[16,1024]{1,0:T(8,128)S(1)} %multiply_add_fusion.1), channel_id=1, source_target_pairs={{0,8},{1,9},{2,10},{3,11},{4,12},{5,13},{6,14},{7,15},{16,24},{17,... | collective-permute-start | bytes 196616 | tf_op jit(solution)/shard_map/ppermute | solution.py:28
  53.2 18.3 %collective-permute-done.4 = f32[16,1024]{1,0:T(8,128)S(1)} collective-permute-done((f32[16,1024]{1,0:T(8,128)S(1)}, f32[16,1024]{1,0:T(8,128)S(1)}, u32[]{:S(2)}, u32[]{:S(2)}) %collective-permute-start.4) | collective-permute-done | bytes 65568 | tf_op jit(solution)/shard_map/ppermute | solution.py:28
  72.3 3.9 %collective-permute-start.5 = (f32[16,1024]{1,0:T(8,128)}, f32[16,1024]{1,0:T(8,128)S(1)}, u32[]{:S(2)}, u32[]{:S(2)}) collective-permute-start(f32[16,1024]{1,0:T(8,128)} %get-tuple-element.26), channel_id=1, source_target_pairs={{0,1},{1,0},{2,3},{3,2},{4,5},{5,4},{6,7},{7,6},{8,9},{9,8},{10,11... | collective-permute-start | bytes 196616 | tf_op jit(solution)/shard_map/ppermute | solution.py:22
  76.3 1.0 %collective-permute-done.5 = f32[16,1024]{1,0:T(8,128)S(1)} collective-permute-done((f32[16,1024]{1,0:T(8,128)}, f32[16,1024]{1,0:T(8,128)S(1)}, u32[]{:S(2)}, u32[]{:S(2)}) %collective-permute-start.5) | collective-permute-done | bytes 65568 | tf_op jit(solution)/shard_map/ppermute | solution.py:22
  77.3 0.9 broadcast_select_fusion.2
  78.2 8.5 %attend.1 = (f32[4,128,512]{2,1,0:T(8,128)S(1)}, f32[4,128,4]{2,1,0:T(8,128)S(1)}, f32[4,128,4]{2,1,0:T(8,128)S(1)}) custom-call(s32[8]{0:T(128)S(1)} %concatenate.8.info_ref, bf16[3,128,2048]{2,1,0:T(8,128)(2,1)S(1)} %bitcast.14, bf16[3,128,1024]{2,1,0:T(8,128)(2,1)S(1)} %collective-permute-done.6.theirs_ref.theirs, ...), custom_call_target="tpu_custom_call" | custom-call | flops 872415232 | bytes 3670016 | tf_op jit(solution)/shard_map/attend/pallas_call | solution.py:388
  86.7 5.8 %attend_last.1 = (bf16[128,512]{1,0:T(8,128)(2,1)S(1)}, bf16[128,512]{1,0:T(8,128)(2,1)S(1)}, bf16[128,512]{1,0:T(8,128)(2,1)S(1)}, bf16[128,512]{1,0:T(8,128)(2,1)S(1)}) custom-call(s32[8]{0:T(128)S(1)} %concatenate.8.info_ref, bf16[3,128,2048]{2,1,0:T(8,128)(2,1)S(1)} %bitcast.15, bf16[3,128,1024]{2,1,0:T(8,128)(2,1)S(1)} %collective-permute-done.6.theirs_ref.theirs, ...), custom_call_target="tpu_custom_call" | custom-call | flops 201326592 | bytes 3145728 | tf_op jit(solution)/shard_map/attend_last/pallas_call | solution.py:462
  93.2 1.6 %collective-permute-start.13 = (bf16[128,512]{1,0:T(8,128)(2,1)S(1)}, bf16[128,512]{1,0:T(8,128)(2,1)S(1)}, u32[]{:S(2)}, u32[]{:S(2)}) collective-permute-start(bf16[128,512]{1,0:T(8,128)(2,1)S(1)} %get-tuple-element.25), channel_id=1, source_target_pairs={{0,3},{1,2},{2,1},{3,0},{4,7},{5,6},{6,5},{7,4},{8,11},{9,10},{10,... | collective-permute-start | bytes 393224 | tf_op jit(solution)/shard_map/ppermute | solution.py:22
  94.8 2.3 %hyena_finish.1 = bf16[128,2048]{1,0:T(8,128)(2,1)} custom-call(f32[128,2048]{1,0:T(8,128)S(1)} %copy-done.3, f32[128,2048]{1,0:T(8,128)S(1)} %copy-done.5, f32[16,2048]{1,0:T(8,128)S(1)} %pad_maximum_fusion.carried_ref, f32[16,1,128]{2,1,0:T(1,128)S(1)} %bitcast.17, f32[16,1,128]{2,1,0:T(1,128)S(1)} %bitcast.19), custom_call_target="tpu_custom_call" | custom-call | flops 201326592 | bytes 2621440 | tf_op jit(solution)/shard_map/hyena_finish/pallas_call | solution.py:184
  97.9 3.1 %collective-permute-done.13.refs_3_ = bf16[128,512]{1,0:T(8,128)(2,1)S(1)} collective-permute-done((bf16[128,512]{1,0:T(8,128)(2,1)S(1)}, bf16[128,512]{1,0:T(8,128)(2,1)S(1)}, u32[]{:S(2)}, u32[]{:S(2)}) %collective-permute-start.13) | collective-permute-done | bytes 131104 | tf_op jit(solution)/shard_map/ppermute | solution.py:22
  101.0 1.4 %assemble.1 = bf16[128,2048]{1,0:T(8,128)(2,1)} custom-call(s32[4]{0:T(128)S(1)} %pad_add_fusion.at_ref, bf16[128,512]{1,0:T(8,128)(2,1)S(1)} %get-tuple-element.22.refs_0_, bf16[128,512]{1,0:T(8,128)(2,1)S(1)} %collective-permute-done.11.refs_1_, bf16[128,512]{1,0:T(8,128)(2,1)S(1)} %collective-permute-done.12.refs_2_, ...), custom_call_target="tpu_custom_call" | custom-call | bytes 1048576 | tf_op jit(solution)/shard_map/assemble/pallas_call | solution.py:490
  (51 shorter events, 4.8 us)
Async XLA Ops:
  0.6 6.3 %copy-start.12 = (f32[128,16]{0,1:T(8,128)S(1)}, f32[128,16]{0,1:T(8,128)}, u32[]{:S(2)}) copy-start(f32[128,16]{0,1:T(8,128)} %param.8) | copy-start | bytes 24580
  0.6 6.5 %copy-start.13 = (f32[128,16]{0,1:T(8,128)S(1)}, f32[128,16]{0,1:T(8,128)}, u32[]{:S(2)}) copy-start(f32[128,16]{0,1:T(8,128)} %param.9) | copy-start | bytes 24580
  0.7 1.4 %copy-start = (bf16[128,3,2048]{2,0,1:T(8,128)(2,1)S(1)}, bf16[128,3,2048]{2,0,1:T(8,128)(2,1)}, u32[]{:S(2)}) copy-start(bf16[128,3,2048]{2,0,1:T(8,128)(2,1)} %param.10) | copy-start | bytes 4718596
  2.1 8.5 %copy-start.7 = (f32[3,3,2048]{2,1,0:T(4,128)S(1)}, f32[3,3,2048]{2,1,0:T(4,128)}, u32[]{:S(2)}) copy-start(f32[3,3,2048]{2,1,0:T(4,128)} %w_ref.1) | copy-start | bytes 221188
  2.2 17.4 %collective-permute-start.6 = (bf16[3,128,1024]{2,1,0:T(8,128)(2,1)S(1)}, bf16[3,128,1024]{2,1,0:T(8,128)(2,1)S(1)}, u32[]{:S(2)}, u32[]{:S(2)}) collective-permute-start(bf16[3,128,1024]{2,1,0:T(8,128)(2,1)S(1)} %halve.1), channel_id=1, source_target_pairs={{0,1},{1,0},{2,3},{3,2},{4,5},{5,4},{6,7},{7,6},{8,9},{9,8},{10,11... | collective-permute-start | bytes 2359304 | tf_op jit(solution)/shard_map/ppermute | solution.py:22
  3.8 6.8 %collective-permute-start = (bf16[2,3,2048]{2,0,1:T(2,128)(2,1)S(1)}, bf16[2,3,2048]{2,0,1:T(2,128)(2,1)S(1)}, u32[]{:S(2)}, u32[]{:S(2)}) collective-permute-start(bf16[2,3,2048]{2,0,1:T(2,128)(2,1)S(1)} %slice.3), channel_id=1, source_target_pairs={{0,1},{1,2},{2,3},{3,4},{4,5},{5,6},{6,7},{7,8},{8,9},{9,10},{10,1... | collective-permute-start | bytes 73736 | tf_op jit(solution)/shard_map/ppermute | solution.py:28
  8.6 10.9 %copy-start.1 = (bf16[128,3,2048]{2,0,1:T(8,128)(2,1)S(1)}, bf16[128,3,2048]{2,0,1:T(8,128)(2,1)}, u32[]{:S(2)}) copy-start(bf16[128,3,2048]{2,0,1:T(8,128)(2,1)} %param.10) | copy-start | bytes 4718596
  10.6 1.4 %copy-start.6 = (bf16[128,3,2048]{2,0,1:T(8,128)(2,1)S(1)}, bf16[128,3,2048]{2,0,1:T(8,128)(2,1)}, u32[]{:S(2)}) copy-start(bf16[128,3,2048]{2,0,1:T(8,128)(2,1)} %param.6) | copy-start | bytes 4718596
  17.5 1.0 copy-start.2
  18.5 1.0 copy-start.4
  19.5 4.3 %collective-permute-start.1 = (f32[16,1024]{1,0:T(8,128)S(1)}, f32[16,1024]{1,0:T(8,128)S(1)}, u32[]{:S(2)}, u32[]{:S(2)}) collective-permute-start(f32[16,1024]{1,0:T(8,128)S(1)} %constant_dynamic-slice_fusion), channel_id=1, source_target_pairs={{0,1},{1,0},{2,3},{3,2},{4,5},{5,4},{6,7},{7,6},{8,9},{9,8},{10,11... | collective-permute-start | bytes 196616 | tf_op jit(solution)/shard_map/ppermute | solution.py:22
  21.2 15.2 %collective-permute-start.8 = (bf16[2,2,128,512]{3,2,1,0:T(8,128)(2,1)}, bf16[2,2,128,512]{3,2,1,0:T(8,128)(2,1)}, u32[]{:S(2)}, u32[]{:S(2)}) collective-permute-start(bf16[2,2,128,512]{3,2,1,0:T(8,128)(2,1)} %get-tuple-element.17), channel_id=1, source_target_pairs={{0,4},{1,5},{2,6},{3,7},{4,8},{5,9},{6,10},{7,11},{8,12},{9,13},{1... | collective-permute-start | bytes 1572872 | tf_op jit(solution)/shard_map/ppermute | solution.py:28
  22.4 26.0 %collective-permute-start.9 = (bf16[2,2,128,512]{3,2,1,0:T(8,128)(2,1)}, bf16[2,2,128,512]{3,2,1,0:T(8,128)(2,1)}, u32[]{:S(2)}, u32[]{:S(2)}) collective-permute-start(bf16[2,2,128,512]{3,2,1,0:T(8,128)(2,1)} %get-tuple-element.18), channel_id=1, source_target_pairs={{0,6},{1,7},{2,4},{3,5},{4,10},{5,11},{6,8},{7,9},{8,14},{9,15},{1... | collective-permute-start | bytes 1572872 | tf_op jit(solution)/shard_map/ppermute | solution.py:28
  23.8 0.6 copy-start.8
  24.4 3.6 %collective-permute-start.2 = (f32[16,1024]{1,0:T(8,128)S(1)}, f32[16,1024]{1,0:T(8,128)S(1)}, u32[]{:S(2)}, u32[]{:S(2)}) collective-permute-start(f32[16,1024]{1,0:T(8,128)S(1)} %select_add_fusion.1), channel_id=1, source_target_pairs={{0,2},{1,3},{2,0},{3,1},{4,6},{5,7},{6,4},{7,5},{8,10},{9,11},{10,... | collective-permute-start | bytes 196616 | tf_op jit(solution)/shard_map/ppermute | solution.py:22
  28.0 0.6 copy-start.10
  28.7 23.2 %collective-permute-start.3 = (f32[16,1024]{1,0:T(8,128)S(1)}, f32[16,1024]{1,0:T(8,128)S(1)}, u32[]{:S(2)}, u32[]{:S(2)}) collective-permute-start(f32[16,1024]{1,0:T(8,128)S(1)} %select_add_fusion), channel_id=1, source_target_pairs={{0,4},{1,5},{2,6},{3,7},{4,8},{5,9},{6,10},{7,11},{8,12},{9,13},{1... | collective-permute-start | bytes 196616 | tf_op jit(solution)/shard_map/ppermute | solution.py:28
  31.4 40.1 %copy-start.9 = (f32[16,1024]{1,0:T(8,128)S(1)}, f32[16,1024]{1,0:T(8,128)}, u32[]{:S(2)}) copy-start(f32[16,1024]{1,0:T(8,128)} %copy-done.8) | copy-start | bytes 196612
  31.4 40.1 %copy-start.11 = (f32[16,1024]{1,0:T(8,128)S(1)}, f32[16,1024]{1,0:T(8,128)}, u32[]{:S(2)}) copy-start(f32[16,1024]{1,0:T(8,128)} %copy-done.10) | copy-start | bytes 196612
  31.4 44.8 %copy-start.14 = (s32[4]{0:T(128)S(1)}, s32[4]{0:T(128)}, u32[]{:S(2)}) copy-start(s32[4]{0:T(128)} %param.11) | copy-start | bytes 52
  31.4 46.8 %collective-permute-start.7 = (bf16[2,3,128,512]{3,2,1,0:T(8,128)(2,1)}, bf16[2,3,128,512]{3,2,1,0:T(8,128)(2,1)S(1)}, u32[]{:S(2)}, u32[]{:S(2)}) collective-permute-start(bf16[2,3,128,512]{3,2,1,0:T(8,128)(2,1)} %pack.2), channel_id=1, source_target_pairs={{0,2},{1,3},{2,0},{3,1},{4,6},{5,7},{6,4},{7,5},{8,10},{9,11},{10,... | collective-permute-start | bytes 2359304 | tf_op jit(solution)/shard_map/ppermute | solution.py:22
  50.6 36.1 %collective-permute-start.10 = (bf16[3,2,128,512]{3,2,1,0:T(8,128)(2,1)}, bf16[3,2,128,512]{3,2,1,0:T(8,128)(2,1)}, u32[]{:S(2)}, u32[]{:S(2)}) collective-permute-start(bf16[3,2,128,512]{3,2,1,0:T(8,128)(2,1)} %onward.1), channel_id=1, source_target_pairs={{0,4},{1,5},{2,6},{3,7},{4,8},{5,9},{6,10},{7,11},{8,12},{9,13},{1... | collective-permute-start | bytes 2359304 | tf_op jit(solution)/shard_map/ppermute | solution.py:28
  51.9 19.6 %collective-permute-start.4 = (f32[16,1024]{1,0:T(8,128)S(1)}, f32[16,1024]{1,0:T(8,128)S(1)}, u32[]{:S(2)}, u32[]{:S(2)}) collective-permute-start(f32[16,1024]{1,0:T(8,128)S(1)} %multiply_add_fusion.1), channel_id=1, source_target_pairs={{0,8},{1,9},{2,10},{3,11},{4,12},{5,13},{6,14},{7,15},{16,24},{17,... | collective-permute-start | bytes 196616 | tf_op jit(solution)/shard_map/ppermute | solution.py:28
  72.3 5.0 %collective-permute-start.5 = (f32[16,1024]{1,0:T(8,128)}, f32[16,1024]{1,0:T(8,128)S(1)}, u32[]{:S(2)}, u32[]{:S(2)}) collective-permute-start(f32[16,1024]{1,0:T(8,128)} %get-tuple-element.26), channel_id=1, source_target_pairs={{0,1},{1,0},{2,3},{3,2},{4,5},{5,4},{6,7},{7,6},{8,9},{9,8},{10,11... | collective-permute-start | bytes 196616 | tf_op jit(solution)/shard_map/ppermute | solution.py:22
  86.7 8.1 %copy-start.3 = (f32[128,2048]{1,0:T(8,128)S(1)}, f32[128,2048]{1,0:T(8,128)}, u32[]{:S(2)}) copy-start(f32[128,2048]{1,0:T(8,128)} %copy-done.2) | copy-start | bytes 3145732
  86.7 8.1 %copy-start.5 = (f32[128,2048]{1,0:T(8,128)S(1)}, f32[128,2048]{1,0:T(8,128)}, u32[]{:S(2)}) copy-start(f32[128,2048]{1,0:T(8,128)} %copy-done.4) | copy-start | bytes 3145732
  92.6 4.6 %collective-permute-start.11 = (bf16[128,512]{1,0:T(8,128)(2,1)S(1)}, bf16[128,512]{1,0:T(8,128)(2,1)S(1)}, u32[]{:S(2)}, u32[]{:S(2)}) collective-permute-start(bf16[128,512]{1,0:T(8,128)(2,1)S(1)} %get-tuple-element.23), channel_id=1, source_target_pairs={{0,1},{1,0},{2,3},{3,2},{4,5},{5,4},{6,7},{7,6},{8,9},{9,8},{10,11... | collective-permute-start | bytes 393224 | tf_op jit(solution)/shard_map/ppermute | solution.py:22
  93.0 4.9 %collective-permute-start.12 = (bf16[128,512]{1,0:T(8,128)(2,1)S(1)}, bf16[128,512]{1,0:T(8,128)(2,1)S(1)}, u32[]{:S(2)}, u32[]{:S(2)}) collective-permute-start(bf16[128,512]{1,0:T(8,128)(2,1)S(1)} %get-tuple-element.24), channel_id=1, source_target_pairs={{0,2},{1,3},{2,0},{3,1},{4,6},{5,7},{6,4},{7,5},{8,10},{9,11},{10,... | collective-permute-start | bytes 393224 | tf_op jit(solution)/shard_map/ppermute | solution.py:22
  93.2 7.8 %collective-permute-start.13 = (bf16[128,512]{1,0:T(8,128)(2,1)S(1)}, bf16[128,512]{1,0:T(8,128)(2,1)S(1)}, u32[]{:S(2)}, u32[]{:S(2)}) collective-permute-start(bf16[128,512]{1,0:T(8,128)(2,1)S(1)} %get-tuple-element.25), channel_id=1, source_target_pairs={{0,3},{1,2},{2,1},{3,0},{4,7},{5,6},{6,5},{7,4},{8,11},{9,10},{10,... | collective-permute-start | bytes 393224 | tf_op jit(solution)/shard_map/ppermute | solution.py:22

commit v3 on v2

--- a/solution.py
+++ b/solution.py
@@ -11,6 +11,7 @@
 
 HEAD = 128
 LANES = 128
+EDGE = 8
 ROW = 4
 
 F32 = jnp.float32
@@ -56,7 +57,80 @@
     return kept
 
 
-def hyena_main_body(modes, x_ref, halo_ref, w_ref, rate_ref, res_ref, near_ref, q_ref, ends_ref, taps_s, u_s):
+def feature(x, halo, w_ref, stream, at):
+    here = x.astype(F32)
+    halo = halo.astype(F32)
+    edge = halo.shape[0]
+    row_at = lax.broadcasted_iota(jnp.int32, here.shape, 0)
+    one = jnp.where(row_at == 0, halo[edge - 1 :], pltpu.roll(here, 1, 0))
+    two = jnp.where(row_at == 1, halo[edge - 1 :], pltpu.roll(here, 2, 0))
+    two = jnp.where(row_at == 0, halo[edge - 2 : edge - 1], two)
+    tap = [w_ref[n, stream : stream + 1, at] for n in range(3)]
+    return tap[0] * here + tap[1] * one + tap[2] * two
+
+
+def hyena_ends_body(modes, x_ref, halo_ref, w_ref, rate_ref, mixed_ref, ends_ref, wide_ref):
+    rows = x_ref.shape[1]
+    parts, _, terms = rate_ref.shape
+    lanes = x_ref.shape[2] // parts
+    filters = terms // modes
+    width = lanes // filters
+    lag = (rows - 1 - lax.broadcasted_iota(jnp.int32, (terms, rows), 1)).astype(F32)
+    own = same_filter(modes, width, terms, lanes)
+    pick = lambda matrix: jnp.sum(jnp.where(own, matrix, 0.0).reshape(filters, modes, lanes), axis=0)
+    for part in range(parts):
+        at = slice(part * lanes, (part + 1) * lanes)
+        key, value = (feature(x_ref[n, :, at], halo_ref[n, :, at], w_ref, n, at) for n in (1, 2))
+        mixed = (key * value).astype(BF16)
+        mixed_ref[:, at] = mixed
+        rate = jnp.broadcast_to(rate_ref[part], (rows, terms)).T
+        powers = jnp.exp(-rate * lag)
+        high = powers.astype(BF16)
+        low = (powers - high.astype(F32)).astype(BF16)
+        ends = jnp.dot(high, mixed, preferred_element_type=F32) + jnp.dot(
+            low, mixed, preferred_element_type=F32
+        )
+        ends_ref[:, at] = pick(ends)
+        wide_ref[:, at] = pick(rate)
+
+
+STEPS = 4
+
+
+def hyena_ends(streams, halo, short_weight, rate_rows, modes):
+    _, rows, channels = streams.shape
+    edge = halo.shape[1]
+    blocks, _, terms = rate_rows.shape
+    parts = blocks // STEPS
+    wide = channels // STEPS
+    by_block = lambda n: (0, n)
+    lead = lambda n: (0, 0, n)
+    return pl.pallas_call(
+        functools.partial(hyena_ends_body, modes),
+        grid=(STEPS,),
+        in_specs=[
+            pl.BlockSpec((3, rows, wide), lead),
+            pl.BlockSpec((3, edge, wide), lead),
+            pl.BlockSpec((3, 3, wide), lead),
+            pl.BlockSpec((parts, 1, terms), lambda n: (n, 0, 0)),
+        ],
+        out_specs=[
+            pl.BlockSpec((rows, wide), by_block),
+            pl.BlockSpec((modes, wide), by_block),
+            pl.BlockSpec((modes, wide), by_block),
+        ],
+        out_shape=[
+            jax.ShapeDtypeStruct((rows, channels), BF16),
+            jax.ShapeDtypeStruct((modes, channels), F32),
+            jax.ShapeDtypeStruct((modes, channels), F32),
+        ],
+        compiler_params=limits(16),
+        cost_estimate=cost(4 * rows * terms * channels, 8 * rows * channels),
+        name="hyena_ends",
+    )(streams, halo, short_weight, rate_rows)
+
+
+def hyena_near_body(modes, x_ref, halo_ref, w_ref, mixed_ref, rate_ref, res_ref, near_ref, q_ref, taps_s, u_s):
     rows = x_ref.shape[1]
     parts, _, terms = rate_ref.shape
     lanes = x_ref.shape[2] // parts
@@ -65,29 +139,16 @@
     row_at = lax.broadcasted_iota(jnp.int32, (rows, lanes), 0)
     lane_at = lax.broadcasted_iota(jnp.int32, (rows, lanes), 1)
     lag = (rows - 1 - lax.broadcasted_iota(jnp.int32, (terms, rows), 1)).astype(F32)
-    own = same_filter(modes, width, terms, lanes)
     zero = jnp.zeros((rows, lanes), BF16)
-
     for part in range(parts):
         at = slice(part * lanes, (part + 1) * lanes)
-
-        def feature(stream):
-            here = x_ref[stream, :, at].astype(F32)
-            halo = halo_ref[stream, :, at].astype(F32)
-            one = jnp.where(row_at == 0, halo[1:2], pltpu.roll(here, 1, 0))
-            two = pltpu.roll(here, 2, 0)
-            two = jnp.where(row_at == 0, halo[0:1], jnp.where(row_at == 1, halo[1:2], two))
-            tap = [w_ref[n, stream : stream + 1, at] for n in range(3)]
-            return tap[0] * here + tap[1] * one + tap[2] * two
-
-        q_ref[:, at] = feature(0)
-        mixed = (feature(1) * feature(2)).astype(BF16)
-
+        q_ref[:, at] = feature(x_ref[0, :, at], halo_ref[0, :, at], w_ref, 0, at)
+        mixed = mixed_ref[:, at]
         coeff = res_ref[part] * jnp.sqrt(2.0 * rate_ref[part] / modes)
         rate = jnp.broadcast_to(rate_ref[part], (rows, terms)).T
         coeff = jnp.broadcast_to(coeff, (rows, terms)).T
-        powers = jnp.exp(-rate * lag)
-        backward = jnp.sum((coeff * powers).reshape(filters, modes, rows), axis=1)
+        powers = coeff * jnp.exp(-rate * lag)
+        backward = jnp.sum(powers.reshape(filters, modes, rows), axis=1)
         for g in range(filters):
             spread = jnp.broadcast_to(backward[g : g + 1], (rows, rows))
             shifted = pltpu.roll(spread, 1, 1, stride=1, stride_axis=0)
@@ -97,19 +158,10 @@
             u_s[part, g * rows : (g + 1) * rows, :] = jnp.where(mine, mixed, zero)
         near_ref[:, at] = jnp.dot(taps_s[part], u_s[part], preferred_element_type=F32)
 
-        high = powers.astype(BF16)
-        low = (powers - high.astype(F32)).astype(BF16)
-        ends = jnp.dot(high, mixed, preferred_element_type=F32) + jnp.dot(
-            low, mixed, preferred_element_type=F32
-        )
-        ends_ref[:, at] = jnp.sum(jnp.where(own, ends, 0.0).reshape(filters, modes, lanes), axis=0)
-
-
-STEPS = 4
-
-
-def hyena_main(streams, halo, short_weight, rate_rows, res_rows, modes):
+
+def hyena_near(streams, halo, short_weight, mixed, rate_rows, res_rows, modes):
     _, rows, channels = streams.shape
+    edge = halo.shape[1]
     blocks, _, terms = rate_rows.shape
     parts = blocks // STEPS
     wide = channels // STEPS
@@ -119,33 +171,32 @@
     lead = lambda n: (0, 0, n)
     whole = lambda n: (n, 0, 0)
     return pl.pallas_call(
-        functools.partial(hyena_main_body, modes),
+        functools.partial(hyena_near_body, modes),
         grid=(STEPS,),
         in_specs=[
-            pl.BlockSpec((3, rows, wide), lead),
-            pl.BlockSpec((3, 2, wide), lead),
+            pl.BlockSpec((1, rows, wide), lead),
+            pl.BlockSpec((1, edge, wide), lead),
             pl.BlockSpec((3, 3, wide), lead),
+            pl.BlockSpec((rows, wide), by_block),
             pl.BlockSpec((parts, 1, terms), whole),
             pl.BlockSpec((parts, 1, terms), whole),
         ],
         out_specs=[
             pl.BlockSpec((rows, wide), by_block),
             pl.BlockSpec((rows, wide), by_block),
-            pl.BlockSpec((modes, wide), by_block),
         ],
         out_shape=[
             jax.ShapeDtypeStruct((rows, channels), F32),
             jax.ShapeDtypeStruct((rows, channels), F32),
-            jax.ShapeDtypeStruct((modes, channels), F32),
         ],
         scratch_shapes=[
             pltpu.VMEM((parts, rows, filters * rows), BF16),
             pltpu.VMEM((parts, filters * rows, lanes), BF16),
         ],
-        compiler_params=limits(24),
-        cost_estimate=cost(2 * rows * rows * filters * channels, 8 * rows * channels),
-        name="hyena_main",
-    )(streams, halo, short_weight, rate_rows, res_rows)
+        compiler_params=limits(16),
+        cost_estimate=cost(2 * rows * rows * filters * channels, 12 * rows * channels),
+        name="hyena_near",
+    )(streams, halo, short_weight, mixed, rate_rows, res_rows)
 
 
 def hyena_out_body(modes, near_ref, q_ref, carried_ref, rate_ref, res_ref, out_ref):
@@ -199,14 +250,11 @@
     )(near, query, carried, rate_rows, res_rows)
 
 
-def scan_states(ends, filter_rate, rows):
-    _, channels = ends.shape
-    half = channels // 2
-    width = channels // filter_rate.shape[0]
+def scan_states(ends, rate, rows):
+    half = ends.shape[1] // 2
     index = lax.axis_index("ctx")
     count = lax.axis_size("ctx") // ROW
     core, side = index % 2, index // 2 % 2
-    rate = jnp.repeat(filter_rate.T, width, axis=1)
     take = lambda matrix, which: lax.dynamic_slice_in_dim(matrix, which * half, half, 1)
     rate = take(rate, core)
     decay = lambda blocks: jnp.exp(-rate * float(rows * blocks))
@@ -500,7 +548,7 @@
 
 def on_device(hyena_qkv, short_weight, filter_rate, filter_residue, attn_qkv, doc_lengths):
     rows, _, channels = attn_qkv.shape
-    _, modes = filter_rate.shape
+    modes = filter_rate.shape[1]
     docs = doc_lengths.shape[0]
     index = lax.axis_index("ctx")
     place = index % ROW
@@ -508,7 +556,7 @@
     fixed = jnp.stack([core, side, place, (index - place) * rows]).astype(jnp.int32)
     info = jnp.concatenate([fixed, doc_lengths])
 
-    halo = ahead(hyena_qkv[rows - 2 :], "ctx", 1)
+    edge = ahead(hyena_qkv[rows - EDGE :], "ctx", 1)
 
     streams = attn_qkv.transpose(1, 0, 2)
     theirs = flip(halve((1 - core).reshape(1).astype(jnp.int32), streams), "ctx", 1)
@@ -522,10 +570,10 @@
     blocks = channels // LANES
     rate_rows = filter_rate.reshape(blocks, 1, -1)
     res_rows = filter_residue.reshape(blocks, 1, -1)
-    near, query, ends = hyena_main(
-        hyena_qkv.transpose(1, 0, 2), halo.transpose(1, 0, 2), short_weight, rate_rows, res_rows, modes
-    )
-    carried = scan_states(ends, filter_rate, rows)
+    inner, edge = hyena_qkv.transpose(1, 0, 2), edge.transpose(1, 0, 2)
+    mixed, ends, wide = hyena_ends(inner, edge, short_weight, rate_rows, modes)
+    near, query = hyena_near(inner, edge, short_weight, mixed, rate_rows, res_rows, modes)
+    carried = scan_states(ends, wide, rows)
     hyena_out = hyena_finish(near, query, carried, rate_rows, res_rows, modes)
 
     acc, top, below = attend(info, docs, streams, theirs, swap, own, cross)

time: 103 us -> 107 us (1.039)
  the two profiles are of different devices: /device:TPU:27 before, /device:TPU:15 now
where the time goes in v3:
time: 107 us; the launch traced here: 105 us
  waiting for transfers between devices  36.5 us (34%)
  Pallas kernels  29.4 us (27%)
  starting transfers between devices  25.6 us (24%)
  local copies, waits for them, and re-layouts  10.8 us (10%)
  other arithmetic  1.77 us (2%)
    ppermute x6, waiting for transfers between devices, ahead(): return lax.ppermute(value, axis, pairs)  29.7 us
    ppermute x6, starting transfers between devices, ahead(): return lax.ppermute(value, axis, pairs)  17.8 us
    pallas_call x1, Pallas kernels, attend(): pl.pallas_call(functools.partial(attend_body, docs), in_specs=[SMEM] + [A...  8.48 us
    unnamed x36, local copies, waits for them, and re-layouts  8.17 us
    ppermute x8, starting transfers between devices, flip(): return lax.ppermute(value, axis, [(at, at ^ bit) for at in range(count)])  7.82 us
    ppermute x8, waiting for transfers between devices, flip(): return lax.ppermute(value, axis, [(at, at ^ bit) for at in range(count)])  6.8 us
    pallas_call x1, Pallas kernels, attend_last(): pl.pallas_call(functools.partial(attend_last_body, docs), in_specs=[SMEM]...  5.7 us
    pallas_call x1, Pallas kernels, hyena_near(): pl.pallas_call(functools.partial(hyena_near_body, modes), grid=(STEPS,),...  4.11 us
  transfers between devices with their start and end apart: 14, of which 7 were waited for; matrix products, arithmetic and copies ran while one was open for 6% of the time, Pallas kernels for 21%

profile of v3, /device:TPU:15, one launch (start us, length us, event | category | flops | bytes accessed | tf_op | source)
XLA Modules:
  0.0 105.0 jit_solution(15545942368609261772)
XLA Ops:
  0.7 1.4 %copy-done = bf16[128,3,2048]{2,0,1:T(8,128)(2,1)S(1)} copy-done((bf16[128,3,2048]{2,0,1:T(8,128)(2,1)S(1)}, bf16[128,3,2048]{2,0,1:T(8,128)(2,1)}, u32[]{:S(2)}) %copy-start) | copy-done | bytes 1572888
  2.9 1.5 %slice.3 = bf16[8,3,2048]{2,0,1:T(8,128)(2,1)} slice(bf16[128,3,2048]{2,0,1:T(8,128)(2,1)} %param.6), slice={[120:128], [0:3], [0:2048]} | slice | bytes 196608 | tf_op jit(solution)/shard_map/slice | solution.py:559
  4.4 3.1 %collective-permute-start = (bf16[8,3,2048]{2,0,1:T(8,128)(2,1)}, bf16[8,3,2048]{2,0,1:T(8,128)(2,1)S(1)}, u32[]{:S(2)}, u32[]{:S(2)}) collective-permute-start(bf16[8,3,2048]{2,0,1:T(8,128)(2,1)} %slice.3), channel_id=1, source_target_pairs={{0,1},{1,2},{2,3},{3,4},{4,5},{5,6},{6,7},{7,8},{8,9},{9,10},{10,1... | collective-permute-start | bytes 294920 | tf_op jit(solution)/shard_map/ppermute | solution.py:29
  7.8 1.7 %collective-permute-done = bf16[8,3,2048]{2,0,1:T(8,128)(2,1)S(1)} collective-permute-done((bf16[8,3,2048]{2,0,1:T(8,128)(2,1)}, bf16[8,3,2048]{2,0,1:T(8,128)(2,1)S(1)}, u32[]{:S(2)}, u32[]{:S(2)}) %collective-permute-start) | collective-permute-done | bytes 98336 | tf_op jit(solution)/shard_map/ppermute | solution.py:29
  9.5 1.4 %copy-done.2 = bf16[128,3,2048]{2,0,1:T(8,128)(2,1)S(1)} copy-done((bf16[128,3,2048]{2,0,1:T(8,128)(2,1)S(1)}, bf16[128,3,2048]{2,0,1:T(8,128)(2,1)}, u32[]{:S(2)}) %copy-start.2) | copy-done | bytes 1572888
  10.9 2.1 %hyena_ends.1 = (bf16[128,2048]{1,0:T(8,128)(2,1)S(1)}, f32[16,2048]{1,0:T(8,128)S(1)}, f32[16,2048]{1,0:T(8,128)S(1)}) custom-call(bf16[3,128,2048]{2,1,0:T(8,128)(2,1)S(1)} %bitcast.15, bf16[3,8,2048]{2,1,0:T(8,128)(2,1)S(1)} %bitcast.17, f32[3,3,2048]{2,1,0:T(4,128)S(1)} %copy-done.6, f32[16,1,128]{2,1,0:T(1,128)S(1)} %bitcast.19), custom_call_target="tpu_custom_call" | custom-call | flops 134217728 | bytes 2097152 | tf_op jit(solution)/shard_map/hyena_ends/pallas_call | solution.py:108
  13.0 0.8 copy-done.4
  13.8 1.2 %collective-permute-start.1 = (f32[16,1024]{1,0:T(8,128)S(1)}, f32[16,1024]{1,0:T(8,128)S(1)}, u32[]{:S(2)}, u32[]{:S(2)}) collective-permute-start(f32[16,1024]{1,0:T(8,128)S(1)} %constant_dynamic-slice_fusion), channel_id=1, source_target_pairs={{0,1},{1,0},{2,3},{3,2},{4,5},{5,4},{6,7},{7,6},{8,9},{9,8},{10,11... | collective-permute-start | bytes 196616 | tf_op jit(solution)/shard_map/ppermute | solution.py:23
  15.1 1.6 %pack.3 = (bf16[2,2,128,512]{3,2,1,0:T(8,128)(2,1)}, bf16[2,2,128,512]{3,2,1,0:T(8,128)(2,1)}) custom-call(s32[4]{0:T(128)S(1)} %pad_add_fusion.at_ref, bf16[3,128,2048]{2,1,0:T(8,128)(2,1)S(1)} %bitcast.11, bf16[3,128,1024]{2,1,0:T(8,128)(2,1)S(1)} %collective-permute-done.6.theirs_ref.theirs), custom_call_target="tpu_custom_call" | custom-call | bytes 2097152 | tf_op jit(solution)/shard_map/pack/pallas_call | solution.py:325
  16.7 3.2 %collective-permute-start.8 = (bf16[2,2,128,512]{3,2,1,0:T(8,128)(2,1)}, bf16[2,2,128,512]{3,2,1,0:T(8,128)(2,1)}, u32[]{:S(2)}, u32[]{:S(2)}) collective-permute-start(bf16[2,2,128,512]{3,2,1,0:T(8,128)(2,1)} %get-tuple-element.21), channel_id=1, source_target_pairs={{0,4},{1,5},{2,6},{3,7},{4,8},{5,9},{6,10},{7,11},{8,12},{9,13},{1... | collective-permute-start | bytes 1572872 | tf_op jit(solution)/shard_map/ppermute | solution.py:29
  19.9 4.0 %collective-permute-start.9 = (bf16[2,2,128,512]{3,2,1,0:T(8,128)(2,1)}, bf16[2,2,128,512]{3,2,1,0:T(8,128)(2,1)}, u32[]{:S(2)}, u32[]{:S(2)}) collective-permute-start(bf16[2,2,128,512]{3,2,1,0:T(8,128)(2,1)} %get-tuple-element.22), channel_id=1, source_target_pairs={{0,6},{1,7},{2,4},{3,5},{4,10},{5,11},{6,8},{7,9},{8,14},{9,15},{1... | collective-permute-start | bytes 1572872 | tf_op jit(solution)/shard_map/ppermute | solution.py:29
  24.9 3.2 %collective-permute-done.2 = f32[16,1024]{1,0:T(8,128)S(1)} collective-permute-done((f32[16,1024]{1,0:T(8,128)S(1)}, f32[16,1024]{1,0:T(8,128)S(1)}, u32[]{:S(2)}, u32[]{:S(2)}) %collective-permute-start.2) | collective-permute-done | bytes 65568 | tf_op jit(solution)/shard_map/ppermute | solution.py:23
  28.1 1.9 %collective-permute-start.3 = (f32[16,1024]{1,0:T(8,128)S(1)}, f32[16,1024]{1,0:T(8,128)S(1)}, u32[]{:S(2)}, u32[]{:S(2)}) collective-permute-start(f32[16,1024]{1,0:T(8,128)S(1)} %select_add_fusion), channel_id=1, source_target_pairs={{0,4},{1,5},{2,6},{3,7},{4,8},{5,9},{6,10},{7,11},{8,12},{9,13},{1... | collective-permute-start | bytes 196616 | tf_op jit(solution)/shard_map/ppermute | solution.py:29
  30.1 1.5 %pack.2 = bf16[2,3,128,512]{3,2,1,0:T(8,128)(2,1)} custom-call(s32[4]{0:T(128)S(1)} %pad_add_fusion.at_ref, bf16[3,128,2048]{2,1,0:T(8,128)(2,1)S(1)} %bitcast.12, bf16[3,128,1024]{2,1,0:T(8,128)(2,1)S(1)} %collective-permute-done.6.theirs_ref.theirs), custom_call_target="tpu_custom_call" | custom-call | bytes 1048576 | tf_op jit(solution)/shard_map/pack/pallas_call | solution.py:325
  32.4 12.1 %collective-permute-done.9.cross_ref.cross = bf16[2,2,128,512]{3,2,1,0:T(8,128)(2,1)} collective-permute-done((bf16[2,2,128,512]{3,2,1,0:T(8,128)(2,1)}, bf16[2,2,128,512]{3,2,1,0:T(8,128)(2,1)}, u32[]{:S(2)}, u32[]{:S(2)}) %collective-permute-start.9) | collective-permute-done | bytes 524320 | tf_op jit(solution)/shard_map/ppermute | solution.py:29
  44.5 2.2 %onward.1 = bf16[3,2,128,512]{3,2,1,0:T(8,128)(2,1)} custom-call(s32[4]{0:T(128)S(1)} %pad_add_fusion.at_ref, bf16[2,2,128,512]{3,2,1,0:T(8,128)(2,1)} %collective-permute-done.8.own_ref.own, bf16[2,2,128,512]{3,2,1,0:T(8,128)(2,1)} %collective-permute-done.9.cross_ref.cross), custom_call_target="tpu_custom_call" | custom-call | bytes 1048576 | tf_op jit(solution)/shard_map/onward/pallas_call | solution.py:351
  46.7 3.2 %collective-permute-start.10 = (bf16[3,2,128,512]{3,2,1,0:T(8,128)(2,1)}, bf16[3,2,128,512]{3,2,1,0:T(8,128)(2,1)}, u32[]{:S(2)}, u32[]{:S(2)}) collective-permute-start(bf16[3,2,128,512]{3,2,1,0:T(8,128)(2,1)} %onward.1), channel_id=1, source_target_pairs={{0,4},{1,5},{2,6},{3,7},{4,8},{5,9},{6,10},{7,11},{8,12},{9,13},{1... | collective-permute-start | bytes 2359304 | tf_op jit(solution)/shard_map/ppermute | solution.py:29
  49.9 2.3 %collective-permute-start.4 = (f32[16,1024]{1,0:T(8,128)S(1)}, f32[16,1024]{1,0:T(8,128)S(1)}, u32[]{:S(2)}, u32[]{:S(2)}) collective-permute-start(f32[16,1024]{1,0:T(8,128)S(1)} %multiply_add_fusion.1), channel_id=1, source_target_pairs={{0,8},{1,9},{2,10},{3,11},{4,12},{5,13},{6,14},{7,15},{16,24},{17,... | collective-permute-start | bytes 196616 | tf_op jit(solution)/shard_map/ppermute | solution.py:29
  52.2 15.5 %collective-permute-done.4 = f32[16,1024]{1,0:T(8,128)S(1)} collective-permute-done((f32[16,1024]{1,0:T(8,128)S(1)}, f32[16,1024]{1,0:T(8,128)S(1)}, u32[]{:S(2)}, u32[]{:S(2)}) %collective-permute-start.4) | collective-permute-done | bytes 65568 | tf_op jit(solution)/shard_map/ppermute | solution.py:29
  68.5 2.9 %collective-permute-start.5 = (f32[16,1024]{1,0:T(8,128)}, f32[16,1024]{1,0:T(8,128)}, u32[]{:S(2)}, u32[]{:S(2)}) collective-permute-start(f32[16,1024]{1,0:T(8,128)} %get-tuple-element.30), channel_id=1, source_target_pairs={{0,1},{1,0},{2,3},{3,2},{4,5},{5,4},{6,7},{7,6},{8,9},{9,8},{10,11... | collective-permute-start | bytes 196616 | tf_op jit(solution)/shard_map/ppermute | solution.py:23
  71.4 1.4 %copy.12 = f32[128,16]{1,0:T(8,128)} copy(f32[128,16]{0,1:T(8,128)} %param.9) | data formatting | bytes 16384 | tf_op args[3]
  72.9 0.9 reshape.14
  73.8 1.4 %copy-done.3 = bf16[128,3,2048]{2,0,1:T(8,128)(2,1)S(1)} copy-done((bf16[128,3,2048]{2,0,1:T(8,128)(2,1)S(1)}, bf16[128,3,2048]{2,0,1:T(8,128)(2,1)}, u32[]{:S(2)}) %copy-start.3) | copy-done | bytes 1572888
  75.2 1.0 copy-done.5
  76.2 4.1 %hyena_near.1 = (f32[128,2048]{1,0:T(8,128)S(1)}, f32[128,2048]{1,0:T(8,128)S(1)}) custom-call(bf16[3,128,2048]{2,1,0:T(8,128)(2,1)S(1)} %bitcast.16, bf16[3,8,2048]{2,1,0:T(8,128)(2,1)S(1)} %bitcast.18, f32[3,3,2048]{2,1,0:T(4,128)S(1)} %copy-done.6, bf16[128,2048]{1,0:T(8,128)(2,1)S(1)} %copy-done.5, f32[16,1,128]{2,1,0:T(1,128)S(1)} %bitcast.20, ...), custom_call_target="tpu_custom_call" | custom-call | flops 536870912 | bytes 3145728 | tf_op jit(solution)/shard_map/hyena_near/pallas_call | solution.py:173
  80.4 0.9 broadcast_select_fusion.2
  81.3 8.5 %attend.1 = (f32[4,128,512]{2,1,0:T(8,128)S(1)}, f32[4,128,4]{2,1,0:T(8,128)S(1)}, f32[4,128,4]{2,1,0:T(8,128)S(1)}) custom-call(s32[8]{0:T(128)S(1)} %concatenate.8.info_ref, bf16[3,128,2048]{2,1,0:T(8,128)(2,1)S(1)} %bitcast.13, bf16[3,128,1024]{2,1,0:T(8,128)(2,1)S(1)} %collective-permute-done.6.theirs_ref.theirs, ...), custom_call_target="tpu_custom_call" | custom-call | flops 872415232 | bytes 3670016 | tf_op jit(solution)/shard_map/attend/pallas_call | solution.py:436
  89.8 5.7 %attend_last.1 = (bf16[128,512]{1,0:T(8,128)(2,1)S(1)}, bf16[128,512]{1,0:T(8,128)(2,1)S(1)}, bf16[128,512]{1,0:T(8,128)(2,1)S(1)}, bf16[128,512]{1,0:T(8,128)(2,1)S(1)}) custom-call(s32[8]{0:T(128)S(1)} %concatenate.8.info_ref, bf16[3,128,2048]{2,1,0:T(8,128)(2,1)S(1)} %bitcast.14, bf16[3,128,1024]{2,1,0:T(8,128)(2,1)S(1)} %collective-permute-done.6.theirs_ref.theirs, ...), custom_call_target="tpu_custom_call" | custom-call | flops 201326592 | bytes 3145728 | tf_op jit(solution)/shard_map/attend_last/pallas_call | solution.py:510
  95.9 1.7 %collective-permute-start.13 = (bf16[128,512]{1,0:T(8,128)(2,1)S(1)}, bf16[128,512]{1,0:T(8,128)(2,1)S(1)}, u32[]{:S(2)}, u32[]{:S(2)}) collective-permute-start(bf16[128,512]{1,0:T(8,128)(2,1)S(1)} %get-tuple-element.29), channel_id=1, source_target_pairs={{0,3},{1,2},{2,1},{3,0},{4,7},{5,6},{6,5},{7,4},{8,11},{9,10},{10,... | collective-permute-start | bytes 393224 | tf_op jit(solution)/shard_map/ppermute | solution.py:23
  97.7 2.3 %hyena_finish.1 = bf16[128,2048]{1,0:T(8,128)(2,1)} custom-call(f32[128,2048]{1,0:T(8,128)S(1)} %get-tuple-element.17.near_ref, f32[128,2048]{1,0:T(8,128)S(1)} %get-tuple-element.18.q_ref, f32[16,2048]{1,0:T(8,128)S(1)} %pad_maximum_fusion.carried_ref, f32[16,1,128]{2,1,0:T(1,128)S(1)} %bitcast.21, f32[16,1,128]{2,1,0:T(1,128)S(1)} %bitcast.23), custom_call_target="tpu_custom_call" | custom-call | flops 201326592 | bytes 2621440 | tf_op jit(solution)/shard_map/hyena_finish/pallas_call | solution.py:235
  100.2 3.4 %collective-permute-done.13.refs_3_ = bf16[128,512]{1,0:T(8,128)(2,1)S(1)} collective-permute-done((bf16[128,512]{1,0:T(8,128)(2,1)S(1)}, bf16[128,512]{1,0:T(8,128)(2,1)S(1)}, u32[]{:S(2)}, u32[]{:S(2)}) %collective-permute-start.13) | collective-permute-done | bytes 131104 | tf_op jit(solution)/shard_map/ppermute | solution.py:23
  103.6 1.4 %assemble.1 = bf16[128,2048]{1,0:T(8,128)(2,1)} custom-call(s32[4]{0:T(128)S(1)} %pad_add_fusion.at_ref, bf16[128,512]{1,0:T(8,128)(2,1)S(1)} %get-tuple-element.26.refs_0_, bf16[128,512]{1,0:T(8,128)(2,1)S(1)} %collective-permute-done.11.refs_1_, bf16[128,512]{1,0:T(8,128)(2,1)S(1)} %collective-permute-done.12.refs_2_, ...), custom_call_target="tpu_custom_call" | custom-call | bytes 1048576 | tf_op jit(solution)/shard_map/assemble/pallas_call | solution.py:538
  (54 shorter events, 4.4 us)
Async XLA Ops:
  0.6 7.0 %copy-start.15 = (f32[128,16]{0,1:T(8,128)S(1)}, f32[128,16]{0,1:T(8,128)}, u32[]{:S(2)}) copy-start(f32[128,16]{0,1:T(8,128)} %param.8) | copy-start | bytes 24580
  0.7 1.4 %copy-start = (bf16[128,3,2048]{2,0,1:T(8,128)(2,1)S(1)}, bf16[128,3,2048]{2,0,1:T(8,128)(2,1)}, u32[]{:S(2)}) copy-start(bf16[128,3,2048]{2,0,1:T(8,128)(2,1)} %param.10) | copy-start | bytes 4718596
  2.1 7.4 %copy-start.6 = (f32[3,3,2048]{2,1,0:T(4,128)S(1)}, f32[3,3,2048]{2,1,0:T(4,128)}, u32[]{:S(2)}) copy-start(f32[3,3,2048]{2,1,0:T(4,128)} %w_ref.3) | copy-start | bytes 221188
  2.1 13.0 %copy-start.1 = (bf16[128,3,2048]{2,0,1:T(8,128)(2,1)S(1)}, bf16[128,3,2048]{2,0,1:T(8,128)(2,1)}, u32[]{:S(2)}) copy-start(bf16[128,3,2048]{2,0,1:T(8,128)(2,1)} %param.10) | copy-start | bytes 4718596
  2.2 13.0 %collective-permute-start.6 = (bf16[3,128,1024]{2,1,0:T(8,128)(2,1)S(1)}, bf16[3,128,1024]{2,1,0:T(8,128)(2,1)S(1)}, u32[]{:S(2)}, u32[]{:S(2)}) collective-permute-start(bf16[3,128,1024]{2,1,0:T(8,128)(2,1)S(1)} %halve.1), channel_id=1, source_target_pairs={{0,1},{1,0},{2,3},{3,2},{4,5},{5,4},{6,7},{7,6},{8,9},{9,8},{10,11... | collective-permute-start | bytes 2359304 | tf_op jit(solution)/shard_map/ppermute | solution.py:23
  4.4 5.1 %collective-permute-start = (bf16[8,3,2048]{2,0,1:T(8,128)(2,1)}, bf16[8,3,2048]{2,0,1:T(8,128)(2,1)S(1)}, u32[]{:S(2)}, u32[]{:S(2)}) collective-permute-start(bf16[8,3,2048]{2,0,1:T(8,128)(2,1)} %slice.3), channel_id=1, source_target_pairs={{0,1},{1,2},{2,3},{3,4},{4,5},{5,6},{6,7},{7,8},{8,9},{9,10},{10,1... | collective-permute-start | bytes 294920 | tf_op jit(solution)/shard_map/ppermute | solution.py:29
  9.5 1.4 %copy-start.2 = (bf16[128,3,2048]{2,0,1:T(8,128)(2,1)S(1)}, bf16[128,3,2048]{2,0,1:T(8,128)(2,1)}, u32[]{:S(2)}) copy-start(bf16[128,3,2048]{2,0,1:T(8,128)(2,1)} %param.6) | copy-start | bytes 4718596
  13.0 0.8 copy-start.4
  13.8 10.2 %copy-start.7 = (f32[16,2048]{1,0:T(8,128)}, f32[16,2048]{1,0:T(8,128)S(1)}, u32[]{:S(2)}) copy-start(f32[16,2048]{1,0:T(8,128)S(1)} %get-tuple-element.20) | copy-start | bytes 393220
  13.8 10.2 %collective-permute-start.1 = (f32[16,1024]{1,0:T(8,128)S(1)}, f32[16,1024]{1,0:T(8,128)S(1)}, u32[]{:S(2)}, u32[]{:S(2)}) collective-permute-start(f32[16,1024]{1,0:T(8,128)S(1)} %constant_dynamic-slice_fusion), channel_id=1, source_target_pairs={{0,1},{1,0},{2,3},{3,2},{4,5},{5,4},{6,7},{7,6},{8,9},{9,8},{10,11... | collective-permute-start | bytes 196616 | tf_op jit(solution)/shard_map/ppermute | solution.py:23
  16.7 15.7 %collective-permute-start.8 = (bf16[2,2,128,512]{3,2,1,0:T(8,128)(2,1)}, bf16[2,2,128,512]{3,2,1,0:T(8,128)(2,1)}, u32[]{:S(2)}, u32[]{:S(2)}) collective-permute-start(bf16[2,2,128,512]{3,2,1,0:T(8,128)(2,1)} %get-tuple-element.21), channel_id=1, source_target_pairs={{0,4},{1,5},{2,6},{3,7},{4,8},{5,9},{6,10},{7,11},{8,12},{9,13},{1... | collective-permute-start | bytes 1572872 | tf_op jit(solution)/shard_map/ppermute | solution.py:29
  19.9 24.6 %collective-permute-start.9 = (bf16[2,2,128,512]{3,2,1,0:T(8,128)(2,1)}, bf16[2,2,128,512]{3,2,1,0:T(8,128)(2,1)}, u32[]{:S(2)}, u32[]{:S(2)}) collective-permute-start(bf16[2,2,128,512]{3,2,1,0:T(8,128)(2,1)} %get-tuple-element.22), channel_id=1, source_target_pairs={{0,6},{1,7},{2,4},{3,5},{4,10},{5,11},{6,8},{7,9},{8,14},{9,15},{1... | collective-permute-start | bytes 1572872 | tf_op jit(solution)/shard_map/ppermute | solution.py:29
  24.0 0.6 copy-start.11
  24.6 3.5 %collective-permute-start.2 = (f32[16,1024]{1,0:T(8,128)S(1)}, f32[16,1024]{1,0:T(8,128)S(1)}, u32[]{:S(2)}, u32[]{:S(2)}) collective-permute-start(f32[16,1024]{1,0:T(8,128)S(1)} %select_add_fusion.1), channel_id=1, source_target_pairs={{0,2},{1,3},{2,0},{3,1},{4,6},{5,7},{6,4},{7,5},{8,10},{9,11},{10,... | collective-permute-start | bytes 196616 | tf_op jit(solution)/shard_map/ppermute | solution.py:23
  28.1 2.0 %copy-start.13 = (f32[16,1024]{1,0:T(8,128)}, f32[16,1024]{1,0:T(8,128)S(1)}, u32[]{:S(2)}) copy-start(f32[16,1024]{1,0:T(8,128)S(1)} %collective-permute-done.2) | copy-start | bytes 196612
  28.1 21.7 %collective-permute-start.3 = (f32[16,1024]{1,0:T(8,128)S(1)}, f32[16,1024]{1,0:T(8,128)S(1)}, u32[]{:S(2)}, u32[]{:S(2)}) collective-permute-start(f32[16,1024]{1,0:T(8,128)S(1)} %select_add_fusion), channel_id=1, source_target_pairs={{0,4},{1,5},{2,6},{3,7},{4,8},{5,9},{6,10},{7,11},{8,12},{9,13},{1... | collective-permute-start | bytes 196616 | tf_op jit(solution)/shard_map/ppermute | solution.py:29
  31.6 36.2 %copy-start.8 = (f32[16,2048]{1,0:T(8,128)S(1)}, f32[16,2048]{1,0:T(8,128)}, u32[]{:S(2)}) copy-start(f32[16,2048]{1,0:T(8,128)} %copy-done.7) | copy-start | bytes 393220
  31.6 36.2 %copy-start.12 = (f32[16,1024]{1,0:T(8,128)S(1)}, f32[16,1024]{1,0:T(8,128)}, u32[]{:S(2)}) copy-start(f32[16,1024]{1,0:T(8,128)} %copy-done.11) | copy-start | bytes 196612
  31.6 36.2 %copy-start.14 = (f32[16,1024]{1,0:T(8,128)S(1)}, f32[16,1024]{1,0:T(8,128)}, u32[]{:S(2)}) copy-start(f32[16,1024]{1,0:T(8,128)} %copy-done.13) | copy-start | bytes 196612
  31.6 39.8 %copy-start.16 = (s32[4]{0:T(128)S(1)}, s32[4]{0:T(128)}, u32[]{:S(2)}) copy-start(s32[4]{0:T(128)} %param.11) | copy-start | bytes 52
  31.6 49.7 %collective-permute-start.7 = (bf16[2,3,128,512]{3,2,1,0:T(8,128)(2,1)}, bf16[2,3,128,512]{3,2,1,0:T(8,128)(2,1)S(1)}, u32[]{:S(2)}, u32[]{:S(2)}) collective-permute-start(bf16[2,3,128,512]{3,2,1,0:T(8,128)(2,1)} %pack.2), channel_id=1, source_target_pairs={{0,2},{1,3},{2,0},{3,1},{4,6},{5,7},{6,4},{7,5},{8,10},{9,11},{10,... | collective-permute-start | bytes 2359304 | tf_op jit(solution)/shard_map/ppermute | solution.py:23
  46.7 43.1 %collective-permute-start.10 = (bf16[3,2,128,512]{3,2,1,0:T(8,128)(2,1)}, bf16[3,2,128,512]{3,2,1,0:T(8,128)(2,1)}, u32[]{:S(2)}, u32[]{:S(2)}) collective-permute-start(bf16[3,2,128,512]{3,2,1,0:T(8,128)(2,1)} %onward.1), channel_id=1, source_target_pairs={{0,4},{1,5},{2,6},{3,7},{4,8},{5,9},{6,10},{7,11},{8,12},{9,13},{1... | collective-permute-start | bytes 2359304 | tf_op jit(solution)/shard_map/ppermute | solution.py:29
  49.9 17.8 %collective-permute-start.4 = (f32[16,1024]{1,0:T(8,128)S(1)}, f32[16,1024]{1,0:T(8,128)S(1)}, u32[]{:S(2)}, u32[]{:S(2)}) collective-permute-start(f32[16,1024]{1,0:T(8,128)S(1)} %multiply_add_fusion.1), channel_id=1, source_target_pairs={{0,8},{1,9},{2,10},{3,11},{4,12},{5,13},{6,14},{7,15},{16,24},{17,... | collective-permute-start | bytes 196616 | tf_op jit(solution)/shard_map/ppermute | solution.py:29
  68.5 11.9 %copy-start.9 = (f32[16,1024]{1,0:T(8,128)S(1)}, f32[16,1024]{1,0:T(8,128)}, u32[]{:S(2)}) copy-start(f32[16,1024]{1,0:T(8,128)} %get-tuple-element.31) | copy-start | bytes 196612
  68.5 11.9 %copy-start.10 = (f32[16,1024]{1,0:T(8,128)S(1)}, f32[16,1024]{1,0:T(8,128)}, u32[]{:S(2)}) copy-start(f32[16,1024]{1,0:T(8,128)} %get-tuple-element.32) | copy-start | bytes 196612
  68.5 11.9 %collective-permute-start.5 = (f32[16,1024]{1,0:T(8,128)}, f32[16,1024]{1,0:T(8,128)}, u32[]{:S(2)}, u32[]{:S(2)}) collective-permute-start(f32[16,1024]{1,0:T(8,128)} %get-tuple-element.30), channel_id=1, source_target_pairs={{0,1},{1,0},{2,3},{3,2},{4,5},{5,4},{6,7},{7,6},{8,9},{9,8},{10,11... | collective-permute-start | bytes 196616 | tf_op jit(solution)/shard_map/ppermute | solution.py:23
  73.8 1.4 %copy-start.3 = (bf16[128,3,2048]{2,0,1:T(8,128)(2,1)S(1)}, bf16[128,3,2048]{2,0,1:T(8,128)(2,1)}, u32[]{:S(2)}) copy-start(bf16[128,3,2048]{2,0,1:T(8,128)(2,1)} %param.6) | copy-start | bytes 4718596
  75.2 1.0 copy-start.5
  95.5 4.6 %collective-permute-start.11 = (bf16[128,512]{1,0:T(8,128)(2,1)S(1)}, bf16[128,512]{1,0:T(8,128)(2,1)S(1)}, u32[]{:S(2)}, u32[]{:S(2)}) collective-permute-start(bf16[128,512]{1,0:T(8,128)(2,1)S(1)} %get-tuple-element.27), channel_id=1, source_target_pairs={{0,1},{1,0},{2,3},{3,2},{4,5},{5,4},{6,7},{7,6},{8,9},{9,8},{10,11... | collective-permute-start | bytes 393224 | tf_op jit(solution)/shard_map/ppermute | solution.py:23
  95.5 4.7 %collective-permute-start.12 = (bf16[128,512]{1,0:T(8,128)(2,1)S(1)}, bf16[128,512]{1,0:T(8,128)(2,1)S(1)}, u32[]{:S(2)}, u32[]{:S(2)}) collective-permute-start(bf16[128,512]{1,0:T(8,128)(2,1)S(1)} %get-tuple-element.28), channel_id=1, source_target_pairs={{0,2},{1,3},{2,0},{3,1},{4,6},{5,7},{6,4},{7,5},{8,10},{9,11},{10,... | collective-permute-start | bytes 393224 | tf_op jit(solution)/shard_map/ppermute | solution.py:23
  95.9 7.7 %collective-permute-start.13 = (bf16[128,512]{1,0:T(8,128)(2,1)S(1)}, bf16[128,512]{1,0:T(8,128)(2,1)S(1)}, u32[]{:S(2)}, u32[]{:S(2)}) collective-permute-start(bf16[128,512]{1,0:T(8,128)(2,1)S(1)} %get-tuple-element.29), channel_id=1, source_target_pairs={{0,3},{1,2},{2,1},{3,0},{4,7},{5,6},{6,5},{7,4},{8,11},{9,10},{10,... | collective-permute-start | bytes 393224 | tf_op jit(solution)/shard_map/ppermute | solution.py:23

commit v4 on v3

--- a/solution.py
+++ b/solution.py
@@ -124,7 +124,7 @@
             jax.ShapeDtypeStruct((modes, channels), F32),
             jax.ShapeDtypeStruct((modes, channels), F32),
         ],
-        compiler_params=limits(16),
+        compiler_params=limits(58),
         cost_estimate=cost(4 * rows * terms * channels, 8 * rows * channels),
         name="hyena_ends",
     )(streams, halo, short_weight, rate_rows)
@@ -193,7 +193,7 @@
             pltpu.VMEM((parts, rows, filters * rows), BF16),
             pltpu.VMEM((parts, filters * rows, lanes), BF16),
         ],
-        compiler_params=limits(16),
+        compiler_params=limits(58),
         cost_estimate=cost(2 * rows * rows * filters * channels, 12 * rows * channels),
         name="hyena_near",
     )(streams, halo, short_weight, mixed, rate_rows, res_rows)
@@ -244,7 +244,7 @@
         ],
         out_specs=pl.BlockSpec((rows, wide), by_block),
         out_shape=jax.ShapeDtypeStruct((rows, channels), BF16),
-        compiler_params=limits(16),
+        compiler_params=limits(58),
         cost_estimate=cost(6 * rows * terms * channels, 10 * rows * channels),
         name="hyena_finish",
     )(near, query, carried, rate_rows, res_rows)
@@ -309,6 +309,20 @@
     )(which, streams)
 
 
+def last_rows(streams):
+    count, rows, channels = streams.shape
+    return pl.pallas_call(
+        lambda rows_ref, out_ref: out_ref.__setitem__(..., rows_ref[:, EDGE:]),
+        grid=(1,),
+        in_specs=[pl.BlockSpec((count, 2 * EDGE, channels), lambda n: (0, rows // (2 * EDGE) - 1, 0))],
+        out_specs=pl.BlockSpec((count, EDGE, channels), lambda n: (0, 0, 0)),
+        out_shape=jax.ShapeDtypeStruct((count, EDGE, channels), streams.dtype),
+        compiler_params=limits(58),
+        cost_estimate=cost(0, 4 * count * EDGE * channels),
+        name="last_rows",
+    )(streams)
+
+
 def pack_body(first, at_ref, streams_ref, theirs_ref, *outs):
     core, side = at_ref[0], at_ref[1]
     quarter = theirs_ref.shape[2] // 2
@@ -333,27 +347,39 @@
     )(where, streams, theirs)
 
 
-def onward_body(at_ref, own_ref, cross_ref, out_ref):
+def onward_body(at_ref, own, cross, out, held, sems):
     place = at_ref[2]
     for block in range(1, ROW):
         slot = place ^ block
+        into = held.at[block - 1]
 
         @pl.when(slot < 2)
         def _():
-            out_ref[block - 1] = own_ref[slot]
+            pltpu.make_async_copy(own.at[slot], into, sems.at[block - 1]).start()
 
         @pl.when(slot >= 2)
         def _():
-            out_ref[block - 1] = cross_ref[slot - 2]
+            pltpu.make_async_copy(cross.at[slot - 2], into, sems.at[block - 1]).start()
+
+    leave = []
+    for block in range(1, ROW):
+        into = held.at[block - 1]
+        pltpu.make_async_copy(own.at[0], into, sems.at[block - 1]).wait()
+        leave.append(pltpu.make_async_copy(into, out.at[block - 1], sems.at[ROW + block - 2]))
+        leave[-1].start()
+    for copy in leave:
+        copy.wait()
 
 
 def onward(where, own, cross):
+    shape = (ROW - 1,) + own.shape[1:]
     return pl.pallas_call(
         onward_body,
-        in_specs=[SMEM, VMEM, VMEM],
-        out_specs=VMEM,
-        out_shape=jax.ShapeDtypeStruct((ROW - 1,) + own.shape[1:], BF16),
-        compiler_params=limits(6),
+        in_specs=[SMEM, ANY, ANY],
+        out_specs=ANY,
+        out_shape=jax.ShapeDtypeStruct(shape, BF16),
+        scratch_shapes=[pltpu.VMEM(shape, BF16), pltpu.SemaphoreType.DMA((2 * ROW - 2,))],
+        compiler_params=limits(8),
         cost_estimate=cost(0, 4 * own.size),
         name="onward",
     )(where, own, cross)
@@ -423,8 +449,8 @@
             scores = jnp.where(allowed, scores, -jnp.inf)
             top = jnp.max(scores, axis=1, keepdims=True)
             weight = jnp.exp2((scores - top) * SCALE)
-            m_ref[block, :, head : head + 1] = top
-            l_ref[block, :, head : head + 1] = jnp.sum(weight, axis=1, keepdims=True)
+            m_ref[block, :, lanes] = jnp.broadcast_to(top, (rows, HEAD))
+            l_ref[block, :, lanes] = jnp.broadcast_to(jnp.sum(weight, axis=1, keepdims=True), (rows, HEAD))
             acc_ref[block, :, lanes] = jnp.dot(
                 weight.astype(BF16), v_s[0:width, lanes], preferred_element_type=F32
             )
@@ -439,9 +465,8 @@
         out_specs=[VMEM] * 3,
         out_shape=[
             jax.ShapeDtypeStruct((ROW, rows, quarter), F32),
-            jax.ShapeDtypeStruct((ROW, rows, heads), F32),
-            jax.ShapeDtypeStruct((ROW, rows, heads), F32),
-        ],
+        ]
+        * 3,
         scratch_shapes=[
             pltpu.VMEM((ROW, rows, quarter), BF16),
             pltpu.VMEM((2 * ROW * rows, quarter), BF16),
@@ -478,7 +503,7 @@
         for head in range(quarter // HEAD):
             lanes = slice(head * HEAD, (head + 1) * HEAD)
             total = acc_ref[block, :, lanes]
-            below = l_ref[block, :, head : head + 1]
+            below = l_ref[block, :, lanes]
             if seen:
                 keys = oldest[block : ROW - 1, 0, :, lanes].reshape(width, HEAD)
                 values = oldest[block : ROW - 1, 1, :, lanes].reshape(width, HEAD)
@@ -489,10 +514,10 @@
                     preferred_element_type=F32,
                 )
                 scores = jnp.where(allowed, scores, -jnp.inf)
-                past = m_ref[block, :, head : head + 1]
+                past = m_ref[block, :, lanes]
                 top = jnp.maximum(past, jnp.max(scores, axis=1, keepdims=True))
                 fade = jnp.exp2((past - top) * SCALE)
-                weight = jnp.exp2((scores - top) * SCALE)
+                weight = jnp.exp2((scores - jnp.concatenate([top] * seen, axis=1)) * SCALE)
                 share = 1.0 / (below * fade + jnp.sum(weight, axis=1, keepdims=True))
                 total = total * (fade * share) + share * jnp.dot(
                     weight.astype(BF16), values, preferred_element_type=F32
@@ -556,7 +581,8 @@
     fixed = jnp.stack([core, side, place, (index - place) * rows]).astype(jnp.int32)
     info = jnp.concatenate([fixed, doc_lengths])
 
-    edge = ahead(hyena_qkv[rows - EDGE :], "ctx", 1)
+    inner = hyena_qkv.transpose(1, 0, 2)
+    edge = ahead(last_rows(inner), "ctx", 1)
 
     streams = attn_qkv.transpose(1, 0, 2)
     theirs = flip(halve((1 - core).reshape(1).astype(jnp.int32), streams), "ctx", 1)
@@ -570,7 +596,6 @@
     blocks = channels // LANES
     rate_rows = filter_rate.reshape(blocks, 1, -1)
     res_rows = filter_residue.reshape(blocks, 1, -1)
-    inner, edge = hyena_qkv.transpose(1, 0, 2), edge.transpose(1, 0, 2)
     mixed, ends, wide = hyena_ends(inner, edge, short_weight, rate_rows, modes)
     near, query = hyena_near(inner, edge, short_weight, mixed, rate_rows, res_rows, modes)
     carried = scan_states(ends, wide, rows)

time: 107 us -> 103 us (0.963)
  Pallas kernels: 29.4 us -> 35.1 us
  local copies, waits for them, and re-layouts: 10.8 us -> 5.25 us
  waiting for transfers between devices: 36.5 us -> 33.5 us
    unnamed x36 -> x28, local copies, waits for them, and re-layouts: 8.17 us -> 2.89 us
    ppermute x8, waiting for transfers between devices: 6.8 us -> 4.48 us  [flip(): return lax.ppermute(value, axis, [(at, at ^ bit) for at in range(count)])]
    pallas_call x1, Pallas kernels: 2.06 us -> 4.22 us  [hyena_ends(): pl.pallas_call(functools.partial(hyena_ends_body, modes), grid=(STEPS,),...]
    pallas_call x1 -> x2, Pallas kernels: 2.17 us -> 4.12 us  [the longest x1 2.43 us: onward(): pl.pallas_call(onward_body, in_specs=[SMEM, ANY, ANY], out_specs=ANY, out...]
    pallas_call x1, Pallas kernels: 4.11 us -> 5.85 us  [hyena_near(): pl.pallas_call(functools.partial(hyena_near_body, modes), grid=(STEPS,),...]
    pallas_call x1, Pallas kernels: 5.7 us -> 3.97 us  [attend_last(): pl.pallas_call(functools.partial(attend_last_body, docs), in_specs=[SMEM]...]
    pallas_call x1, Pallas kernels: 2.34 us -> 4.01 us  [hyena_finish(): pl.pallas_call(functools.partial(hyena_out_body, modes), grid=(STEPS,), i...]
    slice x1 -> x0, local copies, waits for them, and re-layouts: 1.54 us -> none  [on_device(): edge = ahead(hyena_qkv[rows - EDGE:], 'ctx', 1)]
  transfers between devices with their start and end apart: 14 -> 14, of which waited for: 7 -> 6; matrix products, arithmetic and copies ran while one was open for 6% -> 4% of each run, Pallas kernels for 21% -> 29%
where the time goes in v4:
time: 103 us; the launch traced here: 102 us
  Pallas kernels  35.1 us (34%)
  waiting for transfers between devices  33.5 us (33%)
  starting transfers between devices  25.5 us (25%)
  local copies, waits for them, and re-layouts  5.25 us (5%)
  other arithmetic  1.54 us (1%)
    ppermute x6, waiting for transfers between devices, ahead(): return lax.ppermute(value, axis, pairs)  29 us
    ppermute x6, starting transfers between devices, ahead(): return lax.ppermute(value, axis, pairs)  17.7 us
    pallas_call x1, Pallas kernels, attend(): pl.pallas_call(functools.partial(attend_body, docs), in_specs=[SMEM] + [A...  8.47 us
    ppermute x8, starting transfers between devices, flip(): return lax.ppermute(value, axis, [(at, at ^ bit) for at in range(count)])  7.8 us
    pallas_call x1, Pallas kernels, hyena_near(): pl.pallas_call(functools.partial(hyena_near_body, modes), grid=(STEPS,),...  5.85 us
    ppermute x8, waiting for transfers between devices, flip(): return lax.ppermute(value, axis, [(at, at ^ bit) for at in range(count)])  4.48 us
    pallas_call x1, Pallas kernels, hyena_ends(): pl.pallas_call(functools.partial(hyena_ends_body, modes), grid=(STEPS,),...  4.22 us
    pallas_call x1, Pallas kernels, hyena_finish(): pl.pallas_call(functools.partial(hyena_out_body, modes), grid=(STEPS,), i...  4.01 us
  transfers between devices with their start and end apart: 14, of which 6 were waited for; matrix products, arithmetic and copies ran while one was open for 4% of the time, Pallas kernels for 29%

profile of v4, /device:TPU:15, one launch (start us, length us, event | category | flops | bytes accessed | tf_op | source)
XLA Modules:
  0.0 101.9 jit_solution(5806051409650390513)
XLA Ops:
  0.7 1.4 %copy-done = bf16[128,3,2048]{2,0,1:T(8,128)(2,1)S(1)} copy-done((bf16[128,3,2048]{2,0,1:T(8,128)(2,1)S(1)}, bf16[128,3,2048]{2,0,1:T(8,128)(2,1)}, u32[]{:S(2)}) %copy-start) | copy-done | bytes 1572888
  2.1 0.7 collective-permute-start.6
  2.9 1.7 %last_rows.1 = bf16[3,8,2048]{2,1,0:T(8,128)(2,1)} custom-call(bf16[3,128,2048]{2,1,0:T(8,128)(2,1)} %bitcast.14), custom_call_target="tpu_custom_call" | custom-call | bytes 196608 | tf_op jit(solution)/shard_map/last_rows/pallas_call | solution.py:314
  4.6 3.0 %collective-permute-start = (bf16[3,8,2048]{2,1,0:T(8,128)(2,1)}, bf16[3,8,2048]{2,1,0:T(8,128)(2,1)S(1)}, u32[]{:S(2)}, u32[]{:S(2)}) collective-permute-start(bf16[3,8,2048]{2,1,0:T(8,128)(2,1)} %last_rows.1), channel_id=1, source_target_pairs={{0,1},{1,2},{2,3},{3,4},{4,5},{5,6},{6,7},{7,8},{8,9},{9,10},{10,1... | collective-permute-start | bytes 294920 | tf_op jit(solution)/shard_map/ppermute | solution.py:29
  7.8 0.7 reshape.13
  8.5 1.1 %collective-permute-done.halo_ref = bf16[3,8,2048]{2,1,0:T(8,128)(2,1)S(1)} collective-permute-done((bf16[3,8,2048]{2,1,0:T(8,128)(2,1)}, bf16[3,8,2048]{2,1,0:T(8,128)(2,1)S(1)}, u32[]{:S(2)}, u32[]{:S(2)}) %collective-permute-start) | collective-permute-done | bytes 98336 | tf_op jit(solution)/shard_map/ppermute | solution.py:29
  9.6 0.6 copy-done.3
  10.2 4.2 %hyena_ends.1 = (bf16[128,2048]{1,0:T(8,128)(2,1)}, f32[16,2048]{1,0:T(8,128)}, f32[16,2048]{1,0:T(8,128)}) custom-call(bf16[3,128,2048]{2,1,0:T(8,128)(2,1)} %bitcast.15, bf16[3,8,2048]{2,1,0:T(8,128)(2,1)} %copy-done.3, f32[3,3,2048]{2,1,0:T(4,128)} %w_ref.3, f32[16,1,128]{2,1,0:T(1,128)} %bitcast.17), custom_call_target="tpu_custom_call" | custom-call | flops 134217728 | bytes 2097152 | tf_op jit(solution)/shard_map/hyena_ends/pallas_call | solution.py:108
  14.4 0.9 constant_dynamic-slice_fusion
  15.3 1.2 %collective-permute-start.1 = (f32[16,1024]{1,0:T(8,128)S(1)}, f32[16,1024]{1,0:T(8,128)S(1)}, u32[]{:S(2)}, u32[]{:S(2)}) collective-permute-start(f32[16,1024]{1,0:T(8,128)S(1)} %constant_dynamic-slice_fusion), channel_id=1, source_target_pairs={{0,1},{1,0},{2,3},{3,2},{4,5},{5,4},{6,7},{7,6},{8,9},{9,8},{10,11... | collective-permute-start | bytes 196616 | tf_op jit(solution)/shard_map/ppermute | solution.py:23
  16.6 1.6 %pack.3 = (bf16[2,2,128,512]{3,2,1,0:T(8,128)(2,1)}, bf16[2,2,128,512]{3,2,1,0:T(8,128)(2,1)}) custom-call(s32[4]{0:T(128)S(1)} %pad_add_fusion.at_ref, bf16[3,128,2048]{2,1,0:T(8,128)(2,1)S(1)} %bitcast.10, bf16[3,128,1024]{2,1,0:T(8,128)(2,1)S(1)} %collective-permute-done.6.theirs_ref.theirs), custom_call_target="tpu_custom_call" | custom-call | bytes 2097152 | tf_op jit(solution)/shard_map/pack/pallas_call | solution.py:339
  18.2 3.2 %collective-permute-start.8 = (bf16[2,2,128,512]{3,2,1,0:T(8,128)(2,1)}, bf16[2,2,128,512]{3,2,1,0:T(8,128)(2,1)}, u32[]{:S(2)}, u32[]{:S(2)}) collective-permute-start(bf16[2,2,128,512]{3,2,1,0:T(8,128)(2,1)} %get-tuple-element.21), channel_id=1, source_target_pairs={{0,4},{1,5},{2,6},{3,7},{4,8},{5,9},{6,10},{7,11},{8,12},{9,13},{1... | collective-permute-start | bytes 1572872 | tf_op jit(solution)/shard_map/ppermute | solution.py:29
  21.4 4.0 %collective-permute-start.9 = (bf16[2,2,128,512]{3,2,1,0:T(8,128)(2,1)}, bf16[2,2,128,512]{3,2,1,0:T(8,128)(2,1)}, u32[]{:S(2)}, u32[]{:S(2)}) collective-permute-start(bf16[2,2,128,512]{3,2,1,0:T(8,128)(2,1)} %get-tuple-element.22), channel_id=1, source_target_pairs={{0,6},{1,7},{2,4},{3,5},{4,10},{5,11},{6,8},{7,9},{8,14},{9,15},{1... | collective-permute-start | bytes 1572872 | tf_op jit(solution)/shard_map/ppermute | solution.py:29
  26.5 3.2 %collective-permute-done.2 = f32[16,1024]{1,0:T(8,128)S(1)} collective-permute-done((f32[16,1024]{1,0:T(8,128)S(1)}, f32[16,1024]{1,0:T(8,128)S(1)}, u32[]{:S(2)}, u32[]{:S(2)}) %collective-permute-start.2) | collective-permute-done | bytes 65568 | tf_op jit(solution)/shard_map/ppermute | solution.py:23
  29.7 1.9 %collective-permute-start.3 = (f32[16,1024]{1,0:T(8,128)S(1)}, f32[16,1024]{1,0:T(8,128)S(1)}, u32[]{:S(2)}, u32[]{:S(2)}) collective-permute-start(f32[16,1024]{1,0:T(8,128)S(1)} %select_add_fusion), channel_id=1, source_target_pairs={{0,4},{1,5},{2,6},{3,7},{4,8},{5,9},{6,10},{7,11},{8,12},{9,13},{1... | collective-permute-start | bytes 196616 | tf_op jit(solution)/shard_map/ppermute | solution.py:29
  31.7 1.5 %pack.2 = bf16[2,3,128,512]{3,2,1,0:T(8,128)(2,1)} custom-call(s32[4]{0:T(128)S(1)} %pad_add_fusion.at_ref, bf16[3,128,2048]{2,1,0:T(8,128)(2,1)S(1)} %bitcast.11, bf16[3,128,1024]{2,1,0:T(8,128)(2,1)S(1)} %collective-permute-done.6.theirs_ref.theirs), custom_call_target="tpu_custom_call" | custom-call | bytes 1048576 | tf_op jit(solution)/shard_map/pack/pallas_call | solution.py:339
  33.9 12.1 %collective-permute-done.9.cross = bf16[2,2,128,512]{3,2,1,0:T(8,128)(2,1)} collective-permute-done((bf16[2,2,128,512]{3,2,1,0:T(8,128)(2,1)}, bf16[2,2,128,512]{3,2,1,0:T(8,128)(2,1)}, u32[]{:S(2)}, u32[]{:S(2)}) %collective-permute-start.9) | collective-permute-done | bytes 524320 | tf_op jit(solution)/shard_map/ppermute | solution.py:29
  46.0 2.4 %onward.1 = bf16[3,2,128,512]{3,2,1,0:T(8,128)(2,1)} custom-call(s32[4]{0:T(128)S(1)} %pad_add_fusion.at_ref, bf16[2,2,128,512]{3,2,1,0:T(8,128)(2,1)} %collective-permute-done.8.own, bf16[2,2,128,512]{3,2,1,0:T(8,128)(2,1)} %collective-permute-done.9.cross), custom_call_target="tpu_custom_call" | custom-call | bytes 1048576 | tf_op jit(solution)/shard_map/onward/pallas_call | solution.py:376
  48.4 3.2 %collective-permute-start.10 = (bf16[3,2,128,512]{3,2,1,0:T(8,128)(2,1)}, bf16[3,2,128,512]{3,2,1,0:T(8,128)(2,1)}, u32[]{:S(2)}, u32[]{:S(2)}) collective-permute-start(bf16[3,2,128,512]{3,2,1,0:T(8,128)(2,1)} %onward.1), channel_id=1, source_target_pairs={{0,4},{1,5},{2,6},{3,7},{4,8},{5,9},{6,10},{7,11},{8,12},{9,13},{1... | collective-permute-start | bytes 2359304 | tf_op jit(solution)/shard_map/ppermute | solution.py:29
  51.7 2.3 %collective-permute-start.4 = (f32[16,1024]{1,0:T(8,128)S(1)}, f32[16,1024]{1,0:T(8,128)S(1)}, u32[]{:S(2)}, u32[]{:S(2)}) collective-permute-start(f32[16,1024]{1,0:T(8,128)S(1)} %multiply_add_fusion.1), channel_id=1, source_target_pairs={{0,8},{1,9},{2,10},{3,11},{4,12},{5,13},{6,14},{7,15},{16,24},{17,... | collective-permute-start | bytes 196616 | tf_op jit(solution)/shard_map/ppermute | solution.py:29
  54.0 15.5 %collective-permute-done.4 = f32[16,1024]{1,0:T(8,128)S(1)} collective-permute-done((f32[16,1024]{1,0:T(8,128)S(1)}, f32[16,1024]{1,0:T(8,128)S(1)}, u32[]{:S(2)}, u32[]{:S(2)}) %collective-permute-start.4) | collective-permute-done | bytes 65568 | tf_op jit(solution)/shard_map/ppermute | solution.py:29
  69.5 0.7 broadcast_select_fusion.3
  70.2 2.9 %collective-permute-start.5 = (f32[16,1024]{1,0:T(8,128)}, f32[16,1024]{1,0:T(8,128)S(1)}, u32[]{:S(2)}, u32[]{:S(2)}) collective-permute-start(f32[16,1024]{1,0:T(8,128)} %get-tuple-element.30), channel_id=1, source_target_pairs={{0,1},{1,0},{2,3},{3,2},{4,5},{5,4},{6,7},{7,6},{8,9},{9,8},{10,11... | collective-permute-start | bytes 196616 | tf_op jit(solution)/shard_map/ppermute | solution.py:23
  73.3 0.7 reshape.14
  74.0 5.9 %hyena_near.1 = (f32[128,2048]{1,0:T(8,128)}, f32[128,2048]{1,0:T(8,128)}) custom-call(bf16[3,128,2048]{2,1,0:T(8,128)(2,1)} %bitcast.16, bf16[3,8,2048]{2,1,0:T(8,128)(2,1)} %copy-done.3, f32[3,3,2048]{2,1,0:T(4,128)} %w_ref.3, bf16[128,2048]{1,0:T(8,128)(2,1)} %get-tuple-element.16.mixed_ref, f32[16,1,128]{2,1,0:T(1,128)} %bitcast.18, f32[16,1,128]{2,1,0:T(1,128)} %bitcast.20), custom_call_target="tpu_custom_call" | custom-call | flops 536870912 | bytes 3145728 | tf_op jit(solution)/shard_map/hyena_near/pallas_call | solution.py:173
  79.9 8.5 %attend.1 = (f32[4,128,512]{2,1,0:T(8,128)S(1)}, f32[4,128,512]{2,1,0:T(8,128)S(1)}, f32[4,128,512]{2,1,0:T(8,128)S(1)}) custom-call(s32[8]{0:T(128)S(1)} %concatenate.8.info_ref, bf16[3,128,2048]{2,1,0:T(8,128)(2,1)S(1)} %bitcast.12, bf16[3,128,1024]{2,1,0:T(8,128)(2,1)S(1)} %collective-permute-done.6.theirs_ref.theirs, ...), custom_call_target="tpu_custom_call" | custom-call | flops 872415232 | bytes 3670016 | tf_op jit(solution)/shard_map/attend/pallas_call | solution.py:462
  88.4 4.0 %attend_last.1 = (bf16[128,512]{1,0:T(8,128)(2,1)S(1)}, bf16[128,512]{1,0:T(8,128)(2,1)S(1)}, bf16[128,512]{1,0:T(8,128)(2,1)S(1)}, bf16[128,512]{1,0:T(8,128)(2,1)S(1)}) custom-call(s32[8]{0:T(128)S(1)} %concatenate.8.info_ref, bf16[3,128,2048]{2,1,0:T(8,128)(2,1)S(1)} %bitcast.13, bf16[3,128,1024]{2,1,0:T(8,128)(2,1)S(1)} %collective-permute-done.6.theirs_ref.theirs, ...), custom_call_target="tpu_custom_call" | custom-call | flops 201326592 | bytes 3145728 | tf_op jit(solution)/shard_map/attend_last/pallas_call | solution.py:535
  92.8 1.7 %collective-permute-start.13 = (bf16[128,512]{1,0:T(8,128)(2,1)S(1)}, bf16[128,512]{1,0:T(8,128)(2,1)S(1)}, u32[]{:S(2)}, u32[]{:S(2)}) collective-permute-start(bf16[128,512]{1,0:T(8,128)(2,1)S(1)} %get-tuple-element.29), channel_id=1, source_target_pairs={{0,3},{1,2},{2,1},{3,0},{4,7},{5,6},{6,5},{7,4},{8,11},{9,10},{10,... | collective-permute-start | bytes 393224 | tf_op jit(solution)/shard_map/ppermute | solution.py:23
  94.6 0.7 pad_maximum_fusion.carried_ref
  95.2 4.0 %hyena_finish.1 = bf16[128,2048]{1,0:T(8,128)(2,1)} custom-call(f32[128,2048]{1,0:T(8,128)} %get-tuple-element.17.near_ref, f32[128,2048]{1,0:T(8,128)} %get-tuple-element.18.q_ref, f32[16,2048]{1,0:T(8,128)} %pad_maximum_fusion.carried_ref, f32[16,1,128]{2,1,0:T(1,128)} %bitcast.19, f32[16,1,128]{2,1,0:T(1,128)} %bitcast.21), custom_call_target="tpu_custom_call" | custom-call | flops 201326592 | bytes 2621440 | tf_op jit(solution)/shard_map/hyena_finish/pallas_call | solution.py:235
  99.2 1.3 %collective-permute-done.13.refs_3_ = bf16[128,512]{1,0:T(8,128)(2,1)S(1)} collective-permute-done((bf16[128,512]{1,0:T(8,128)(2,1)S(1)}, bf16[128,512]{1,0:T(8,128)(2,1)S(1)}, u32[]{:S(2)}, u32[]{:S(2)}) %collective-permute-start.13) | collective-permute-done | bytes 131104 | tf_op jit(solution)/shard_map/ppermute | solution.py:23
  100.5 1.4 %assemble.1 = bf16[128,2048]{1,0:T(8,128)(2,1)} custom-call(s32[4]{0:T(128)S(1)} %pad_add_fusion.at_ref, bf16[128,512]{1,0:T(8,128)(2,1)S(1)} %get-tuple-element.26.refs_0_, bf16[128,512]{1,0:T(8,128)(2,1)S(1)} %collective-permute-done.11.refs_1_, bf16[128,512]{1,0:T(8,128)(2,1)S(1)} %collective-permute-done.12.refs_2_, ...), custom_call_target="tpu_custom_call" | custom-call | bytes 1048576 | tf_op jit(solution)/shard_map/assemble/pallas_call | solution.py:563
  (46 shorter events, 2.8 us)
Async XLA Ops:
  0.7 1.4 %copy-start = (bf16[128,3,2048]{2,0,1:T(8,128)(2,1)S(1)}, bf16[128,3,2048]{2,0,1:T(8,128)(2,1)}, u32[]{:S(2)}) copy-start(bf16[128,3,2048]{2,0,1:T(8,128)(2,1)} %param.10) | copy-start | bytes 4718596
  2.1 5.6 %copy-start.10 = (f32[128,16]{0,1:T(8,128)S(1)}, f32[128,16]{0,1:T(8,128)}, u32[]{:S(2)}) copy-start(f32[128,16]{0,1:T(8,128)} %param.8) | copy-start | bytes 24580
  2.1 14.5 %collective-permute-start.6 = (bf16[3,128,1024]{2,1,0:T(8,128)(2,1)S(1)}, bf16[3,128,1024]{2,1,0:T(8,128)(2,1)S(1)}, u32[]{:S(2)}, u32[]{:S(2)}) collective-permute-start(bf16[3,128,1024]{2,1,0:T(8,128)(2,1)S(1)} %halve.1), channel_id=1, source_target_pairs={{0,1},{1,0},{2,3},{3,2},{4,5},{5,4},{6,7},{7,6},{8,9},{9,8},{10,11... | collective-permute-start | bytes 2359304 | tf_op jit(solution)/shard_map/ppermute | solution.py:23
  2.9 13.7 %copy-start.1 = (bf16[128,3,2048]{2,0,1:T(8,128)(2,1)S(1)}, bf16[128,3,2048]{2,0,1:T(8,128)(2,1)}, u32[]{:S(2)}) copy-start(bf16[128,3,2048]{2,0,1:T(8,128)(2,1)} %param.10) | copy-start | bytes 4718596
  4.6 5.0 %collective-permute-start = (bf16[3,8,2048]{2,1,0:T(8,128)(2,1)}, bf16[3,8,2048]{2,1,0:T(8,128)(2,1)S(1)}, u32[]{:S(2)}, u32[]{:S(2)}) collective-permute-start(bf16[3,8,2048]{2,1,0:T(8,128)(2,1)} %last_rows.1), channel_id=1, source_target_pairs={{0,1},{1,2},{2,3},{3,4},{4,5},{5,6},{6,7},{7,8},{8,9},{9,10},{10,1... | collective-permute-start | bytes 294920 | tf_op jit(solution)/shard_map/ppermute | solution.py:29
  9.6 0.6 copy-start.3
  14.4 11.6 %copy-start.2 = (f32[16,2048]{1,0:T(8,128)S(1)}, f32[16,2048]{1,0:T(8,128)}, u32[]{:S(2)}) copy-start(f32[16,2048]{1,0:T(8,128)} %get-tuple-element.19) | copy-start | bytes 393220
  14.4 11.6 %copy-start.4 = (f32[16,2048]{1,0:T(8,128)S(1)}, f32[16,2048]{1,0:T(8,128)}, u32[]{:S(2)}) copy-start(f32[16,2048]{1,0:T(8,128)} %get-tuple-element.20) | copy-start | bytes 393220
  15.3 10.1 %collective-permute-start.1 = (f32[16,1024]{1,0:T(8,128)S(1)}, f32[16,1024]{1,0:T(8,128)S(1)}, u32[]{:S(2)}, u32[]{:S(2)}) collective-permute-start(f32[16,1024]{1,0:T(8,128)S(1)} %constant_dynamic-slice_fusion), channel_id=1, source_target_pairs={{0,1},{1,0},{2,3},{3,2},{4,5},{5,4},{6,7},{7,6},{8,9},{9,8},{10,11... | collective-permute-start | bytes 196616 | tf_op jit(solution)/shard_map/ppermute | solution.py:23
  18.2 15.7 %collective-permute-start.8 = (bf16[2,2,128,512]{3,2,1,0:T(8,128)(2,1)}, bf16[2,2,128,512]{3,2,1,0:T(8,128)(2,1)}, u32[]{:S(2)}, u32[]{:S(2)}) collective-permute-start(bf16[2,2,128,512]{3,2,1,0:T(8,128)(2,1)} %get-tuple-element.21), channel_id=1, source_target_pairs={{0,4},{1,5},{2,6},{3,7},{4,8},{5,9},{6,10},{7,11},{8,12},{9,13},{1... | collective-permute-start | bytes 1572872 | tf_op jit(solution)/shard_map/ppermute | solution.py:29
  21.4 24.6 %collective-permute-start.9 = (bf16[2,2,128,512]{3,2,1,0:T(8,128)(2,1)}, bf16[2,2,128,512]{3,2,1,0:T(8,128)(2,1)}, u32[]{:S(2)}, u32[]{:S(2)}) collective-permute-start(bf16[2,2,128,512]{3,2,1,0:T(8,128)(2,1)} %get-tuple-element.22), channel_id=1, source_target_pairs={{0,6},{1,7},{2,4},{3,5},{4,10},{5,11},{6,8},{7,9},{8,14},{9,15},{1... | collective-permute-start | bytes 1572872 | tf_op jit(solution)/shard_map/ppermute | solution.py:29
  25.5 0.6 copy-start.6
  26.1 3.6 %collective-permute-start.2 = (f32[16,1024]{1,0:T(8,128)S(1)}, f32[16,1024]{1,0:T(8,128)S(1)}, u32[]{:S(2)}, u32[]{:S(2)}) collective-permute-start(f32[16,1024]{1,0:T(8,128)S(1)} %select_add_fusion.1), channel_id=1, source_target_pairs={{0,2},{1,3},{2,0},{3,1},{4,6},{5,7},{6,4},{7,5},{8,10},{9,11},{10,... | collective-permute-start | bytes 196616 | tf_op jit(solution)/shard_map/ppermute | solution.py:23
  29.7 2.0 %copy-start.8 = (f32[16,1024]{1,0:T(8,128)}, f32[16,1024]{1,0:T(8,128)S(1)}, u32[]{:S(2)}) copy-start(f32[16,1024]{1,0:T(8,128)S(1)} %collective-permute-done.2) | copy-start | bytes 196612
  29.7 21.9 %collective-permute-start.3 = (f32[16,1024]{1,0:T(8,128)S(1)}, f32[16,1024]{1,0:T(8,128)S(1)}, u32[]{:S(2)}, u32[]{:S(2)}) collective-permute-start(f32[16,1024]{1,0:T(8,128)S(1)} %select_add_fusion), channel_id=1, source_target_pairs={{0,4},{1,5},{2,6},{3,7},{4,8},{5,9},{6,10},{7,11},{8,12},{9,13},{1... | collective-permute-start | bytes 196616 | tf_op jit(solution)/shard_map/ppermute | solution.py:29
  33.1 36.4 %copy-start.7 = (f32[16,1024]{1,0:T(8,128)S(1)}, f32[16,1024]{1,0:T(8,128)}, u32[]{:S(2)}) copy-start(f32[16,1024]{1,0:T(8,128)} %copy-done.6) | copy-start | bytes 196612
  33.1 36.4 %copy-start.9 = (f32[16,1024]{1,0:T(8,128)S(1)}, f32[16,1024]{1,0:T(8,128)}, u32[]{:S(2)}) copy-start(f32[16,1024]{1,0:T(8,128)} %copy-done.8) | copy-start | bytes 196612
  33.1 40.0 %copy-start.12 = (s32[4]{0:T(128)S(1)}, s32[4]{0:T(128)}, u32[]{:S(2)}) copy-start(s32[4]{0:T(128)} %param.11) | copy-start | bytes 52
  33.1 40.0 %copy-start.11 = (f32[128,16]{0,1:T(8,128)S(1)}, f32[128,16]{0,1:T(8,128)}, u32[]{:S(2)}) copy-start(f32[128,16]{0,1:T(8,128)} %param.9) | copy-start | bytes 24580
  33.2 46.7 %collective-permute-start.7 = (bf16[2,3,128,512]{3,2,1,0:T(8,128)(2,1)}, bf16[2,3,128,512]{3,2,1,0:T(8,128)(2,1)S(1)}, u32[]{:S(2)}, u32[]{:S(2)}) collective-permute-start(bf16[2,3,128,512]{3,2,1,0:T(8,128)(2,1)} %pack.2), channel_id=1, source_target_pairs={{0,2},{1,3},{2,0},{3,1},{4,6},{5,7},{6,4},{7,5},{8,10},{9,11},{10,... | collective-permute-start | bytes 2359304 | tf_op jit(solution)/shard_map/ppermute | solution.py:23
  48.4 39.9 %collective-permute-start.10 = (bf16[3,2,128,512]{3,2,1,0:T(8,128)(2,1)}, bf16[3,2,128,512]{3,2,1,0:T(8,128)(2,1)}, u32[]{:S(2)}, u32[]{:S(2)}) collective-permute-start(bf16[3,2,128,512]{3,2,1,0:T(8,128)(2,1)} %onward.1), channel_id=1, source_target_pairs={{0,4},{1,5},{2,6},{3,7},{4,8},{5,9},{6,10},{7,11},{8,12},{9,13},{1... | collective-permute-start | bytes 2359304 | tf_op jit(solution)/shard_map/ppermute | solution.py:29
  51.7 17.8 %collective-permute-start.4 = (f32[16,1024]{1,0:T(8,128)S(1)}, f32[16,1024]{1,0:T(8,128)S(1)}, u32[]{:S(2)}, u32[]{:S(2)}) collective-permute-start(f32[16,1024]{1,0:T(8,128)S(1)} %multiply_add_fusion.1), channel_id=1, source_target_pairs={{0,8},{1,9},{2,10},{3,11},{4,12},{5,13},{6,14},{7,15},{16,24},{17,... | collective-permute-start | bytes 196616 | tf_op jit(solution)/shard_map/ppermute | solution.py:29
  70.2 9.6 %copy-start.5 = (f32[16,1024]{1,0:T(8,128)S(1)}, f32[16,1024]{1,0:T(8,128)}, u32[]{:S(2)}) copy-start(f32[16,1024]{1,0:T(8,128)} %get-tuple-element.32) | copy-start | bytes 196612
  70.2 9.6 %collective-permute-start.5 = (f32[16,1024]{1,0:T(8,128)}, f32[16,1024]{1,0:T(8,128)S(1)}, u32[]{:S(2)}, u32[]{:S(2)}) collective-permute-start(f32[16,1024]{1,0:T(8,128)} %get-tuple-element.30), channel_id=1, source_target_pairs={{0,1},{1,0},{2,3},{3,2},{4,5},{5,4},{6,7},{7,6},{8,9},{9,8},{10,11... | collective-permute-start | bytes 196616 | tf_op jit(solution)/shard_map/ppermute | solution.py:23
  92.3 6.9 %collective-permute-start.11 = (bf16[128,512]{1,0:T(8,128)(2,1)S(1)}, bf16[128,512]{1,0:T(8,128)(2,1)S(1)}, u32[]{:S(2)}, u32[]{:S(2)}) collective-permute-start(bf16[128,512]{1,0:T(8,128)(2,1)S(1)} %get-tuple-element.27), channel_id=1, source_target_pairs={{0,1},{1,0},{2,3},{3,2},{4,5},{5,4},{6,7},{7,6},{8,9},{9,8},{10,11... | collective-permute-start | bytes 393224 | tf_op jit(solution)/shard_map/ppermute | solution.py:23
  92.4 6.8 %collective-permute-start.12 = (bf16[128,512]{1,0:T(8,128)(2,1)S(1)}, bf16[128,512]{1,0:T(8,128)(2,1)S(1)}, u32[]{:S(2)}, u32[]{:S(2)}) collective-permute-start(bf16[128,512]{1,0:T(8,128)(2,1)S(1)} %get-tuple-element.28), channel_id=1, source_target_pairs={{0,2},{1,3},{2,0},{3,1},{4,6},{5,7},{6,4},{7,5},{8,10},{9,11},{10,... | collective-permute-start | bytes 393224 | tf_op jit(solution)/shard_map/ppermute | solution.py:23
  92.8 7.7 %collective-permute-start.13 = (bf16[128,512]{1,0:T(8,128)(2,1)S(1)}, bf16[128,512]{1,0:T(8,128)(2,1)S(1)}, u32[]{:S(2)}, u32[]{:S(2)}) collective-permute-start(bf16[128,512]{1,0:T(8,128)(2,1)S(1)} %get-tuple-element.29), channel_id=1, source_target_pairs={{0,3},{1,2},{2,1},{3,0},{4,7},{5,6},{6,5},{7,4},{8,11},{9,10},{10,... | collective-permute-start | bytes 393224 | tf_op jit(solution)/shard_map/ppermute | solution.py:23

commit v5 on v3

--- a/solution.py
+++ b/solution.py
@@ -23,9 +23,9 @@
     return lax.ppermute(value, axis, [(at, at ^ bit) for at in range(count)])
 
 
-def ahead(value, axis, steps, bit=0):
+def ahead(value, axis, steps, bit=0, first=0):
     count = lax.axis_size(axis)
-    pairs = [(at, (at + steps) ^ bit) for at in range(count - steps)]
+    pairs = [(at, (at + steps) ^ bit) for at in range(first, count - steps)]
     return lax.ppermute(value, axis, pairs)
 
 
@@ -193,7 +193,7 @@
             pltpu.VMEM((parts, rows, filters * rows), BF16),
             pltpu.VMEM((parts, filters * rows, lanes), BF16),
         ],
-        compiler_params=limits(16),
+        compiler_params=limits(58),
         cost_estimate=cost(2 * rows * rows * filters * channels, 12 * rows * channels),
         name="hyena_near",
     )(streams, halo, short_weight, mixed, rate_rows, res_rows)
@@ -244,7 +244,7 @@
         ],
         out_specs=pl.BlockSpec((rows, wide), by_block),
         out_shape=jax.ShapeDtypeStruct((rows, channels), BF16),
-        compiler_params=limits(16),
+        compiler_params=limits(58),
         cost_estimate=cost(6 * rows * terms * channels, 10 * rows * channels),
         name="hyena_finish",
     )(near, query, carried, rate_rows, res_rows)
@@ -286,27 +286,35 @@
     return pl.ds(pl.multiple_of(start * size, size), size)
 
 
-def halve_body(at_ref, streams_ref, out_ref):
-    del at_ref
-    out_ref[...] = streams_ref[...]
-
-
-def halve(which, streams):
-    count, rows, channels = streams.shape
-    half = channels // 2
-    return pl.pallas_call(
-        halve_body,
-        grid_spec=pltpu.PrefetchScalarGridSpec(
-            num_scalar_prefetch=1,
-            grid=(1,),
-            in_specs=[pl.BlockSpec((count, rows, half), lambda n, at: (0, 0, at[0]))],
-            out_specs=pl.BlockSpec((count, rows, half), lambda n, at: (0, 0, 0)),
-        ),
-        out_shape=jax.ShapeDtypeStruct((count, rows, half), streams.dtype),
-        compiler_params=limits(8),
-        cost_estimate=cost(0, 4 * count * rows * half),
-        name="halve",
-    )(which, streams)
+def front_body(at_ref, attn, hyena, theirs_ref, edge_ref, sems):
+    rows, half = theirs_ref.shape[1:]
+    away = attn.at[:, :, lanes_from(1 - at_ref[0], half)]
+    edge = hyena.at[:, rows - EDGE : rows, :]
+    copies = [
+        pltpu.make_async_copy(away, theirs_ref, sems.at[0]),
+        pltpu.make_async_copy(edge, edge_ref, sems.at[1]),
+    ]
+    for copy in copies:
+        copy.start()
+    for copy in copies:
+        copy.wait()
+
+
+def front(where, attn, hyena):
+    count, rows, channels = attn.shape
+    return pl.pallas_call(
+        front_body,
+        in_specs=[SMEM, ANY, ANY],
+        out_specs=[VMEM, VMEM],
+        out_shape=[
+            jax.ShapeDtypeStruct((count, rows, channels // 2), attn.dtype),
+            jax.ShapeDtypeStruct((count, EDGE, channels), hyena.dtype),
+        ],
+        scratch_shapes=[pltpu.SemaphoreType.DMA((2,))],
+        compiler_params=limits(58),
+        cost_estimate=cost(0, 4 * count * rows * channels // 2),
+        name="front",
+    )(where, attn, hyena)
 
 
 def pack_body(first, at_ref, streams_ref, theirs_ref, *outs):
@@ -331,32 +339,6 @@
         cost_estimate=cost(0, 8 * amount * rows * half),
         name="pack",
     )(where, streams, theirs)
-
-
-def onward_body(at_ref, own_ref, cross_ref, out_ref):
-    place = at_ref[2]
-    for block in range(1, ROW):
-        slot = place ^ block
-
-        @pl.when(slot < 2)
-        def _():
-            out_ref[block - 1] = own_ref[slot]
-
-        @pl.when(slot >= 2)
-        def _():
-            out_ref[block - 1] = cross_ref[slot - 2]
-
-
-def onward(where, own, cross):
-    return pl.pallas_call(
-        onward_body,
-        in_specs=[SMEM, VMEM, VMEM],
-        out_specs=VMEM,
-        out_shape=jax.ShapeDtypeStruct((ROW - 1,) + own.shape[1:], BF16),
-        compiler_params=limits(6),
-        cost_estimate=cost(0, 4 * own.size),
-        name="onward",
-    )(where, own, cross)
 
 
 FIXED = 4
@@ -423,8 +405,8 @@
             scores = jnp.where(allowed, scores, -jnp.inf)
             top = jnp.max(scores, axis=1, keepdims=True)
             weight = jnp.exp2((scores - top) * SCALE)
-            m_ref[block, :, head : head + 1] = top
-            l_ref[block, :, head : head + 1] = jnp.sum(weight, axis=1, keepdims=True)
+            m_ref[block, :, lanes] = jnp.broadcast_to(top, (rows, HEAD))
+            l_ref[block, :, lanes] = jnp.broadcast_to(jnp.sum(weight, axis=1, keepdims=True), (rows, HEAD))
             acc_ref[block, :, lanes] = jnp.dot(
                 weight.astype(BF16), v_s[0:width, lanes], preferred_element_type=F32
             )
@@ -439,9 +421,8 @@
         out_specs=[VMEM] * 3,
         out_shape=[
             jax.ShapeDtypeStruct((ROW, rows, quarter), F32),
-            jax.ShapeDtypeStruct((ROW, rows, heads), F32),
-            jax.ShapeDtypeStruct((ROW, rows, heads), F32),
-        ],
+        ]
+        * 3,
         scratch_shapes=[
             pltpu.VMEM((ROW, rows, quarter), BF16),
             pltpu.VMEM((2 * ROW * rows, quarter), BF16),
@@ -455,15 +436,20 @@
 
 
 def attend_last_body(
-    docs, info_ref, streams, theirs, swap, oldest, acc_ref, m_ref, l_ref, out0, out1, out2, out3, q_s, o_s, sems
+    docs, info_ref, streams, theirs, swap, own, cross, acc_ref, m_ref, l_ref, out0, out1, out2, out3, q_s, kv_s, o_s, sems
 ):
     place, base = info_ref[2], info_ref[3]
     rows, quarter = q_s.shape[1:]
     copies = []
+
+    def bring(source, target):
+        copies.append(pltpu.make_async_copy(source, target, sems.at[len(copies)]))
+        copies[-1].start()
+
     for slot in range(ROW):
-        part = row_part(info_ref, streams, theirs, swap, slot, 0, quarter)
-        copies.append(pltpu.make_async_copy(part, q_s.at[place ^ slot], sems.at[slot]))
-        copies[-1].start()
+        block = place ^ slot
+        bring(row_part(info_ref, streams, theirs, swap, slot, 0, quarter), q_s.at[block])
+        bring(own.at[slot] if slot < 2 else cross.at[slot - 2], kv_s.at[block])
     for copy in copies:
         copy.wait()
     for block in range(ROW):
@@ -478,10 +464,10 @@
         for head in range(quarter // HEAD):
             lanes = slice(head * HEAD, (head + 1) * HEAD)
             total = acc_ref[block, :, lanes]
-            below = l_ref[block, :, head : head + 1]
+            below = l_ref[block, :, lanes]
             if seen:
-                keys = oldest[block : ROW - 1, 0, :, lanes].reshape(width, HEAD)
-                values = oldest[block : ROW - 1, 1, :, lanes].reshape(width, HEAD)
+                keys = kv_s[block + 1 : ROW, 0, :, lanes].reshape(width, HEAD)
+                values = kv_s[block + 1 : ROW, 1, :, lanes].reshape(width, HEAD)
                 scores = lax.dot_general(
                     q_s[block, :, lanes],
                     keys,
@@ -489,10 +475,10 @@
                     preferred_element_type=F32,
                 )
                 scores = jnp.where(allowed, scores, -jnp.inf)
-                past = m_ref[block, :, head : head + 1]
+                past = m_ref[block, :, lanes]
                 top = jnp.maximum(past, jnp.max(scores, axis=1, keepdims=True))
                 fade = jnp.exp2((past - top) * SCALE)
-                weight = jnp.exp2((scores - top) * SCALE)
+                weight = jnp.exp2((scores - jnp.concatenate([top] * seen, axis=1)) * SCALE)
                 share = 1.0 / (below * fade + jnp.sum(weight, axis=1, keepdims=True))
                 total = total * (fade * share) + share * jnp.dot(
                     weight.astype(BF16), values, preferred_element_type=F32
@@ -504,23 +490,24 @@
         out[...] = o_s[slot]
 
 
-def attend_last(info, docs, streams, theirs, swap, oldest, acc, top, below):
+def attend_last(info, docs, streams, theirs, swap, own, cross, acc, top, below):
     _, rows, quarter = acc.shape
     heads = quarter // HEAD
     return pl.pallas_call(
         functools.partial(attend_last_body, docs),
-        in_specs=[SMEM] + [ANY] * 3 + [VMEM] * 4,
+        in_specs=[SMEM] + [ANY] * 5 + [VMEM] * 3,
         out_specs=[VMEM] * ROW,
         out_shape=[jax.ShapeDtypeStruct((rows, quarter), BF16)] * ROW,
         scratch_shapes=[
             pltpu.VMEM((ROW, rows, quarter), BF16),
+            pltpu.VMEM((ROW, 2, rows, quarter), BF16),
             pltpu.VMEM((ROW, rows, quarter), BF16),
-            pltpu.SemaphoreType.DMA((ROW,)),
+            pltpu.SemaphoreType.DMA((2 * ROW,)),
         ],
         compiler_params=limits(16),
         cost_estimate=cost(6 * 4 * rows * rows * quarter, 12 * ROW * rows * quarter, 6 * heads * rows * rows),
         name="attend_last",
-    )(info, streams, theirs, swap, oldest, acc, top, below)
+    )(info, streams, theirs, swap, own, cross, acc, top, below)
 
 
 def assemble_body(at_ref, *refs):
@@ -556,28 +543,31 @@
     fixed = jnp.stack([core, side, place, (index - place) * rows]).astype(jnp.int32)
     info = jnp.concatenate([fixed, doc_lengths])
 
-    edge = ahead(hyena_qkv[rows - EDGE :], "ctx", 1)
-
+    inner = hyena_qkv.transpose(1, 0, 2)
     streams = attn_qkv.transpose(1, 0, 2)
-    theirs = flip(halve((1 - core).reshape(1).astype(jnp.int32), streams), "ctx", 1)
+    theirs, edge = front(fixed, streams, inner)
+
+    theirs = flip(theirs, "ctx", 1)
+    edge = ahead(edge, "ctx", 1)
     own, cross = pack(fixed, streams, theirs, 1, 2)
+    cross = ahead(cross, "ctx", ROW, 2)
     own = ahead(own, "ctx", ROW)
-    cross = ahead(cross, "ctx", ROW, 2)
     (swap,) = pack(fixed, streams, theirs, 0, 1)
     swap = flip(swap, "ctx", 2)
-    oldest = ahead(onward(fixed, own, cross), "ctx", ROW)
+    older_cross = ahead(cross, "ctx", ROW, 0, ROW)
+    older_own = ahead(own, "ctx", ROW, 0, ROW)
 
     blocks = channels // LANES
+    edge, filter_rate, filter_residue = lax.optimization_barrier((edge, filter_rate, filter_residue))
     rate_rows = filter_rate.reshape(blocks, 1, -1)
     res_rows = filter_residue.reshape(blocks, 1, -1)
-    inner, edge = hyena_qkv.transpose(1, 0, 2), edge.transpose(1, 0, 2)
     mixed, ends, wide = hyena_ends(inner, edge, short_weight, rate_rows, modes)
     near, query = hyena_near(inner, edge, short_weight, mixed, rate_rows, res_rows, modes)
     carried = scan_states(ends, wide, rows)
     hyena_out = hyena_finish(near, query, carried, rate_rows, res_rows, modes)
 
     acc, top, below = attend(info, docs, streams, theirs, swap, own, cross)
-    made = attend_last(info, docs, streams, theirs, swap, oldest, acc, top, below)
+    made = attend_last(info, docs, streams, theirs, swap, older_own, older_cross, acc, top, below)
     pieces = [made[0]] + [flip(made[n], "ctx", n) for n in range(1, ROW)]
     attn_out = assemble(fixed, pieces)
     return (hyena_out, attn_out)

time: 107 us -> 93.7 us (0.88)
  the two profiles are of different devices: /device:TPU:15 before, /device:TPU:19 now
where the time goes in v5:
time: 93.7 us; the launch traced here: 93 us
  Pallas kernels  31.4 us (34%)
  waiting for transfers between devices  28.2 us (30%)
  starting transfers between devices  26.5 us (28%)
  local copies, waits for them, and re-layouts  3.11 us (3%)
  other arithmetic  2.89 us (3%)
  between operations  1.01 us (1%)
    ppermute x7, waiting for transfers between devices, ahead(): return lax.ppermute(value, axis, pairs)  25.6 us
    ppermute x7, starting transfers between devices, ahead(): return lax.ppermute(value, axis, pairs)  17.6 us
    ppermute x8, starting transfers between devices, flip(): return lax.ppermute(value, axis, [(at, at ^ bit) for at in range(count)])  8.85 us
    pallas_call x1, Pallas kernels, attend(): pl.pallas_call(functools.partial(attend_body, docs), in_specs=[SMEM] + [A...  8.43 us
    pallas_call x1, Pallas kernels, hyena_near(): pl.pallas_call(functools.partial(hyena_near_body, modes), grid=(STEPS,),...  5.85 us
    pallas_call x1, Pallas kernels, attend_last(): pl.pallas_call(functools.partial(attend_last_body, docs), in_specs=[SMEM]...  4.36 us
    pallas_call x1, Pallas kernels, hyena_finish(): pl.pallas_call(functools.partial(hyena_out_body, modes), grid=(STEPS,), i...  4.01 us
    pallas_call x1, Pallas kernels, front(): pl.pallas_call(front_body, in_specs=[SMEM, ANY, ANY], out_specs=[VMEM, VM...  2.85 us
  transfers between devices with their start and end apart: 15, of which 5 were waited for; matrix products, arithmetic and copies ran while one was open for 4% of the time, Pallas kernels for 25%

profile of v5, /device:TPU:19, one launch (start us, length us, event | category | flops | bytes accessed | tf_op | source)
XLA Modules:
  0.0 93.0 jit_solution(1641071939309414494)
XLA Ops:
  1.3 2.8 %front.1 = (bf16[3,128,1024]{2,1,0:T(8,128)(2,1)}, bf16[3,8,2048]{2,1,0:T(8,128)(2,1)}) custom-call(s32[4]{0:T(128)} %pad_add_fusion.at_ref, bf16[3,128,2048]{2,1,0:T(8,128)(2,1)} %bitcast.8, bf16[3,128,2048]{2,1,0:T(8,128)(2,1)} %bitcast.13), custom_call_target="tpu_custom_call" | custom-call | bytes 1572864 | tf_op jit(solution)/shard_map/front/pallas_call | solution.py:305
  4.1 0.7 collective-permute-start.6
  4.9 3.2 %collective-permute-start = (bf16[3,8,2048]{2,1,0:T(8,128)(2,1)}, bf16[3,8,2048]{2,1,0:T(8,128)(2,1)S(1)}, u32[]{:S(2)}, u32[]{:S(2)}) collective-permute-start(bf16[3,8,2048]{2,1,0:T(8,128)(2,1)} %get-tuple-element.21), channel_id=1, source_target_pairs={{0,1},{1,2},{2,3},{3,4},{4,5},{5,6},{6,7},{7,8},{8,9},{9,10},{10,1... | collective-permute-start | bytes 294920 | tf_op jit(solution)/shard_map/ppermute | solution.py:29
  8.1 1.9 %collective-permute-done.halo_ref = bf16[3,8,2048]{2,1,0:T(8,128)(2,1)S(1)} collective-permute-done((bf16[3,8,2048]{2,1,0:T(8,128)(2,1)}, bf16[3,8,2048]{2,1,0:T(8,128)(2,1)S(1)}, u32[]{:S(2)}, u32[]{:S(2)}) %collective-permute-start) | collective-permute-done | bytes 98336 | tf_op jit(solution)/shard_map/ppermute | solution.py:29
  10.2 2.1 %hyena_ends.1 = (bf16[128,2048]{1,0:T(8,128)(2,1)S(1)}, f32[16,2048]{1,0:T(8,128)S(1)}, f32[16,2048]{1,0:T(8,128)S(1)}) custom-call(bf16[3,128,2048]{2,1,0:T(8,128)(2,1)S(1)} %bitcast.15, bf16[3,8,2048]{2,1,0:T(8,128)(2,1)S(1)} %collective-permute-done.halo_ref, f32[3,3,2048]{2,1,0:T(4,128)S(1)} %copy-done.3, f32[16,1,128]{2,1,0:T(1,128)S(1)} %bitcast.16), custom_call_target="tpu_custom_call" | custom-call | flops 134217728 | bytes 2097152 | tf_op jit(solution)/shard_map/hyena_ends/pallas_call | solution.py:108
  12.3 0.8 copy-done.2
  13.1 0.7 copy-done.5
  13.7 2.1 %collective-permute-start.1 = (f32[16,1024]{1,0:T(8,128)S(1)}, f32[16,1024]{1,0:T(8,128)S(1)}, u32[]{:S(2)}, u32[]{:S(2)}) collective-permute-start(f32[16,1024]{1,0:T(8,128)S(1)} %constant_dynamic-slice_fusion), channel_id=1, source_target_pairs={{0,1},{1,0},{2,3},{3,2},{4,5},{5,4},{6,7},{7,6},{8,9},{9,8},{10,11... | collective-permute-start | bytes 196616 | tf_op jit(solution)/shard_map/ppermute | solution.py:23
  15.8 0.9 collective-permute-done.1
  16.7 0.9 select_add_fusion.1
  18.0 1.2 %pack.3 = (bf16[2,2,128,512]{3,2,1,0:T(8,128)(2,1)S(1)}, bf16[2,2,128,512]{3,2,1,0:T(8,128)(2,1)S(1)}) custom-call(s32[4]{0:T(128)S(1)} %copy-done.8, bf16[3,128,2048]{2,1,0:T(8,128)(2,1)S(1)} %bitcast.9, bf16[3,128,1024]{2,1,0:T(8,128)(2,1)} %collective-permute-done.6.theirs_ref.theirs), custom_call_target="tpu_custom_call" | custom-call | bytes 2097152 | tf_op jit(solution)/shard_map/pack/pallas_call | solution.py:333
  19.3 4.0 %collective-permute-start.10 = (bf16[2,2,128,512]{3,2,1,0:T(8,128)(2,1)S(1)}, bf16[2,2,128,512]{3,2,1,0:T(8,128)(2,1)}, u32[]{:S(2)}, u32[]{:S(2)}) collective-permute-start(bf16[2,2,128,512]{3,2,1,0:T(8,128)(2,1)S(1)} %get-tuple-element.32), channel_id=1, source_target_pairs={{0,6},{1,7},{2,4},{3,5},{4,10},{5,11},{6,8},{7,9},{8,14},{9,15},{1... | collective-permute-start | bytes 1572872 | tf_op jit(solution)/shard_map/ppermute | solution.py:29
  23.3 1.9 %collective-permute-start.8 = (bf16[2,2,128,512]{3,2,1,0:T(8,128)(2,1)S(1)}, bf16[2,2,128,512]{3,2,1,0:T(8,128)(2,1)}, u32[]{:S(2)}, u32[]{:S(2)}) collective-permute-start(bf16[2,2,128,512]{3,2,1,0:T(8,128)(2,1)S(1)} %get-tuple-element.31), channel_id=1, source_target_pairs={{0,4},{1,5},{2,6},{3,7},{4,8},{5,9},{6,10},{7,11},{8,12},{9,13},{1... | collective-permute-start | bytes 1572872 | tf_op jit(solution)/shard_map/ppermute | solution.py:29
  25.9 2.0 %collective-permute-start.3 = (f32[16,1024]{1,0:T(8,128)S(1)}, f32[16,1024]{1,0:T(8,128)S(1)}, u32[]{:S(2)}, u32[]{:S(2)}) collective-permute-start(f32[16,1024]{1,0:T(8,128)S(1)} %select_add_fusion), channel_id=1, source_target_pairs={{0,4},{1,5},{2,6},{3,7},{4,8},{5,9},{6,10},{7,11},{8,12},{9,13},{1... | collective-permute-start | bytes 196616 | tf_op jit(solution)/shard_map/ppermute | solution.py:29
  28.0 1.2 %pack.2 = bf16[2,3,128,512]{3,2,1,0:T(8,128)(2,1)S(1)} custom-call(s32[4]{0:T(128)S(1)} %copy-done.8, bf16[3,128,2048]{2,1,0:T(8,128)(2,1)S(1)} %bitcast.10, bf16[3,128,1024]{2,1,0:T(8,128)(2,1)} %collective-permute-done.6.theirs_ref.theirs), custom_call_target="tpu_custom_call" | custom-call | bytes 1048576 | tf_op jit(solution)/shard_map/pack/pallas_call | solution.py:333
  29.6 18.0 %collective-permute-done.3 = f32[16,1024]{1,0:T(8,128)S(1)} collective-permute-done((f32[16,1024]{1,0:T(8,128)S(1)}, f32[16,1024]{1,0:T(8,128)S(1)}, u32[]{:S(2)}, u32[]{:S(2)}) %collective-permute-start.3) | collective-permute-done | bytes 65568 | tf_op jit(solution)/shard_map/ppermute | solution.py:29
  47.7 1.3 %collective-permute-start.4 = (f32[16,1024]{1,0:T(8,128)S(1)}, f32[16,1024]{1,0:T(8,128)S(1)}, u32[]{:S(2)}, u32[]{:S(2)}) collective-permute-start(f32[16,1024]{1,0:T(8,128)S(1)} %multiply_add_fusion.1), channel_id=1, source_target_pairs={{0,8},{1,9},{2,10},{3,11},{4,12},{5,13},{6,14},{7,15},{16,24},{17,... | collective-permute-start | bytes 196616 | tf_op jit(solution)/shard_map/ppermute | solution.py:29
  49.0 3.2 %collective-permute-start.11 = (bf16[2,2,128,512]{3,2,1,0:T(8,128)(2,1)}, bf16[2,2,128,512]{3,2,1,0:T(8,128)(2,1)}, u32[]{:S(2)}, u32[]{:S(2)}) collective-permute-start(bf16[2,2,128,512]{3,2,1,0:T(8,128)(2,1)} %collective-permute-done.10.cross), channel_id=1, source_target_pairs={{4,8},{5,9},{6,10},{7,11},{8,12},{9,13},{10,14},{11,15},{20,24},{2... | collective-permute-start | bytes 1572872 | tf_op jit(solution)/shard_map/ppermute | solution.py:29
  52.2 1.9 %collective-permute-start.9 = (bf16[2,2,128,512]{3,2,1,0:T(8,128)(2,1)}, bf16[2,2,128,512]{3,2,1,0:T(8,128)(2,1)}, u32[]{:S(2)}, u32[]{:S(2)}) collective-permute-start(bf16[2,2,128,512]{3,2,1,0:T(8,128)(2,1)} %collective-permute-done.8.own), channel_id=1, source_target_pairs={{4,8},{5,9},{6,10},{7,11},{8,12},{9,13},{10,14},{11,15},{20,24},{2... | collective-permute-start | bytes 1572872 | tf_op jit(solution)/shard_map/ppermute | solution.py:29
  54.2 0.7 broadcast_select_fusion.3
  54.9 2.1 %collective-permute-start.5 = (f32[16,1024]{1,0:T(8,128)}, f32[16,1024]{1,0:T(8,128)S(1)}, u32[]{:S(2)}, u32[]{:S(2)}) collective-permute-start(f32[16,1024]{1,0:T(8,128)} %get-tuple-element.40), channel_id=1, source_target_pairs={{0,1},{1,0},{2,3},{3,2},{4,5},{5,4},{6,7},{7,6},{8,9},{9,8},{10,11... | collective-permute-start | bytes 196616 | tf_op jit(solution)/shard_map/ppermute | solution.py:23
  57.1 0.7 reshape.11
  57.8 5.9 %hyena_near.1 = (f32[128,2048]{1,0:T(8,128)}, f32[128,2048]{1,0:T(8,128)}) custom-call(bf16[3,128,2048]{2,1,0:T(8,128)(2,1)} %bitcast.14, bf16[3,8,2048]{2,1,0:T(8,128)(2,1)} %copy-done.4, f32[3,3,2048]{2,1,0:T(4,128)} %w_ref.3, bf16[128,2048]{1,0:T(8,128)(2,1)} %copy-done.2, f32[16,1,128]{2,1,0:T(1,128)} %bitcast.17, f32[16,1,128]{2,1,0:T(1,128)} %bitcast.19), custom_call_target="tpu_custom_call" | custom-call | flops 536870912 | bytes 3145728 | tf_op jit(solution)/shard_map/hyena_near/pallas_call | solution.py:173
  63.7 8.4 %attend.1 = (f32[4,128,512]{2,1,0:T(8,128)S(1)}, f32[4,128,512]{2,1,0:T(8,128)S(1)}, f32[4,128,512]{2,1,0:T(8,128)S(1)}) custom-call(s32[8]{0:T(128)S(1)} %concatenate.8.info_ref, bf16[3,128,2048]{2,1,0:T(8,128)(2,1)S(1)} %bitcast.11, bf16[3,128,1024]{2,1,0:T(8,128)(2,1)} %collective-permute-done.6.theirs_ref.theirs, ...), custom_call_target="tpu_custom_call" | custom-call | flops 872415232 | bytes 3670016 | tf_op jit(solution)/shard_map/attend/pallas_call | solution.py:418
  72.1 5.6 %collective-permute-done.9.own = bf16[2,2,128,512]{3,2,1,0:T(8,128)(2,1)} collective-permute-done((bf16[2,2,128,512]{3,2,1,0:T(8,128)(2,1)}, bf16[2,2,128,512]{3,2,1,0:T(8,128)(2,1)}, u32[]{:S(2)}, u32[]{:S(2)}) %collective-permute-start.9) | collective-permute-done | bytes 524320 | tf_op jit(solution)/shard_map/ppermute | solution.py:29
  77.8 4.4 %attend_last.1 = (bf16[128,512]{1,0:T(8,128)(2,1)S(1)}, bf16[128,512]{1,0:T(8,128)(2,1)S(1)}, bf16[128,512]{1,0:T(8,128)(2,1)S(1)}, bf16[128,512]{1,0:T(8,128)(2,1)S(1)}) custom-call(s32[8]{0:T(128)S(1)} %concatenate.8.info_ref, bf16[3,128,2048]{2,1,0:T(8,128)(2,1)S(1)} %bitcast.12, bf16[3,128,1024]{2,1,0:T(8,128)(2,1)} %collective-permute-done.6.theirs_ref.theirs, ...), custom_call_target="tpu_custom_call" | custom-call | flops 201326592 | bytes 3145728 | tf_op jit(solution)/shard_map/attend_last/pallas_call | solution.py:496
  82.1 1.5 %collective-permute-start.12 = (bf16[128,512]{1,0:T(8,128)(2,1)S(1)}, bf16[128,512]{1,0:T(8,128)(2,1)S(1)}, u32[]{:S(2)}, u32[]{:S(2)}) collective-permute-start(bf16[128,512]{1,0:T(8,128)(2,1)S(1)} %get-tuple-element.37), channel_id=1, source_target_pairs={{0,1},{1,0},{2,3},{3,2},{4,5},{5,4},{6,7},{7,6},{8,9},{9,8},{10,11... | collective-permute-start | bytes 393224 | tf_op jit(solution)/shard_map/ppermute | solution.py:23
  84.0 1.4 %collective-permute-start.14 = (bf16[128,512]{1,0:T(8,128)(2,1)S(1)}, bf16[128,512]{1,0:T(8,128)(2,1)S(1)}, u32[]{:S(2)}, u32[]{:S(2)}) collective-permute-start(bf16[128,512]{1,0:T(8,128)(2,1)S(1)} %get-tuple-element.39), channel_id=1, source_target_pairs={{0,3},{1,2},{2,1},{3,0},{4,7},{5,6},{6,5},{7,4},{8,11},{9,10},{10,... | collective-permute-start | bytes 393224 | tf_op jit(solution)/shard_map/ppermute | solution.py:23
  85.3 0.7 pad_maximum_fusion.carried_ref
  86.0 4.0 %hyena_finish.1 = bf16[128,2048]{1,0:T(8,128)(2,1)} custom-call(f32[128,2048]{1,0:T(8,128)} %get-tuple-element.26.near_ref, f32[128,2048]{1,0:T(8,128)} %get-tuple-element.27.q_ref, f32[16,2048]{1,0:T(8,128)} %pad_maximum_fusion.carried_ref, f32[16,1,128]{2,1,0:T(1,128)} %bitcast.18, f32[16,1,128]{2,1,0:T(1,128)} %bitcast.20), custom_call_target="tpu_custom_call" | custom-call | flops 201326592 | bytes 2621440 | tf_op jit(solution)/shard_map/hyena_finish/pallas_call | solution.py:235
  90.0 1.6 %collective-permute-done.14.refs_3_ = bf16[128,512]{1,0:T(8,128)(2,1)S(1)} collective-permute-done((bf16[128,512]{1,0:T(8,128)(2,1)S(1)}, bf16[128,512]{1,0:T(8,128)(2,1)S(1)}, u32[]{:S(2)}, u32[]{:S(2)}) %collective-permute-start.14) | collective-permute-done | bytes 131104 | tf_op jit(solution)/shard_map/ppermute | solution.py:23
  91.6 1.4 %assemble.1 = bf16[128,2048]{1,0:T(8,128)(2,1)} custom-call(s32[4]{0:T(128)S(1)} %copy-done.8, bf16[128,512]{1,0:T(8,128)(2,1)S(1)} %get-tuple-element.36.refs_0_, bf16[128,512]{1,0:T(8,128)(2,1)S(1)} %collective-permute-done.12.refs_1_, bf16[128,512]{1,0:T(8,128)(2,1)S(1)} %collective-permute-done.13.refs_2_, ...), custom_call_target="tpu_custom_call" | custom-call | bytes 1048576 | tf_op jit(solution)/shard_map/assemble/pallas_call | solution.py:525
  (52 shorter events, 2.8 us)
Async XLA Ops:
  1.3 8.7 %copy-start.13 = (f32[128,16]{0,1:T(8,128)S(1)}, f32[128,16]{0,1:T(8,128)}, u32[]{:S(2)}) copy-start(f32[128,16]{0,1:T(8,128)} %param.8) | copy-start | bytes 24580
  1.3 8.9 %copy-start.1 = (bf16[128,3,2048]{2,0,1:T(8,128)(2,1)S(1)}, bf16[128,3,2048]{2,0,1:T(8,128)(2,1)}, u32[]{:S(2)}) copy-start(bf16[128,3,2048]{2,0,1:T(8,128)(2,1)} %param.6) | copy-start | bytes 4718596
  1.3 8.9 %copy-start.3 = (f32[3,3,2048]{2,1,0:T(4,128)S(1)}, f32[3,3,2048]{2,1,0:T(4,128)}, u32[]{:S(2)}) copy-start(f32[3,3,2048]{2,1,0:T(4,128)} %w_ref.3) | copy-start | bytes 221188
  4.1 13.9 %copy-start = (bf16[128,3,2048]{2,0,1:T(8,128)(2,1)S(1)}, bf16[128,3,2048]{2,0,1:T(8,128)(2,1)}, u32[]{:S(2)}) copy-start(bf16[128,3,2048]{2,0,1:T(8,128)(2,1)} %param.10) | copy-start | bytes 4718596
  4.1 13.9 %copy-start.8 = (s32[4]{0:T(128)S(1)}, s32[4]{0:T(128)}, u32[]{:S(2)}) copy-start(s32[4]{0:T(128)} %pad_add_fusion.at_ref) | copy-start | bytes 52
  4.1 13.9 %collective-permute-start.6 = (bf16[3,128,1024]{2,1,0:T(8,128)(2,1)}, bf16[3,128,1024]{2,1,0:T(8,128)(2,1)}, u32[]{:S(2)}, u32[]{:S(2)}) collective-permute-start(bf16[3,128,1024]{2,1,0:T(8,128)(2,1)} %get-tuple-element.30), channel_id=1, source_target_pairs={{0,1},{1,0},{2,3},{3,2},{4,5},{5,4},{6,7},{7,6},{8,9},{9,8},{10,11... | collective-permute-start | bytes 2359304 | tf_op jit(solution)/shard_map/ppermute | solution.py:23
  4.9 5.1 %collective-permute-start = (bf16[3,8,2048]{2,1,0:T(8,128)(2,1)}, bf16[3,8,2048]{2,1,0:T(8,128)(2,1)S(1)}, u32[]{:S(2)}, u32[]{:S(2)}) collective-permute-start(bf16[3,8,2048]{2,1,0:T(8,128)(2,1)} %get-tuple-element.21), channel_id=1, source_target_pairs={{0,1},{1,2},{2,3},{3,4},{4,5},{5,6},{6,7},{7,8},{8,9},{9,10},{10,1... | collective-permute-start | bytes 294920 | tf_op jit(solution)/shard_map/ppermute | solution.py:29
  10.0 9.3 %copy-start.4 = (bf16[3,8,2048]{2,1,0:T(8,128)(2,1)}, bf16[3,8,2048]{2,1,0:T(8,128)(2,1)S(1)}, u32[]{:S(2)}) copy-start(bf16[3,8,2048]{2,1,0:T(8,128)(2,1)S(1)} %collective-permute-done.halo_ref) | copy-start | bytes 294916
  10.2 9.1 %copy-start.7 = (f32[16,1,128]{2,0,1:T(8,128)}, f32[16,1,128]{2,0,1:T(8,128)S(1)}, u32[]{:S(2)}) copy-start(f32[16,1,128]{2,0,1:T(8,128)S(1)} %reshape.10) | copy-start | bytes 24580
  12.3 0.8 copy-start.2
  13.1 0.7 copy-start.5
  13.7 3.0 %collective-permute-start.1 = (f32[16,1024]{1,0:T(8,128)S(1)}, f32[16,1024]{1,0:T(8,128)S(1)}, u32[]{:S(2)}, u32[]{:S(2)}) collective-permute-start(f32[16,1024]{1,0:T(8,128)S(1)} %constant_dynamic-slice_fusion), channel_id=1, source_target_pairs={{0,1},{1,0},{2,3},{3,2},{4,5},{5,4},{6,7},{7,6},{8,9},{9,8},{10,11... | collective-permute-start | bytes 196616 | tf_op jit(solution)/shard_map/ppermute | solution.py:23
  16.7 8.6 %copy-start.9 = (f32[16,1024]{1,0:T(8,128)}, f32[16,1024]{1,0:T(8,128)S(1)}, u32[]{:S(2)}) copy-start(f32[16,1024]{1,0:T(8,128)S(1)} %collective-permute-done.1) | copy-start | bytes 196612
  17.6 7.7 %collective-permute-start.2 = (f32[16,1024]{1,0:T(8,128)S(1)}, f32[16,1024]{1,0:T(8,128)S(1)}, u32[]{:S(2)}, u32[]{:S(2)}) collective-permute-start(f32[16,1024]{1,0:T(8,128)S(1)} %select_add_fusion.1), channel_id=1, source_target_pairs={{0,2},{1,3},{2,0},{3,1},{4,6},{5,7},{6,4},{7,5},{8,10},{9,11},{10,... | collective-permute-start | bytes 196616 | tf_op jit(solution)/shard_map/ppermute | solution.py:23
  19.3 29.7 %collective-permute-start.10 = (bf16[2,2,128,512]{3,2,1,0:T(8,128)(2,1)S(1)}, bf16[2,2,128,512]{3,2,1,0:T(8,128)(2,1)}, u32[]{:S(2)}, u32[]{:S(2)}) collective-permute-start(bf16[2,2,128,512]{3,2,1,0:T(8,128)(2,1)S(1)} %get-tuple-element.32), channel_id=1, source_target_pairs={{0,6},{1,7},{2,4},{3,5},{4,10},{5,11},{6,8},{7,9},{8,14},{9,15},{1... | collective-permute-start | bytes 1572872 | tf_op jit(solution)/shard_map/ppermute | solution.py:29
  23.3 28.9 %collective-permute-start.8 = (bf16[2,2,128,512]{3,2,1,0:T(8,128)(2,1)S(1)}, bf16[2,2,128,512]{3,2,1,0:T(8,128)(2,1)}, u32[]{:S(2)}, u32[]{:S(2)}) collective-permute-start(bf16[2,2,128,512]{3,2,1,0:T(8,128)(2,1)S(1)} %get-tuple-element.31), channel_id=1, source_target_pairs={{0,4},{1,5},{2,6},{3,7},{4,8},{5,9},{6,10},{7,11},{8,12},{9,13},{1... | collective-permute-start | bytes 1572872 | tf_op jit(solution)/shard_map/ppermute | solution.py:29
  25.3 0.6 copy-start.11
  25.9 28.3 %copy-start.6 = (f32[16,2048]{1,0:T(8,128)S(1)}, f32[16,2048]{1,0:T(8,128)}, u32[]{:S(2)}) copy-start(f32[16,2048]{1,0:T(8,128)} %copy-done.5) | copy-start | bytes 393220
  25.9 31.0 %copy-start.15 = (s32[4]{0:T(128)S(1)}, s32[4]{0:T(128)}, u32[]{:S(2)}) copy-start(s32[4]{0:T(128)} %param.11) | copy-start | bytes 52
  25.9 31.1 %copy-start.14 = (f32[128,16]{0,1:T(8,128)S(1)}, f32[128,16]{0,1:T(8,128)}, u32[]{:S(2)}) copy-start(f32[128,16]{0,1:T(8,128)} %param.9) | copy-start | bytes 24580
  25.9 21.7 %collective-permute-start.3 = (f32[16,1024]{1,0:T(8,128)S(1)}, f32[16,1024]{1,0:T(8,128)S(1)}, u32[]{:S(2)}, u32[]{:S(2)}) collective-permute-start(f32[16,1024]{1,0:T(8,128)S(1)} %select_add_fusion), channel_id=1, source_target_pairs={{0,4},{1,5},{2,6},{3,7},{4,8},{5,9},{6,10},{7,11},{8,12},{9,13},{1... | collective-permute-start | bytes 196616 | tf_op jit(solution)/shard_map/ppermute | solution.py:29
  28.0 26.2 %copy-start.10 = (f32[16,1024]{1,0:T(8,128)S(1)}, f32[16,1024]{1,0:T(8,128)}, u32[]{:S(2)}) copy-start(f32[16,1024]{1,0:T(8,128)} %copy-done.9) | copy-start | bytes 196612
  28.0 26.2 %copy-start.12 = (f32[16,1024]{1,0:T(8,128)S(1)}, f32[16,1024]{1,0:T(8,128)}, u32[]{:S(2)}) copy-start(f32[16,1024]{1,0:T(8,128)} %copy-done.11) | copy-start | bytes 196612
  29.2 34.5 %collective-permute-start.7 = (bf16[2,3,128,512]{3,2,1,0:T(8,128)(2,1)S(1)}, bf16[2,3,128,512]{3,2,1,0:T(8,128)(2,1)S(1)}, u32[]{:S(2)}, u32[]{:S(2)}) collective-permute-start(bf16[2,3,128,512]{3,2,1,0:T(8,128)(2,1)S(1)} %pack.2), channel_id=1, source_target_pairs={{0,2},{1,3},{2,0},{3,1},{4,6},{5,7},{6,4},{7,5},{8,10},{9,11},{10,... | collective-permute-start | bytes 2359304 | tf_op jit(solution)/shard_map/ppermute | solution.py:23
  47.7 6.5 %collective-permute-start.4 = (f32[16,1024]{1,0:T(8,128)S(1)}, f32[16,1024]{1,0:T(8,128)S(1)}, u32[]{:S(2)}, u32[]{:S(2)}) collective-permute-start(f32[16,1024]{1,0:T(8,128)S(1)} %multiply_add_fusion.1), channel_id=1, source_target_pairs={{0,8},{1,9},{2,10},{3,11},{4,12},{5,13},{6,14},{7,15},{16,24},{17,... | collective-permute-start | bytes 196616 | tf_op jit(solution)/shard_map/ppermute | solution.py:29
  49.0 23.1 %collective-permute-start.11 = (bf16[2,2,128,512]{3,2,1,0:T(8,128)(2,1)}, bf16[2,2,128,512]{3,2,1,0:T(8,128)(2,1)}, u32[]{:S(2)}, u32[]{:S(2)}) collective-permute-start(bf16[2,2,128,512]{3,2,1,0:T(8,128)(2,1)} %collective-permute-done.10.cross), channel_id=1, source_target_pairs={{4,8},{5,9},{6,10},{7,11},{8,12},{9,13},{10,14},{11,15},{20,24},{2... | collective-permute-start | bytes 1572872 | tf_op jit(solution)/shard_map/ppermute | solution.py:29
  52.2 25.6 %collective-permute-start.9 = (bf16[2,2,128,512]{3,2,1,0:T(8,128)(2,1)}, bf16[2,2,128,512]{3,2,1,0:T(8,128)(2,1)}, u32[]{:S(2)}, u32[]{:S(2)}) collective-permute-start(bf16[2,2,128,512]{3,2,1,0:T(8,128)(2,1)} %collective-permute-done.8.own), channel_id=1, source_target_pairs={{4,8},{5,9},{6,10},{7,11},{8,12},{9,13},{10,14},{11,15},{20,24},{2... | collective-permute-start | bytes 1572872 | tf_op jit(solution)/shard_map/ppermute | solution.py:29
  54.9 8.8 %collective-permute-start.5 = (f32[16,1024]{1,0:T(8,128)}, f32[16,1024]{1,0:T(8,128)S(1)}, u32[]{:S(2)}, u32[]{:S(2)}) collective-permute-start(f32[16,1024]{1,0:T(8,128)} %get-tuple-element.40), channel_id=1, source_target_pairs={{0,1},{1,0},{2,3},{3,2},{4,5},{5,4},{6,7},{7,6},{8,9},{9,8},{10,11... | collective-permute-start | bytes 196616 | tf_op jit(solution)/shard_map/ppermute | solution.py:23
  82.1 7.9 %collective-permute-start.12 = (bf16[128,512]{1,0:T(8,128)(2,1)S(1)}, bf16[128,512]{1,0:T(8,128)(2,1)S(1)}, u32[]{:S(2)}, u32[]{:S(2)}) collective-permute-start(bf16[128,512]{1,0:T(8,128)(2,1)S(1)} %get-tuple-element.37), channel_id=1, source_target_pairs={{0,1},{1,0},{2,3},{3,2},{4,5},{5,4},{6,7},{7,6},{8,9},{9,8},{10,11... | collective-permute-start | bytes 393224 | tf_op jit(solution)/shard_map/ppermute | solution.py:23
  83.6 6.4 %collective-permute-start.13 = (bf16[128,512]{1,0:T(8,128)(2,1)S(1)}, bf16[128,512]{1,0:T(8,128)(2,1)S(1)}, u32[]{:S(2)}, u32[]{:S(2)}) collective-permute-start(bf16[128,512]{1,0:T(8,128)(2,1)S(1)} %get-tuple-element.38), channel_id=1, source_target_pairs={{0,2},{1,3},{2,0},{3,1},{4,6},{5,7},{6,4},{7,5},{8,10},{9,11},{10,... | collective-permute-start | bytes 393224 | tf_op jit(solution)/shard_map/ppermute | solution.py:23
  84.0 7.7 %collective-permute-start.14 = (bf16[128,512]{1,0:T(8,128)(2,1)S(1)}, bf16[128,512]{1,0:T(8,128)(2,1)S(1)}, u32[]{:S(2)}, u32[]{:S(2)}) collective-permute-start(bf16[128,512]{1,0:T(8,128)(2,1)S(1)} %get-tuple-element.39), channel_id=1, source_target_pairs={{0,3},{1,2},{2,1},{3,0},{4,7},{5,6},{6,5},{7,4},{8,11},{9,10},{10,... | collective-permute-start | bytes 393224 | tf_op jit(solution)/shard_map/ppermute | solution.py:23

commit v6 on v5

v6 whole, which is shorter than its diff:
```python
import functools
import math

import jax
import jax.numpy as jnp
from jax import lax
from jax.experimental import pallas as pl
from jax.experimental.pallas import tpu as pltpu
from jax.sharding import PartitionSpec as P


HEAD = 128
LANES = 128
EDGE = 8
ROW = 4

F32 = jnp.float32
BF16 = jnp.bfloat16


def flip(value, axis, bit):
    count = lax.axis_size(axis)
    return lax.ppermute(value, axis, [(at, at ^ bit) for at in range(count)])


def side_of(at):
    return at // 2 % 2


def ahead(value, axis, steps, bit=0, first=0, side=None):
    count = lax.axis_size(axis)
    pairs = [
        (at, (at + steps) ^ bit)
        for at in range(first, count - steps)
        if side is None or side_of(at) == side
    ]
    return lax.ppermute(value, axis, pairs)


def spot():
    index = lax.axis_index("ctx")
    return index & 1, lax.shift_right_logical(index, 1) & 1, index & (ROW - 1), index // ROW


ALL_VMEM = 67043328


def limits(mib):
    return pltpu.CompilerParams(vmem_limit_bytes=mib << 20)


def cost(flops, moved, exps=0):
    return pl.CostEstimate(flops=flops, bytes_accessed=moved, transcendentals=exps)


VMEM = pl.BlockSpec(memory_space=pltpu.VMEM)
SMEM = pl.BlockSpec(memory_space=pltpu.SMEM)
ANY = pl.BlockSpec(memory_space=pl.ANY)
HBM = pl.BlockSpec(memory_space=pltpu.HBM)


def same_filter(modes, width, terms, lanes):
    row_at = lax.broadcasted_iota(jnp.int32, (terms, lanes), 0)
    lane_at = lax.broadcasted_iota(jnp.int32, (terms, lanes), 1)
    kept = None
    for g in range(terms // modes):
        both = (
            (row_at >= g * modes)
            & (row_at < (g + 1) * modes)
            & (lane_at >= g * width)
            & (lane_at < (g + 1) * width)
        )
        kept = both if kept is None else kept | both
    return kept


def feature(x, halo, w_ref, stream, at):
    here = x.astype(F32)
    halo = halo.astype(F32)
    edge = halo.shape[0]
    row_at = lax.broadcasted_iota(jnp.int32, here.shape, 0)
    one = jnp.where(row_at == 0, halo[edge - 1 :], pltpu.roll(here, 1, 0))
    two = jnp.where(row_at == 1, halo[edge - 1 :], pltpu.roll(here, 2, 0))
    two = jnp.where(row_at == 0, halo[edge - 2 : edge - 1], two)
    tap = [w_ref[n, stream : stream + 1, at] for n in range(3)]
    return tap[0] * here + tap[1] * one + tap[2] * two


def of_step(table_ref):
    groups = table_ref.shape[1]
    return pltpu.roll(table_ref[...], groups - pl.program_id(0) * (groups // STEPS), 1)


def down(table, part, filters, lanes):
    columns = [table[:, part * filters + g : part * filters + g + 1] for g in range(filters)]
    return jnp.concatenate([jnp.broadcast_to(c, (c.shape[0], lanes)) for c in columns], axis=0)


def hyena_ends_body(filters, x_ref, halo_ref, w_ref, rate_ref, mixed_ref, ends_ref, wide_ref):
    rows = x_ref.shape[1]
    modes, groups = rate_ref.shape
    parts = groups // STEPS // filters
    terms = filters * modes
    lanes = x_ref.shape[2] // parts
    width = lanes // filters
    rates = of_step(rate_ref)
    lag = (rows - 1 - lax.broadcasted_iota(jnp.int32, (terms, rows), 1)).astype(F32)
    own = same_filter(modes, width, terms, lanes)
    pick = lambda matrix: jnp.sum(jnp.where(own, matrix, 0.0).reshape(filters, modes, lanes), axis=0)
    for part in range(parts):
        at = slice(part * lanes, (part + 1) * lanes)
        key, value = (feature(x_ref[n, :, at], halo_ref[n, :, at], w_ref, n, at) for n in (1, 2))
        mixed = (key * value).astype(BF16)
        mixed_ref[:, at] = mixed
        rate = down(rates, part, filters, rows)
        powers = jnp.exp(-rate * lag)
        high = powers.astype(BF16)
        low = (powers - high.astype(F32)).astype(BF16)
        ends = jnp.dot(high, mixed, preferred_element_type=F32) + jnp.dot(
            low, mixed, preferred_element_type=F32
        )
        ends_ref[:, at] = pick(ends)
        wide_ref[:, at] = pick(rate)


STEPS = 4


def hyena_ends(streams, halo, short_weight, rates):
    _, rows, channels = streams.shape
    edge = halo.shape[1]
    modes, groups = rates.shape
    filters = groups * LANES // channels
    terms = filters * modes
    wide = channels // STEPS
    by_block = lambda n: (0, n)
    lead = lambda n: (0, 0, n)
    return pl.pallas_call(
        functools.partial(hyena_ends_body, filters),
        grid=(STEPS,),
        in_specs=[
            pl.BlockSpec((3, rows, wide), lead),
            pl.BlockSpec((3, edge, wide), lead),
            pl.BlockSpec((3, 3, wide), lead),
            pl.BlockSpec((modes, groups), lambda n: (0, 0)),
        ],
        out_specs=[
            pl.BlockSpec((rows, wide), by_block),
            pl.BlockSpec((modes, wide), by_block),
            pl.BlockSpec((modes, wide), by_block),
        ],
        out_shape=[
            jax.ShapeDtypeStruct((rows, channels), BF16),
            jax.ShapeDtypeStruct((modes, channels), F32),
            jax.ShapeDtypeStruct((modes, channels), F32),
        ],
        compiler_params=limits(16),
        cost_estimate=cost(4 * rows * terms * channels, 8 * rows * channels),
        name="hyena_ends",
    )(streams, halo, short_weight, rates)


def hyena_near_body(filters, x_ref, halo_ref, w_ref, mixed_ref, rate_ref, res_ref, near_ref, q_ref, taps_s, u_s):
    rows = x_ref.shape[1]
    modes, groups = rate_ref.shape
    parts = groups // STEPS // filters
    terms = filters * modes
    lanes = x_ref.shape[2] // parts
    width = lanes // filters
    rates = of_step(rate_ref)
    coeffs = of_step(res_ref) * jnp.sqrt(2.0 * rates / modes)
    row_at = lax.broadcasted_iota(jnp.int32, (rows, lanes), 0)
    lane_at = lax.broadcasted_iota(jnp.int32, (rows, lanes), 1)
    lag = (rows - 1 - lax.broadcasted_iota(jnp.int32, (terms, rows), 1)).astype(F32)
    zero = jnp.zeros((rows, lanes), BF16)
    for part in range(parts):
        at = slice(part * lanes, (part + 1) * lanes)
        q_ref[:, at] = feature(x_ref[0, :, at], halo_ref[0, :, at], w_ref, 0, at)
        mixed = mixed_ref[:, at]
        rate = down(rates, part, filters, rows)
        powers = down(coeffs, part, filters, rows) * jnp.exp(-rate * lag)
        backward = jnp.sum(powers.reshape(filters, modes, rows), axis=1)
        for g in range(filters):
            spread = jnp.broadcast_to(backward[g : g + 1], (rows, rows))
            shifted = pltpu.roll(spread, 1, 1, stride=1, stride_axis=0)
            kept = jnp.where(lane_at <= row_at, shifted, 0.0)
            taps_s[part, :, g * rows : (g + 1) * rows] = kept.astype(BF16)
            mine = (lane_at >= g * width) & (lane_at < (g + 1) * width)
            u_s[part, g * rows : (g + 1) * rows, :] = jnp.where(mine, mixed, zero)
        near_ref[:, at] = jnp.dot(taps_s[part], u_s[part], preferred_element_type=F32)


def hyena_near(streams, halo, short_weight, mixed, rates, residues):
    _, rows, channels = streams.shape
    edge = halo.shape[1]
    modes, groups = rates.shape
    lanes = LANES
    filters = groups * lanes // channels
    parts = groups // STEPS // filters
    wide = channels // STEPS
    by_block = lambda n: (0, n)
    lead = lambda n: (0, 0, n)
    whole = lambda n: (0, 0)
    return pl.pallas_call(
        functools.partial(hyena_near_body, filters),
        grid=(STEPS,),
        in_specs=[
            pl.BlockSpec((1, rows, wide), lead),
            pl.BlockSpec((1, edge, wide), lead),
            pl.BlockSpec((3, 3, wide), lead),
            pl.BlockSpec((rows, wide), by_block),
            pl.BlockSpec((modes, groups), whole),
            pl.BlockSpec((modes, groups), whole),
        ],
        out_specs=[
            pl.BlockSpec((rows, wide), by_block),
            pl.BlockSpec((rows, wide), by_block),
        ],
        out_shape=[
            jax.ShapeDtypeStruct((rows, channels), F32),
            jax.ShapeDtypeStruct((rows, channels), F32),
        ],
        scratch_shapes=[
            pltpu.VMEM((parts, rows, filters * rows), BF16),
            pltpu.VMEM((parts, filters * rows, lanes), BF16),
        ],
        compiler_params=limits(58),
        cost_estimate=cost(2 * rows * rows * filters * channels, 12 * rows * channels),
        name="hyena_near",
    )(streams, halo, short_weight, mixed, rates, residues)


def hyena_out_body(filters, near_ref, q_ref, carried_ref, rate_ref, res_ref, out_ref):
    rows = near_ref.shape[0]
    modes, groups = rate_ref.shape
    parts = groups // STEPS // filters
    terms = filters * modes
    lanes = near_ref.shape[1] // parts
    width = lanes // filters
    rates = of_step(rate_ref)
    coeffs = of_step(res_ref) * jnp.sqrt(2.0 * rates / modes)
    lag = (1 + lax.broadcasted_iota(jnp.int32, (terms, rows), 1)).astype(F32)
    own = same_filter(modes, width, terms, lanes)
    for part in range(parts):
        at = slice(part * lanes, (part + 1) * lanes)
        rate = down(rates, part, filters, rows)
        powers = (down(coeffs, part, filters, rows) * jnp.exp(-rate * lag)).T
        p_high = powers.astype(BF16)
        p_low = (powers - p_high.astype(F32)).astype(BF16)
        carried = jnp.where(own, jnp.concatenate([carried_ref[:, at]] * filters, axis=0), 0.0)
        c_high = carried.astype(BF16)
        c_low = (carried - c_high.astype(F32)).astype(BF16)
        far = (
            jnp.dot(p_high, c_high, preferred_element_type=F32)
            + jnp.dot(p_low, c_high, preferred_element_type=F32)
            + jnp.dot(p_high, c_low, preferred_element_type=F32)
        )
        out_ref[:, at] = (q_ref[:, at] * (near_ref[:, at] + far)).astype(BF16)


def hyena_finish(near, query, carried, rates, residues):
    rows, channels = near.shape
    modes, groups = rates.shape
    filters = groups * LANES // channels
    terms = filters * modes
    wide = channels // STEPS
    by_block = lambda n: (0, n)
    whole = lambda n: (0, 0)
    return pl.pallas_call(
        functools.partial(hyena_out_body, filters),
        grid=(STEPS,),
        in_specs=[
            pl.BlockSpec((rows, wide), by_block),
            pl.BlockSpec((rows, wide), by_block),
            pl.BlockSpec((modes, wide), by_block),
            pl.BlockSpec((modes, groups), whole),
            pl.BlockSpec((modes, groups), whole),
        ],
        out_specs=pl.BlockSpec((rows, wide), by_block),
        out_shape=jax.ShapeDtypeStruct((rows, channels), BF16),
        compiler_params=limits(16),
        cost_estimate=cost(6 * rows * terms * channels, 10 * rows * channels),
        name="hyena_finish",
    )(near, query, carried, rates, residues)


def scan_states(ends, rate, rows):
    half = ends.shape[1] // 2
    index = lax.axis_index("ctx")
    count = lax.axis_size("ctx") // ROW
    core, side = index % 2, index // 2 % 2
    take = lambda matrix, which: lax.dynamic_slice_in_dim(matrix, which * half, half, 1)
    rate = take(rate, core)
    decay = lambda blocks: jnp.exp(-rate * float(rows * blocks))
    mine = take(ends, core)
    theirs = flip(take(ends, 1 - core), "ctx", 1)
    even = jnp.where(core == 0, mine, theirs)
    odd = jnp.where(core == 0, theirs, mine)
    chip = decay(1) * even + odd
    other = flip(chip, "ctx", 2)
    left = jnp.where(side == 0, chip, other)
    total = decay(2) * left + jnp.where(side == 0, other, chip)
    before = ahead(total, "ctx", ROW)
    reach = 2
    while reach < count:
        upto = total + decay(ROW) * before
        earlier = ahead(upto, "ctx", ROW * reach)
        before = before + decay(ROW * (reach - 1)) * earlier
        reach *= 2
    before = jnp.where(side == 0, before, decay(2) * before + left)
    second = decay(1) * before + even
    keep = jnp.where(core == 0, before, second)
    back = flip(jnp.where(core == 0, second, before), "ctx", 1)
    return jnp.concatenate(
        [jnp.where(core == 0, keep, back), jnp.where(core == 0, back, keep)], axis=1
    )


def lanes_from(start, size):
    return pl.ds(pl.multiple_of(start * size, size), size)


def front_body(attn, hyena, theirs_ref, edge_ref, sems):
    rows, half = theirs_ref.shape[1:]
    away = attn.at[:, :, lanes_from(1 - spot()[0], half)]
    edge = hyena.at[:, rows - EDGE : rows, :]
    copies = [
        pltpu.make_async_copy(away, theirs_ref, sems.at[0]),
        pltpu.make_async_copy(edge, edge_ref, sems.at[1]),
    ]
    for copy in copies:
        copy.start()
    for copy in copies:
        copy.wait()


def front(attn, hyena):
    count, rows, channels = attn.shape
    return pl.pallas_call(
        front_body,
        in_specs=[HBM, HBM],
        out_specs=[VMEM, VMEM],
        out_shape=[
            jax.ShapeDtypeStruct((count, rows, channels // 2), attn.dtype),
            jax.ShapeDtypeStruct((count, EDGE, channels), hyena.dtype),
        ],
        scratch_shapes=[pltpu.SemaphoreType.DMA((2,))],
        compiler_params=pltpu.CompilerParams(vmem_limit_bytes=ALL_VMEM - (5 << 18)),
        cost_estimate=cost(0, 4 * count * rows * channels // 2),
        name="front",
    )(attn, hyena)


def pack_body(first, streams_ref, theirs_ref, *outs):
    core, side, _, _ = spot()
    slots = (0, 1) if first == 0 else (1 - core, core)
    quarter = theirs_ref.shape[2] // 2
    for out, away in zip(outs, (0, 1)[-len(outs) :]):
        to = 1 - side if away else side
        for stream in range(first, 3):
            out[slots[0], stream - first] = streams_ref[stream, :, lanes_from(2 * core + to, quarter)]
            out[slots[1], stream - first] = theirs_ref[stream, :, lanes_from(to, quarter)]


def pack(streams, theirs, first, amount):
    _, rows, half = theirs.shape
    shape = jax.ShapeDtypeStruct((2, 3 - first, rows, half // 2), BF16)
    return pl.pallas_call(
        functools.partial(pack_body, first),
        in_specs=[VMEM, VMEM],
        out_specs=[VMEM] * amount,
        out_shape=[shape] * amount,
        compiler_params=limits(10),
        cost_estimate=cost(0, 8 * amount * rows * half),
        name="pack",
    )(streams, theirs)


def contig_start(docs_ref, position):
    first = jnp.zeros_like(position)
    bound = jnp.int32(0)
    for n in range(docs_ref.shape[0]):
        bound = bound + docs_ref[n]
        first = jnp.where(position >= bound, bound, first)
    return first


def row_part(streams, theirs, swap, slot, stream, quarter):
    core, side, _, _ = spot()
    if slot == 0:
        return streams.at[stream, :, lanes_from(2 * core + side, quarter)]
    if slot == 1:
        return theirs.at[stream, :, lanes_from(side, quarter)]
    return swap.at[slot - 2, stream]


SCALE = math.log2(math.e) / math.sqrt(HEAD)


KEYS = 256


def attend_body(docs_ref, streams, theirs, swap, own, cross, acc_ref, m_ref, l_ref, q_s, k_s, v_s, bias_s, s_s, sems):
    _, side, place, row = spot()
    rows, quarter = q_s.shape[1:]
    base = row * (ROW * rows)
    copies = []

    def bring(source, target):
        copies.append(pltpu.make_async_copy(source, target, sems.at[len(copies)]))
        copies[-1].start()

    for n in range(2):
        for old, which in ((own, side), (cross, 1 - side)):
            older = lanes_from(2 * which + 1 - n, rows)
            bring(old.at[n, 0], k_s.at[older])
            bring(old.at[n, 1], v_s.at[older])
    for slot in range(ROW):
        part = lambda stream: row_part(streams, theirs, swap, slot, stream, quarter)
        block = place ^ slot
        newer = lanes_from(ROW + block, rows)
        bring(part(0), q_s.at[block])
        bring(part(1), k_s.at[newer])
        bring(part(2), v_s.at[newer])
    for copy in copies:
        copy.wait()

    for block in range(ROW):
        width = (ROW + 1 + block) * rows
        position = base + block * rows + lax.broadcasted_iota(jnp.int32, (rows, 1), 0)
        first = contig_start(docs_ref, position)
        at = base - ROW * rows + lax.broadcasted_iota(jnp.int32, (rows, width), 1)
        bias_s[:, 0:width] = jnp.where((at >= first) & (at <= position), 0.0, -jnp.inf)
        tiles = [slice(n, min(n + KEYS, width)) for n in range(0, width, KEYS)]
        for head in range(quarter // HEAD):
            lanes = slice(head * HEAD, (head + 1) * HEAD)
            turn = head % 2
            top = None
            for tile in tiles:
                scores = lax.dot_general(
                    q_s[block, :, lanes],
                    k_s[tile, lanes],
                    (((1,), (1,)), ((), ())),
                    preferred_element_type=F32,
                )
                scores = scores + bias_s[:, tile]
                s_s[turn, :, tile] = scores
                for n in range(0, tile.stop - tile.start, LANES):
                    some = scores[:, n : n + LANES]
                    top = some if top is None else jnp.maximum(top, some)
            top = jnp.broadcast_to(jnp.max(top, axis=1, keepdims=True), (rows, LANES))
            m_ref[block, :, lanes] = top
            total = jnp.zeros((rows, HEAD), F32)
            below = jnp.zeros((rows, LANES), F32)
            for tile in tiles:
                count = (tile.stop - tile.start) // LANES
                weight = jnp.exp2((s_s[turn, :, tile] - jnp.concatenate([top] * count, axis=1)) * SCALE)
                for n in range(count):
                    below = below + weight[:, n * LANES : (n + 1) * LANES]
                total = total + jnp.dot(weight.astype(BF16), v_s[tile, lanes], preferred_element_type=F32)
            l_ref[block, :, lanes] = jnp.broadcast_to(
                jnp.sum(below, axis=1, keepdims=True), (rows, LANES)
            )
            acc_ref[block, :, lanes] = total


def attend(doc_lengths, streams, theirs, swap, own, cross):
    _, _, rows, quarter = own.shape
    heads = quarter // HEAD
    return pl.pallas_call(
        attend_body,
        in_specs=[SMEM] + [ANY] * 5,
        out_specs=[VMEM] * 3,
        out_shape=[
            jax.ShapeDtypeStruct((ROW, rows, quarter), F32),
        ]
        * 3,
        scratch_shapes=[
            pltpu.VMEM((ROW, rows, quarter), BF16),
            pltpu.VMEM((2 * ROW * rows, quarter), BF16),
            pltpu.VMEM((2 * ROW * rows, quarter), BF16),
            pltpu.VMEM((rows, 2 * ROW * rows), F32),
            pltpu.VMEM((2, rows, 2 * ROW * rows), F32),
            pltpu.SemaphoreType.DMA((5 * ROW,)),
        ],
        compiler_params=limits(20),
        cost_estimate=cost(26 * 4 * rows * rows * quarter, 14 * ROW * rows * quarter, 26 * heads * rows * rows),
        name="attend",
    )(doc_lengths, streams, theirs, swap, own, cross)


def attend_last_body(docs_ref, streams, theirs, swap, *refs):
    olds, (acc_ref, m_ref, l_ref), outs, (q_s, kv_s, o_s, sems) = refs[:4], refs[4:7], refs[7:11], refs[11:]
    _, side, place, row = spot()
    rows, quarter = q_s.shape[1:]
    base = row * (ROW * rows)
    copies = []

    def copy_of(source, target, n):
        return pltpu.make_async_copy(source, target, sems.at[n])

    for slot in range(ROW):
        copies.append(copy_of(row_part(streams, theirs, swap, slot, 0, quarter), q_s.at[place ^ slot], slot))
        copies[-1].start()
    for which in range(2):
        large, small = olds[2 * which : 2 * which + 2]
        arrived = [
            copy_of(small.at[0], kv_s.at[0], ROW),
            copy_of(large.at[1], kv_s.at[1], ROW + 1),
            copy_of(large.at[0], kv_s.at[2], ROW + 2),
        ]

        @pl.when(side == which)
        def _():
            for copy in arrived:
                copy.start()

    for copy in copies + arrived:
        copy.wait()
    for block in range(ROW):
        slot = place ^ block
        seen = ROW - 1 - block
        width = seen * rows
        if seen:
            position = base + block * rows + lax.broadcasted_iota(jnp.int32, (rows, 1), 0)
            first = contig_start(docs_ref, position)
            at = base - (ROW + seen) * rows + lax.broadcasted_iota(jnp.int32, (rows, width), 1)
            allowed = at >= first
        for head in range(quarter // HEAD):
            lanes = slice(head * HEAD, (head + 1) * HEAD)
            total = acc_ref[block, :, lanes]
            below = l_ref[block, :, lanes]
            if seen:
                keys = kv_s[block : ROW - 1, 0, :, lanes].reshape(width, HEAD)
                values = kv_s[block : ROW - 1, 1, :, lanes].reshape(width, HEAD)
                scores = lax.dot_general(
                    q_s[block, :, lanes],
                    keys,
                    (((1,), (1,)), ((), ())),
                    preferred_element_type=F32,
                )
                scores = jnp.where(allowed, scores, -jnp.inf)
                past = m_ref[block, :, lanes]
                top = jnp.maximum(past, jnp.max(scores, axis=1, keepdims=True))
                fade = jnp.exp2((past - top) * SCALE)
                weight = jnp.exp2((scores - jnp.concatenate([top] * seen, axis=1)) * SCALE)
                share = 1.0 / (below * fade + jnp.sum(weight, axis=1, keepdims=True))
                total = total * (fade * share) + share * jnp.dot(
                    weight.astype(BF16), values, preferred_element_type=F32
                )
            else:
                total = total * (1.0 / below)
            o_s[slot, :, lanes] = total.astype(BF16)
    for slot, out in enumerate(outs):
        out[...] = o_s[slot]


def attend_last(doc_lengths, streams, theirs, swap, olds, acc, top, below):
    _, rows, quarter = acc.shape
    heads = quarter // HEAD
    return pl.pallas_call(
        attend_last_body,
        in_specs=[SMEM] + [ANY] * 7 + [VMEM] * 3,
        out_specs=[VMEM] * ROW,
        out_shape=[jax.ShapeDtypeStruct((rows, quarter), BF16)] * ROW,
        scratch_shapes=[
            pltpu.VMEM((ROW, rows, quarter), BF16),
            pltpu.VMEM((ROW - 1, 2, rows, quarter), BF16),
            pltpu.VMEM((ROW, rows, quarter), BF16),
            pltpu.SemaphoreType.DMA((2 * ROW,)),
        ],
        compiler_params=limits(16),
        cost_estimate=cost(6 * 4 * rows * rows * quarter, 12 * ROW * rows * quarter, 6 * heads * rows * rows),
        name="attend_last",
    )(doc_lengths, streams, theirs, swap, *olds, acc, top, below)


def assemble_body(*refs):
    place = spot()[2]
    *pieces, out_ref = refs
    quarter = pieces[0].shape[1]
    for slot, piece in enumerate(pieces):
        maker = place ^ slot
        which = 2 * (maker & 1) + lax.shift_right_logical(maker, 1)
        out_ref[:, lanes_from(which, quarter)] = piece[...]


def assemble(pieces):
    rows, quarter = pieces[0].shape
    return pl.pallas_call(
        assemble_body,
        in_specs=[VMEM] * ROW,
        out_specs=VMEM,
        out_shape=jax.ShapeDtypeStruct((rows, ROW * quarter), BF16),
        compiler_params=limits(6),
        cost_estimate=cost(0, 16 * rows * quarter),
        name="assemble",
    )(*pieces)


def on_device(hyena_qkv, short_weight, filter_rate, filter_residue, attn_qkv, doc_lengths):
    rows = attn_qkv.shape[0]
    inner = hyena_qkv.transpose(1, 0, 2)
    streams = attn_qkv.transpose(1, 0, 2)
    rates, residues = filter_rate.T, filter_residue.T
    theirs, edge = front(streams, inner)

    theirs = flip(theirs, "ctx", 1)
    edge = ahead(edge, "ctx", 1)
    own, cross = pack(streams, theirs, 1, 2)
    cross = ahead(cross, "ctx", ROW, 2)
    own = ahead(own, "ctx", ROW)
    (swap,) = pack(streams, theirs, 0, 1)
    swap = flip(swap, "ctx", 2)
    olds = (
        ahead(cross, "ctx", ROW, 0, ROW, 0),
        ahead(own[:1], "ctx", ROW, 0, ROW, 0),
        ahead(own, "ctx", ROW, 0, ROW, 1),
        ahead(cross[:1], "ctx", ROW, 0, ROW, 1),
    )

    mixed, ends, wide = hyena_ends(inner, edge, short_weight, rates)
    near, query = hyena_near(inner, edge, short_weight, mixed, rates, residues)
    carried = scan_states(ends, wide, rows)
    hyena_out = hyena_finish(near, query, carried, rates, residues)

    acc, top, below = attend(doc_lengths, streams, theirs, swap, own, cross)
    made = attend_last(doc_lengths, streams, theirs, swap, olds, acc, top, below)
    pieces = [made[0]] + [flip(made[n], "ctx", n) for n in range(1, ROW)]
    attn_out = assemble(pieces)
    return (hyena_out, attn_out)


def solution(mesh):
    in_specs = (
        P(("group", "ctx"), None, None),
        P(),
        P(),
        P(),
        P(("group", "ctx"), None, None),
        P("group"),
    )
    out_specs = (P(("group", "ctx"), None), P(("group", "ctx"), None))
    return jax.shard_map(
        on_device, mesh=mesh, in_specs=in_specs, out_specs=out_specs, check_vma=False
    )
```

time: 93.7 us -> 89 us (0.950)
  the two profiles are of different devices: /device:TPU:19 before, /device:TPU:15 now
where the time goes in v6:
time: 89 us; the launch traced here: 87.3 us
  starting transfers between devices  30.5 us (34%)
  Pallas kernels  27.5 us (31%)
  waiting for transfers between devices  23.2 us (26%)
  other arithmetic  2.59 us (3%)
  local copies, waits for them, and re-layouts  2.34 us (3%)
  between operations  1.07 us (1%)
    ppermute x9, starting transfers between devices, ahead(): return lax.ppermute(value, axis, pairs)  21.2 us
    ppermute x9, waiting for transfers between devices, ahead(): return lax.ppermute(value, axis, pairs)  19.6 us
    ppermute x8, starting transfers between devices, flip(): return lax.ppermute(value, axis, [(at, at ^ bit) for at in range(count)])  9.33 us
    pallas_call x1, Pallas kernels, attend(): pl.pallas_call(attend_body, in_specs=[SMEM] + [ANY] * 5, out_specs=[VMEM]...  8.7 us
    pallas_call x1, Pallas kernels, hyena_near(): pl.pallas_call(functools.partial(hyena_near_body, filters), grid=(STEPS,)...  6.54 us
    ppermute x8, waiting for transfers between devices, flip(): return lax.ppermute(value, axis, [(at, at ^ bit) for at in range(count)])  3.61 us
    pallas_call x1, Pallas kernels, attend_last(): pl.pallas_call(attend_last_body, in_specs=[SMEM] + [ANY] * 7 + [VMEM] * 3...  3.5 us
    pallas_call x1, Pallas kernels, hyena_finish(): pl.pallas_call(functools.partial(hyena_out_body, filters), grid=(STEPS,),...  3.45 us
  transfers between devices with their start and end apart: 17, of which 4 were waited for; matrix products, arithmetic and copies ran while one was open for 3% of the time, Pallas kernels for 24%

profile of v6, /device:TPU:15, one launch (start us, length us, event | category | flops | bytes accessed | tf_op | source)
XLA Modules:
  0.0 87.3 jit_solution(10502981761516567760)
XLA Ops:
  0.7 2.1 %front.1 = (bf16[3,128,1024]{2,1,0:T(8,128)(2,1)}, bf16[3,8,2048]{2,1,0:T(8,128)(2,1)}) custom-call(bf16[3,128,2048]{2,1,0:T(8,128)(2,1)} %bitcast.4, bf16[3,128,2048]{2,1,0:T(8,128)(2,1)} %bitcast.9), custom_call_target="tpu_custom_call" | custom-call | bytes 1572864 | tf_op jit(solution)/shard_map/front/pallas_call | solution.py:339
  2.8 0.7 collective-permute-start.6
  3.5 3.2 %collective-permute-start = (bf16[3,8,2048]{2,1,0:T(8,128)(2,1)}, bf16[3,8,2048]{2,1,0:T(8,128)(2,1)S(1)}, u32[]{:S(2)}, u32[]{:S(2)}) collective-permute-start(bf16[3,8,2048]{2,1,0:T(8,128)(2,1)} %get-tuple-element.18), channel_id=1, source_target_pairs={{0,1},{1,2},{2,3},{3,4},{4,5},{5,6},{6,7},{7,8},{8,9},{9,10},{10,1... | collective-permute-start | bytes 294920 | tf_op jit(solution)/shard_map/ppermute | solution.py:37
  6.7 1.9 %collective-permute-done.halo_ref = bf16[3,8,2048]{2,1,0:T(8,128)(2,1)S(1)} collective-permute-done((bf16[3,8,2048]{2,1,0:T(8,128)(2,1)}, bf16[3,8,2048]{2,1,0:T(8,128)(2,1)S(1)}, u32[]{:S(2)}, u32[]{:S(2)}) %collective-permute-start) | collective-permute-done | bytes 98336 | tf_op jit(solution)/shard_map/ppermute | solution.py:37
  8.6 1.4 %copy-done.1 = bf16[128,3,2048]{2,0,1:T(8,128)(2,1)S(1)} copy-done((bf16[128,3,2048]{2,0,1:T(8,128)(2,1)S(1)}, bf16[128,3,2048]{2,0,1:T(8,128)(2,1)}, u32[]{:S(2)}) %copy-start.1) | copy-done | bytes 1572888
  10.1 2.2 %hyena_ends.1 = (bf16[128,2048]{1,0:T(8,128)(2,1)S(1)}, f32[16,2048]{1,0:T(8,128)S(1)}, f32[16,2048]{1,0:T(8,128)S(1)}) custom-call(bf16[3,128,2048]{2,1,0:T(8,128)(2,1)S(1)} %bitcast.11, bf16[3,8,2048]{2,1,0:T(8,128)(2,1)S(1)} %collective-permute-done.halo_ref, f32[3,3,2048]{2,1,0:T(4,128)S(1)} %copy-done.5, f32[16,128]{1,0:T(8,128)S(1)} %bitcast.13), custom_call_target="tpu_custom_call" | custom-call | flops 134217728 | bytes 2097152 | tf_op jit(solution)/shard_map/hyena_ends/pallas_call | solution.py:138
  12.3 0.8 copy-done.4
  13.1 1.2 %collective-permute-start.1 = (f32[16,1024]{1,0:T(8,128)S(1)}, f32[16,1024]{1,0:T(8,128)S(1)}, u32[]{:S(2)}, u32[]{:S(2)}) collective-permute-start(f32[16,1024]{1,0:T(8,128)S(1)} %constant_dynamic-slice_fusion), channel_id=1, source_target_pairs={{0,1},{1,0},{2,3},{3,2},{4,5},{5,4},{6,7},{7,6},{8,9},{9,8},{10,11... | collective-permute-start | bytes 196616 | tf_op jit(solution)/shard_map/ppermute | solution.py:23
  14.3 0.9 %collective-permute-done.1 = f32[16,1024]{1,0:T(8,128)S(1)} collective-permute-done((f32[16,1024]{1,0:T(8,128)S(1)}, f32[16,1024]{1,0:T(8,128)S(1)}, u32[]{:S(2)}, u32[]{:S(2)}) %collective-permute-start.1) | collective-permute-done | bytes 65568 | tf_op jit(solution)/shard_map/ppermute | solution.py:23
  15.3 1.2 %collective-permute-start.2 = (f32[16,1024]{1,0:T(8,128)S(1)}, f32[16,1024]{1,0:T(8,128)S(1)}, u32[]{:S(2)}, u32[]{:S(2)}) collective-permute-start(f32[16,1024]{1,0:T(8,128)S(1)} %select_add_fusion.1), channel_id=1, source_target_pairs={{0,2},{1,3},{2,0},{3,1},{4,6},{5,7},{6,4},{7,5},{8,10},{9,11},{10,... | collective-permute-start | bytes 196616 | tf_op jit(solution)/shard_map/ppermute | solution.py:23
  16.6 3.2 %collective-permute-start.10 = (bf16[2,2,128,512]{3,2,1,0:T(8,128)(2,1)S(1)}, bf16[2,2,128,512]{3,2,1,0:T(8,128)(2,1)S(1)}, u32[]{:S(2)}, u32[]{:S(2)}) collective-permute-start(bf16[2,2,128,512]{3,2,1,0:T(8,128)(2,1)S(1)} %get-tuple-element.26), channel_id=1, source_target_pairs={{0,4},{1,5},{2,6},{3,7},{4,8},{5,9},{6,10},{7,11},{8,12},{9,13},{1... | collective-permute-start | bytes 1572872 | tf_op jit(solution)/shard_map/ppermute | solution.py:37
  19.8 3.3 %collective-permute-start.8 = (bf16[2,2,128,512]{3,2,1,0:T(8,128)(2,1)S(1)}, bf16[2,2,128,512]{3,2,1,0:T(8,128)(2,1)S(1)}, u32[]{:S(2)}, u32[]{:S(2)}) collective-permute-start(bf16[2,2,128,512]{3,2,1,0:T(8,128)(2,1)S(1)} %get-tuple-element.25), channel_id=1, source_target_pairs={{0,6},{1,7},{2,4},{3,5},{4,10},{5,11},{6,8},{7,9},{8,14},{9,15},{1... | collective-permute-start | bytes 1572872 | tf_op jit(solution)/shard_map/ppermute | solution.py:37
  23.1 1.9 %collective-permute-start.3 = (f32[16,1024]{1,0:T(8,128)S(1)}, f32[16,1024]{1,0:T(8,128)S(1)}, u32[]{:S(2)}, u32[]{:S(2)}) collective-permute-start(f32[16,1024]{1,0:T(8,128)S(1)} %select_add_fusion), channel_id=1, source_target_pairs={{0,4},{1,5},{2,6},{3,7},{4,8},{5,9},{6,10},{7,11},{8,12},{9,13},{1... | collective-permute-start | bytes 196616 | tf_op jit(solution)/shard_map/ppermute | solution.py:37
  25.1 1.2 %collective-permute-start.7 = (bf16[2,3,128,512]{3,2,1,0:T(8,128)(2,1)S(1)}, bf16[2,3,128,512]{3,2,1,0:T(8,128)(2,1)S(1)}, u32[]{:S(2)}, u32[]{:S(2)}) collective-permute-start(bf16[2,3,128,512]{3,2,1,0:T(8,128)(2,1)S(1)} %pack.2), channel_id=1, source_target_pairs={{0,2},{1,3},{2,0},{3,1},{4,6},{5,7},{6,4},{7,5},{8,10},{9,11},{10,... | collective-permute-start | bytes 2359304 | tf_op jit(solution)/shard_map/ppermute | solution.py:23
  26.3 17.7 %collective-permute-done.3 = f32[16,1024]{1,0:T(8,128)S(1)} collective-permute-done((f32[16,1024]{1,0:T(8,128)S(1)}, f32[16,1024]{1,0:T(8,128)S(1)}, u32[]{:S(2)}, u32[]{:S(2)}) %collective-permute-start.3) | collective-permute-done | bytes 65568 | tf_op jit(solution)/shard_map/ppermute | solution.py:37
  44.0 4.2 %collective-permute-start.4 = (f32[16,1024]{1,0:T(8,128)S(1)}, f32[16,1024]{1,0:T(8,128)S(1)}, u32[]{:S(2)}, u32[]{:S(2)}) collective-permute-start(f32[16,1024]{1,0:T(8,128)S(1)} %multiply_add_fusion.1), channel_id=1, source_target_pairs={{0,8},{1,9},{2,10},{3,11},{4,12},{5,13},{6,14},{7,15},{16,24},{17,... | collective-permute-start | bytes 196616 | tf_op jit(solution)/shard_map/ppermute | solution.py:37
  48.3 1.3 %collective-permute-start.12 = (bf16[2,2,128,512]{3,2,1,0:T(8,128)(2,1)S(1)}, bf16[2,2,128,512]{3,2,1,0:T(8,128)(2,1)S(1)}, u32[]{:S(2)}, u32[]{:S(2)}) collective-permute-start(bf16[2,2,128,512]{3,2,1,0:T(8,128)(2,1)S(1)} %collective-permute-done.10.own), channel_id=1, source_target_pairs={{6,10},{7,11},{10,14},{11,15},{22,26},{23,27},{26,30},{27,31}} | collective-permute-start | bytes 1572872 | tf_op jit(solution)/shard_map/ppermute | solution.py:37
  49.6 0.7 collective-permute-start.9
  50.4 1.7 %broadcast_select_fusion.3 = (f32[16,1024]{1,0:T(8,128)}, f32[16,1024]{1,0:T(8,128)}, f32[16,1024]{1,0:T(8,128)}) fusion(pred[]{:T(512)S(6)} %eq.7, f32[16,1024]{1,0:T(8,128)} %copy-done.15, f32[16,2048]{1,0:T(8,128)} %copy-done.7, s32[]{:T(128)S(6)} %select_n.69, f32[16,2048]{1,0:T(8,128)S(1)} %get-tuple-element.22, f32[16,1024]{1,0:T(8,128)} %copy-done.12, ...), kind=kLoop, calls=%fused_computation.14 | loop fusion | flops 229376 | bytes 655366 | tf_op jit(solution)/shard_map/jit(_where)/select_n | solution.py:313
  52.0 2.8 %collective-permute-start.5 = (f32[16,1024]{1,0:T(8,128)}, f32[16,1024]{1,0:T(8,128)}, u32[]{:S(2)}, u32[]{:S(2)}) collective-permute-start(f32[16,1024]{1,0:T(8,128)} %get-tuple-element.34), channel_id=1, source_target_pairs={{0,1},{1,0},{2,3},{3,2},{4,5},{5,4},{6,7},{7,6},{8,9},{9,8},{10,11... | collective-permute-start | bytes 196616 | tf_op jit(solution)/shard_map/ppermute | solution.py:23
  54.8 6.5 %hyena_near.1 = (f32[128,2048]{1,0:T(8,128)}, f32[128,2048]{1,0:T(8,128)}) custom-call(bf16[3,128,2048]{2,1,0:T(8,128)(2,1)} %bitcast.10, bf16[3,8,2048]{2,1,0:T(8,128)(2,1)} %copy-done.6, f32[3,3,2048]{2,1,0:T(4,128)} %w_ref.3, bf16[128,2048]{1,0:T(8,128)(2,1)} %copy-done.4, f32[16,128]{1,0:T(8,128)} %bitcast.12, f32[16,128]{1,0:T(8,128)} %bitcast.15), custom_call_target="tpu_custom_call" | custom-call | flops 536870912 | bytes 3145728 | tf_op jit(solution)/shard_map/hyena_near/pallas_call | solution.py:204
  61.3 0.7 collective-permute-start.11
  62.1 2.7 %collective-permute-start.13 = (bf16[1,2,128,512]{3,2,1,0:T(8,128)(2,1)S(1)}, bf16[1,2,128,512]{3,2,1,0:T(8,128)(2,1)S(1)}, u32[]{:S(2)}, u32[]{:S(2)}) collective-permute-start(bf16[1,2,128,512]{3,2,1,0:T(8,128)(2,1)S(1)} %slice.9), channel_id=1, source_target_pairs={{6,10},{7,11},{10,14},{11,15},{22,26},{23,27},{26,30},{27,31}} | collective-permute-start | bytes 786440 | tf_op jit(solution)/shard_map/ppermute | solution.py:37
  64.8 0.9 broadcast_select_fusion.2
  65.7 8.7 %attend.1 = (f32[4,128,512]{2,1,0:T(8,128)S(1)}, f32[4,128,512]{2,1,0:T(8,128)S(1)}, f32[4,128,512]{2,1,0:T(8,128)S(1)}) custom-call(s32[4]{0:T(128)S(1)} %copy-done.11, bf16[3,128,2048]{2,1,0:T(8,128)(2,1)S(1)} %bitcast.7, bf16[3,128,1024]{2,1,0:T(8,128)(2,1)S(1)} %collective-permute-done.6.theirs_ref.theirs, ...), custom_call_target="tpu_custom_call" | custom-call | flops 872415232 | bytes 3670016 | tf_op jit(solution)/shard_map/attend/pallas_call | solution.py:470
  74.5 3.5 %attend_last.1 = (bf16[128,512]{1,0:T(8,128)(2,1)S(1)}, bf16[128,512]{1,0:T(8,128)(2,1)S(1)}, bf16[128,512]{1,0:T(8,128)(2,1)S(1)}, bf16[128,512]{1,0:T(8,128)(2,1)S(1)}) custom-call(s32[4]{0:T(128)S(1)} %copy-done.11, bf16[3,128,2048]{2,1,0:T(8,128)(2,1)S(1)} %bitcast.8, bf16[3,128,1024]{2,1,0:T(8,128)(2,1)S(1)} %collective-permute-done.6.theirs_ref.theirs, ...), custom_call_target="tpu_custom_call" | custom-call | flops 201326592 | bytes 3145728 | tf_op jit(solution)/shard_map/attend_last/pallas_call | solution.py:561
  78.0 0.4 collective-permute-start.14
  78.4 0.3 collective-permute-start.15
  78.7 1.5 %collective-permute-start.16 = (bf16[128,512]{1,0:T(8,128)(2,1)S(1)}, bf16[128,512]{1,0:T(8,128)(2,1)S(1)}, u32[]{:S(2)}, u32[]{:S(2)}) collective-permute-start(bf16[128,512]{1,0:T(8,128)(2,1)S(1)} %get-tuple-element.33), channel_id=1, source_target_pairs={{0,3},{1,2},{2,1},{3,0},{4,7},{5,6},{6,5},{7,4},{8,11},{9,10},{10,... | collective-permute-start | bytes 393224 | tf_op jit(solution)/shard_map/ppermute | solution.py:23
  80.3 3.4 %hyena_finish.1 = bf16[128,2048]{1,0:T(8,128)(2,1)} custom-call(f32[128,2048]{1,0:T(8,128)S(1)} %copy-done.2, f32[128,2048]{1,0:T(8,128)S(1)} %copy-done.3, f32[16,2048]{1,0:T(8,128)S(1)} %pad_maximum_fusion.carried_ref, f32[16,128]{1,0:T(8,128)S(1)} %bitcast.14, f32[16,128]{1,0:T(8,128)S(1)} %bitcast.16), custom_call_target="tpu_custom_call" | custom-call | flops 201326592 | bytes 2621440 | tf_op jit(solution)/shard_map/hyena_finish/pallas_call | solution.py:269
  83.7 2.7 %collective-permute-done.16.refs_3_ = bf16[128,512]{1,0:T(8,128)(2,1)S(1)} collective-permute-done((bf16[128,512]{1,0:T(8,128)(2,1)S(1)}, bf16[128,512]{1,0:T(8,128)(2,1)S(1)}, u32[]{:S(2)}, u32[]{:S(2)}) %collective-permute-start.16) | collective-permute-done | bytes 131104 | tf_op jit(solution)/shard_map/ppermute | solution.py:23
  86.4 0.8 assemble.1
  (54 shorter events, 0.4 us)
Async XLA Ops:
  0.6 8.0 %copy-start.5 = (f32[3,3,2048]{2,1,0:T(4,128)S(1)}, f32[3,3,2048]{2,1,0:T(4,128)}, u32[]{:S(2)}) copy-start(f32[3,3,2048]{2,1,0:T(4,128)} %w_ref.3) | copy-start | bytes 221188
  0.6 8.0 %copy-start.8 = (f32[128,16]{0,1:T(8,128)S(1)}, f32[128,16]{0,1:T(8,128)}, u32[]{:S(2)}) copy-start(f32[128,16]{0,1:T(8,128)} %param.8) | copy-start | bytes 24580
  2.8 13.7 %copy-start = (bf16[128,3,2048]{2,0,1:T(8,128)(2,1)S(1)}, bf16[128,3,2048]{2,0,1:T(8,128)(2,1)}, u32[]{:S(2)}) copy-start(bf16[128,3,2048]{2,0,1:T(8,128)(2,1)} %param.10) | copy-start | bytes 4718596
  2.8 13.7 %collective-permute-start.6 = (bf16[3,128,1024]{2,1,0:T(8,128)(2,1)}, bf16[3,128,1024]{2,1,0:T(8,128)(2,1)S(1)}, u32[]{:S(2)}, u32[]{:S(2)}) collective-permute-start(bf16[3,128,1024]{2,1,0:T(8,128)(2,1)} %get-tuple-element.24), channel_id=1, source_target_pairs={{0,1},{1,0},{2,3},{3,2},{4,5},{5,4},{6,7},{7,6},{8,9},{9,8},{10,11... | collective-permute-start | bytes 2359304 | tf_op jit(solution)/shard_map/ppermute | solution.py:23
  3.5 5.1 %collective-permute-start = (bf16[3,8,2048]{2,1,0:T(8,128)(2,1)}, bf16[3,8,2048]{2,1,0:T(8,128)(2,1)S(1)}, u32[]{:S(2)}, u32[]{:S(2)}) collective-permute-start(bf16[3,8,2048]{2,1,0:T(8,128)(2,1)} %get-tuple-element.18), channel_id=1, source_target_pairs={{0,1},{1,2},{2,3},{3,4},{4,5},{5,6},{6,7},{7,8},{8,9},{9,10},{10,1... | collective-permute-start | bytes 294920 | tf_op jit(solution)/shard_map/ppermute | solution.py:37
  8.6 7.9 %copy-start.6 = (bf16[3,8,2048]{2,1,0:T(8,128)(2,1)}, bf16[3,8,2048]{2,1,0:T(8,128)(2,1)S(1)}, u32[]{:S(2)}) copy-start(bf16[3,8,2048]{2,1,0:T(8,128)(2,1)S(1)} %collective-permute-done.halo_ref) | copy-start | bytes 294916
  13.1 35.1 %copy-start.7 = (f32[16,2048]{1,0:T(8,128)}, f32[16,2048]{1,0:T(8,128)S(1)}, u32[]{:S(2)}) copy-start(f32[16,2048]{1,0:T(8,128)S(1)} %get-tuple-element.23) | copy-start | bytes 393220
  13.1 2.1 %collective-permute-start.1 = (f32[16,1024]{1,0:T(8,128)S(1)}, f32[16,1024]{1,0:T(8,128)S(1)}, u32[]{:S(2)}, u32[]{:S(2)}) collective-permute-start(f32[16,1024]{1,0:T(8,128)S(1)} %constant_dynamic-slice_fusion), channel_id=1, source_target_pairs={{0,1},{1,0},{2,3},{3,2},{4,5},{5,4},{6,7},{7,6},{8,9},{9,8},{10,11... | collective-permute-start | bytes 196616 | tf_op jit(solution)/shard_map/ppermute | solution.py:23
  15.2 33.0 %copy-start.15 = (f32[16,1024]{1,0:T(8,128)}, f32[16,1024]{1,0:T(8,128)S(1)}, u32[]{:S(2)}) copy-start(f32[16,1024]{1,0:T(8,128)S(1)} %collective-permute-done.1) | copy-start | bytes 196612
  15.3 33.0 %copy-start.12 = (f32[16,1024]{1,0:T(8,128)}, f32[16,1024]{1,0:T(8,128)S(1)}, u32[]{:S(2)}) copy-start(f32[16,1024]{1,0:T(8,128)S(1)} %select_add_fusion.1) | copy-start | bytes 196612
  15.3 7.8 %collective-permute-start.2 = (f32[16,1024]{1,0:T(8,128)S(1)}, f32[16,1024]{1,0:T(8,128)S(1)}, u32[]{:S(2)}, u32[]{:S(2)}) collective-permute-start(f32[16,1024]{1,0:T(8,128)S(1)} %select_add_fusion.1), channel_id=1, source_target_pairs={{0,2},{1,3},{2,0},{3,1},{4,6},{5,7},{6,4},{7,5},{8,10},{9,11},{10,... | collective-permute-start | bytes 196616 | tf_op jit(solution)/shard_map/ppermute | solution.py:23
  16.6 31.7 %collective-permute-start.10 = (bf16[2,2,128,512]{3,2,1,0:T(8,128)(2,1)S(1)}, bf16[2,2,128,512]{3,2,1,0:T(8,128)(2,1)S(1)}, u32[]{:S(2)}, u32[]{:S(2)}) collective-permute-start(bf16[2,2,128,512]{3,2,1,0:T(8,128)(2,1)S(1)} %get-tuple-element.26), channel_id=1, source_target_pairs={{0,4},{1,5},{2,6},{3,7},{4,8},{5,9},{6,10},{7,11},{8,12},{9,13},{1... | collective-permute-start | bytes 1572872 | tf_op jit(solution)/shard_map/ppermute | solution.py:37
  19.8 29.9 %collective-permute-start.8 = (bf16[2,2,128,512]{3,2,1,0:T(8,128)(2,1)S(1)}, bf16[2,2,128,512]{3,2,1,0:T(8,128)(2,1)S(1)}, u32[]{:S(2)}, u32[]{:S(2)}) collective-permute-start(bf16[2,2,128,512]{3,2,1,0:T(8,128)(2,1)S(1)} %get-tuple-element.25), channel_id=1, source_target_pairs={{0,6},{1,7},{2,4},{3,5},{4,10},{5,11},{6,8},{7,9},{8,14},{9,15},{1... | collective-permute-start | bytes 1572872 | tf_op jit(solution)/shard_map/ppermute | solution.py:37
  23.1 25.2 %copy-start.16 = (f32[16,1024]{1,0:T(8,128)}, f32[16,1024]{1,0:T(8,128)S(1)}, u32[]{:S(2)}) copy-start(f32[16,1024]{1,0:T(8,128)S(1)} %collective-permute-done.2) | copy-start | bytes 196612
  23.1 20.9 %collective-permute-start.3 = (f32[16,1024]{1,0:T(8,128)S(1)}, f32[16,1024]{1,0:T(8,128)S(1)}, u32[]{:S(2)}, u32[]{:S(2)}) collective-permute-start(f32[16,1024]{1,0:T(8,128)S(1)} %select_add_fusion), channel_id=1, source_target_pairs={{0,4},{1,5},{2,6},{3,7},{4,8},{5,9},{6,10},{7,11},{8,12},{9,13},{1... | collective-permute-start | bytes 196616 | tf_op jit(solution)/shard_map/ppermute | solution.py:37
  25.1 40.6 %collective-permute-start.7 = (bf16[2,3,128,512]{3,2,1,0:T(8,128)(2,1)S(1)}, bf16[2,3,128,512]{3,2,1,0:T(8,128)(2,1)S(1)}, u32[]{:S(2)}, u32[]{:S(2)}) collective-permute-start(bf16[2,3,128,512]{3,2,1,0:T(8,128)(2,1)S(1)} %pack.2), channel_id=1, source_target_pairs={{0,2},{1,3},{2,0},{3,1},{4,6},{5,7},{6,4},{7,5},{8,10},{9,11},{10,... | collective-permute-start | bytes 2359304 | tf_op jit(solution)/shard_map/ppermute | solution.py:23
  44.0 6.3 %collective-permute-start.4 = (f32[16,1024]{1,0:T(8,128)S(1)}, f32[16,1024]{1,0:T(8,128)S(1)}, u32[]{:S(2)}, u32[]{:S(2)}) collective-permute-start(f32[16,1024]{1,0:T(8,128)S(1)} %multiply_add_fusion.1), channel_id=1, source_target_pairs={{0,8},{1,9},{2,10},{3,11},{4,12},{5,13},{6,14},{7,15},{16,24},{17,... | collective-permute-start | bytes 196616 | tf_op jit(solution)/shard_map/ppermute | solution.py:37
  48.3 26.1 %collective-permute-start.12 = (bf16[2,2,128,512]{3,2,1,0:T(8,128)(2,1)S(1)}, bf16[2,2,128,512]{3,2,1,0:T(8,128)(2,1)S(1)}, u32[]{:S(2)}, u32[]{:S(2)}) collective-permute-start(bf16[2,2,128,512]{3,2,1,0:T(8,128)(2,1)S(1)} %collective-permute-done.10.own), channel_id=1, source_target_pairs={{6,10},{7,11},{10,14},{11,15},{22,26},{23,27},{26,30},{27,31}} | collective-permute-start | bytes 1572872 | tf_op jit(solution)/shard_map/ppermute | solution.py:37
  49.6 24.8 %collective-permute-start.9 = (bf16[2,2,128,512]{3,2,1,0:T(8,128)(2,1)S(1)}, bf16[2,2,128,512]{3,2,1,0:T(8,128)(2,1)S(1)}, u32[]{:S(2)}, u32[]{:S(2)}) collective-permute-start(bf16[2,2,128,512]{3,2,1,0:T(8,128)(2,1)S(1)} %collective-permute-done.8.cross), channel_id=1, source_target_pairs={{4,8},{5,9},{8,12},{9,13},{20,24},{21,25},{24,28},{25,29}} | collective-permute-start | bytes 1572872 | tf_op jit(solution)/shard_map/ppermute | solution.py:37
  52.0 10.1 %collective-permute-start.5 = (f32[16,1024]{1,0:T(8,128)}, f32[16,1024]{1,0:T(8,128)}, u32[]{:S(2)}, u32[]{:S(2)}) collective-permute-start(f32[16,1024]{1,0:T(8,128)} %get-tuple-element.34), channel_id=1, source_target_pairs={{0,1},{1,0},{2,3},{3,2},{4,5},{5,4},{6,7},{7,6},{8,9},{9,8},{10,11... | collective-permute-start | bytes 196616 | tf_op jit(solution)/shard_map/ppermute | solution.py:23
  54.8 10.0 %copy-start.13 = (f32[16,1024]{1,0:T(8,128)S(1)}, f32[16,1024]{1,0:T(8,128)}, u32[]{:S(2)}) copy-start(f32[16,1024]{1,0:T(8,128)} %get-tuple-element.35) | copy-start | bytes 196612
  54.8 10.0 %copy-start.14 = (f32[16,1024]{1,0:T(8,128)S(1)}, f32[16,1024]{1,0:T(8,128)}, u32[]{:S(2)}) copy-start(f32[16,1024]{1,0:T(8,128)} %get-tuple-element.36) | copy-start | bytes 196612
  54.8 10.9 %copy-start.11 = (s32[4]{0:T(128)S(1)}, s32[4]{0:T(128)}, u32[]{:S(2)}) copy-start(s32[4]{0:T(128)} %docs_ref.3) | copy-start | bytes 52
  61.3 13.1 %collective-permute-start.11 = (bf16[1,2,128,512]{3,2,1,0:T(8,128)(2,1)S(1)}, bf16[1,2,128,512]{3,2,1,0:T(8,128)(2,1)S(1)}, u32[]{:S(2)}, u32[]{:S(2)}) collective-permute-start(bf16[1,2,128,512]{3,2,1,0:T(8,128)(2,1)S(1)} %slice.8), channel_id=1, source_target_pairs={{4,8},{5,9},{8,12},{9,13},{20,24},{21,25},{24,28},{25,29}} | collective-permute-start | bytes 786440 | tf_op jit(solution)/shard_map/ppermute | solution.py:37
  62.1 12.4 %collective-permute-start.13 = (bf16[1,2,128,512]{3,2,1,0:T(8,128)(2,1)S(1)}, bf16[1,2,128,512]{3,2,1,0:T(8,128)(2,1)S(1)}, u32[]{:S(2)}, u32[]{:S(2)}) collective-permute-start(bf16[1,2,128,512]{3,2,1,0:T(8,128)(2,1)S(1)} %slice.9), channel_id=1, source_target_pairs={{6,10},{7,11},{10,14},{11,15},{22,26},{23,27},{26,30},{27,31}} | collective-permute-start | bytes 786440 | tf_op jit(solution)/shard_map/ppermute | solution.py:37
  74.5 5.8 %copy-start.2 = (f32[128,2048]{1,0:T(8,128)S(1)}, f32[128,2048]{1,0:T(8,128)}, u32[]{:S(2)}) copy-start(f32[128,2048]{1,0:T(8,128)} %get-tuple-element.20.near_ref) | copy-start | bytes 3145732
  74.5 5.8 %copy-start.3 = (f32[128,2048]{1,0:T(8,128)S(1)}, f32[128,2048]{1,0:T(8,128)}, u32[]{:S(2)}) copy-start(f32[128,2048]{1,0:T(8,128)} %get-tuple-element.21.q_ref) | copy-start | bytes 3145732
  74.5 5.8 %copy-start.9 = (f32[128,16]{0,1:T(8,128)S(1)}, f32[128,16]{0,1:T(8,128)}, u32[]{:S(2)}) copy-start(f32[128,16]{0,1:T(8,128)} %param.8) | copy-start | bytes 24580
  74.5 5.8 %copy-start.10 = (f32[128,16]{0,1:T(8,128)S(1)}, f32[128,16]{0,1:T(8,128)}, u32[]{:S(2)}) copy-start(f32[128,16]{0,1:T(8,128)} %param.9) | copy-start | bytes 24580
  78.0 5.7 %collective-permute-start.14 = (bf16[128,512]{1,0:T(8,128)(2,1)S(1)}, bf16[128,512]{1,0:T(8,128)(2,1)S(1)}, u32[]{:S(2)}, u32[]{:S(2)}) collective-permute-start(bf16[128,512]{1,0:T(8,128)(2,1)S(1)} %get-tuple-element.31), channel_id=1, source_target_pairs={{0,1},{1,0},{2,3},{3,2},{4,5},{5,4},{6,7},{7,6},{8,9},{9,8},{10,11... | collective-permute-start | bytes 393224 | tf_op jit(solution)/shard_map/ppermute | solution.py:23
  78.4 5.3 %collective-permute-start.15 = (bf16[128,512]{1,0:T(8,128)(2,1)S(1)}, bf16[128,512]{1,0:T(8,128)(2,1)S(1)}, u32[]{:S(2)}, u32[]{:S(2)}) collective-permute-start(bf16[128,512]{1,0:T(8,128)(2,1)S(1)} %get-tuple-element.32), channel_id=1, source_target_pairs={{0,2},{1,3},{2,0},{3,1},{4,6},{5,7},{6,4},{7,5},{8,10},{9,11},{10,... | collective-permute-start | bytes 393224 | tf_op jit(solution)/shard_map/ppermute | solution.py:23
  78.7 7.7 %collective-permute-start.16 = (bf16[128,512]{1,0:T(8,128)(2,1)S(1)}, bf16[128,512]{1,0:T(8,128)(2,1)S(1)}, u32[]{:S(2)}, u32[]{:S(2)}) collective-permute-start(bf16[128,512]{1,0:T(8,128)(2,1)S(1)} %get-tuple-element.33), channel_id=1, source_target_pairs={{0,3},{1,2},{2,1},{3,0},{4,7},{5,6},{6,5},{7,4},{8,11},{9,10},{10,... | collective-permute-start | bytes 393224 | tf_op jit(solution)/shard_map/ppermute | solution.py:23
  (2 other events, 2.2 us)
